TPU v7x, 32 devices: a whole 2x2x4 slice. The times are simulated.
32 devices in a mesh: fsdp: 8 (over y, x, core), dp: 4 (over z).
Axes of the slice: x: 2, y: 2, z: 4, core: 2. Of those that a mesh axis runs over, the one named last changes fastest.
Arguments:
- tokens: bfloat16 [32768, 768], P(('fsdp', 'dp')), may hold values from -6 to 6
- crop_ids: int32 [32768], P(('fsdp', 'dp')), may hold values from 0 to 23, as said below
- gain_first: bfloat16 [768], P('fsdp'), may hold values from 0.25 to 1.75
- shift_first: bfloat16 [768], P('fsdp'), may hold values from -1 to 1
- joint_weight: bfloat16 [768, 2304], P('fsdp'), may hold values from -0.3125 to 0.3125
- joint_bias: bfloat16 [2, 768], P(None, 'fsdp'), may hold values from -1 to 1
- output_weight: bfloat16 [768, 768], P('fsdp'), may hold values from -0.4375 to 0.4375
- output_bias: bfloat16 [768], P('fsdp'), may hold values from -1 to 1
- gain_second: bfloat16 [768], P('fsdp'), may hold values from 0.25 to 1.75
- shift_second: bfloat16 [768], P('fsdp'), may hold values from -1 to 1
- up_weight: bfloat16 [768, 3072], P('fsdp'), may hold values from -0.21875 to 0.21875
- up_bias: bfloat16 [3072], P('fsdp'), may hold values from -1 to 1
- down_weight: bfloat16 [3072, 768], P('fsdp'), may hold values from -0.15625 to 0.15625
- down_bias: bfloat16 [768], P('fsdp'), may hold values from -1 to 1
- cotangent: bfloat16 [32768, 768], P(('fsdp', 'dp')), may hold values from -6 to 6
Outputs:
- activations: float32 [32768, 768], P(('fsdp', 'dp'))
- input_grad: float32 [32768, 768], P(('fsdp', 'dp'))
- grad_gain_first: float32 [768], P('fsdp')
- grad_shift_first: float32 [768], P('fsdp')
- grad_joint_weight: float32 [768, 2304], P('fsdp')
- grad_joint_bias: float32 [2, 768], P(None, 'fsdp')
- grad_output_weight: float32 [768, 768], P('fsdp')
- grad_output_bias: float32 [768], P('fsdp')
- grad_gain_second: float32 [768], P('fsdp')
- grad_shift_second: float32 [768], P('fsdp')
- grad_up_weight: float32 [768, 3072], P('fsdp')
- grad_up_bias: float32 [3072], P('fsdp')
- grad_down_weight: float32 [3072, 768], P('fsdp')
- grad_down_bias: float32 [768], P('fsdp')
Inputs may be any that keep to these rules, and one draw needn't show every extreme that they name: `crop_ids`: each device's 1024 tokens hold whole crops in random order: at least one global crop of 197 tokens, local crops of 37 tokens, and at most one shorter remainder crop; the first device's block holds exactly one global crop. Ids number the crops of a block from 0 in order of position; a crop has at most 197 tokens and every block has a crop of exactly 197.
All inputs are finite; a program needn't handle non-finite values.
Results may differ from a plain program's by a relative error of at most 0.015.
Values may be sent and summed in bfloat16 or wider, within the bound.
No kernel may reach another device: no remote copies, remote signals or barrier semaphores. Data moves between devices by JAX's collectives and lax.ppermute only.
A program may use at most 256 MiB of HBM per device.

v0:
```python
import jax
import jax.numpy as jnp
from jax import lax
from jax.sharding import PartitionSpec as P

HD = 64


def layer_norm(values, gain, shift):
    center = values - jnp.mean(values, axis=-1, keepdims=True)
    spread = jnp.mean(center * center, axis=-1, keepdims=True)
    return center * lax.rsqrt(spread + 1e-06) * gain + shift


def exact_gelu(values):
    return jax.nn.gelu(values, approximate=False)


def on_device(
    tokens,
    crop_ids,
    gain_first,
    shift_first,
    joint_weight,
    joint_bias,
    output_weight,
    output_bias,
    gain_second,
    shift_second,
    up_weight,
    up_bias,
    down_weight,
    down_bias,
    cotangent,
):
    row_count = tokens.shape[0]
    model_width = tokens.shape[1]
    head_count = model_width // HD
    score_scale = HD ** (-0.5)
    block_rows = min(512, row_count)
    block_count = row_count // block_rows
    attn_full = (
        lax.all_gather(gain_first, "fsdp", axis=0, tiled=True),
        lax.all_gather(shift_first, "fsdp", axis=0, tiled=True),
        lax.all_gather(joint_weight, "fsdp", axis=0, tiled=True),
        lax.all_gather(joint_bias, "fsdp", axis=1, tiled=True),
        lax.all_gather(output_weight, "fsdp", axis=0, tiled=True),
        lax.all_gather(output_bias, "fsdp", axis=0, tiled=True),
    )
    gain_one, shift_one, joint_full, joint_bias_full, output_full, output_bias_full = attn_full
    inputs = tokens.astype(jnp.float32)
    normed_first, pull_first = jax.vjp(
        layer_norm, inputs, gain_one.astype(jnp.float32), shift_one.astype(jnp.float32)
    )
    hidden_first = normed_first.astype(jnp.bfloat16)
    bias_joint = joint_bias_full.astype(jnp.float32)
    bias_row = jnp.concatenate(
        [bias_joint[0], jnp.zeros((model_width,), jnp.float32), bias_joint[1]]
    )
    joint_proj = (
        jnp.dot(hidden_first, joint_full, preferred_element_type=jnp.float32) + bias_row
    ).astype(jnp.bfloat16)
    queries = joint_proj[:, :model_width].reshape(row_count, head_count, HD)
    key_rows = joint_proj[:, model_width : 2 * model_width].reshape(row_count, head_count, HD)
    value_rows = joint_proj[:, 2 * model_width :].reshape(row_count, head_count, HD)
    query_blocks = queries.reshape(block_count, block_rows, head_count, HD)
    crop_blocks = crop_ids.reshape(block_count, block_rows)

    def masked_scores(query_block, crop_block):
        scores = (
            jnp.einsum("qhd,khd->hqk", query_block, key_rows, preferred_element_type=jnp.float32)
            * score_scale
        )
        same_crop = crop_block[:, None] == crop_ids[None, :]
        return jnp.where(same_crop[None], scores, -1e30)

    def attend(inputs_block):
        query_block, crop_block = inputs_block
        scores = masked_scores(query_block, crop_block)
        top_score = jnp.max(scores, axis=-1, keepdims=True)
        expo = jnp.exp(scores - top_score)
        total = jnp.sum(expo, axis=-1, keepdims=True)
        weights_low = (expo / total).astype(jnp.bfloat16)
        mixed_block = jnp.einsum(
            "hqk,khd->qhd", weights_low, value_rows, preferred_element_type=jnp.float32
        )
        log_total = top_score[..., 0] + jnp.log(total[..., 0])
        return (mixed_block.astype(jnp.bfloat16), log_total)

    mixed_blocks, log_totals = lax.map(attend, (query_blocks, crop_blocks))
    mixed_heads = mixed_blocks.reshape(row_count, model_width)
    branch_first = jnp.dot(
        mixed_heads, output_full, preferred_element_type=jnp.float32
    ) + output_bias_full.astype(jnp.float32)
    middle = inputs + branch_first
    mlp_full = (
        lax.all_gather(gain_second, "fsdp", axis=0, tiled=True),
        lax.all_gather(shift_second, "fsdp", axis=0, tiled=True),
        lax.all_gather(up_weight, "fsdp", axis=0, tiled=True),
        lax.all_gather(up_bias, "fsdp", axis=0, tiled=True),
        lax.all_gather(down_weight, "fsdp", axis=0, tiled=True),
        lax.all_gather(down_bias, "fsdp", axis=0, tiled=True),
    )
    gain_two, shift_two, up_full, up_bias_full, down_full, down_bias_full = mlp_full
    normed_second, pull_second = jax.vjp(
        layer_norm, middle, gain_two.astype(jnp.float32), shift_two.astype(jnp.float32)
    )
    hidden_second = normed_second.astype(jnp.bfloat16)
    up_value = jnp.dot(
        hidden_second, up_full, preferred_element_type=jnp.float32
    ) + up_bias_full.astype(jnp.float32)
    active_value, pull_gelu = jax.vjp(exact_gelu, up_value)
    active = active_value.astype(jnp.bfloat16)
    activations = (
        middle
        + jnp.dot(active, down_full, preferred_element_type=jnp.float32)
        + down_bias_full.astype(jnp.float32)
    )
    mlp_back = (
        lax.all_gather(gain_second, "fsdp", axis=0, tiled=True),
        lax.all_gather(shift_second, "fsdp", axis=0, tiled=True),
        lax.all_gather(up_weight, "fsdp", axis=0, tiled=True),
        lax.all_gather(up_bias, "fsdp", axis=0, tiled=True),
        lax.all_gather(down_weight, "fsdp", axis=0, tiled=True),
        lax.all_gather(down_bias, "fsdp", axis=0, tiled=True),
    )
    up_back = mlp_back[2]
    down_back = mlp_back[4]
    grad_out = cotangent.astype(jnp.float32)
    grad_down_bias = jnp.sum(grad_out, axis=0)
    grad_down_weight = jnp.einsum(
        "tf,td->fd", active, cotangent, preferred_element_type=jnp.float32
    )
    grad_active = jnp.einsum("td,fd->tf", cotangent, down_back, preferred_element_type=jnp.float32)
    (grad_up_value,) = pull_gelu(grad_active)
    grad_up_low = grad_up_value.astype(jnp.bfloat16)
    grad_up_bias = jnp.sum(grad_up_low.astype(jnp.float32), axis=0)
    grad_up_weight = jnp.einsum(
        "td,tf->df", hidden_second, grad_up_low, preferred_element_type=jnp.float32
    )
    grad_hidden_second = jnp.einsum(
        "tf,df->td", grad_up_low, up_back, preferred_element_type=jnp.float32
    )
    grad_middle, grad_gain_second, grad_shift_second = pull_second(grad_hidden_second)
    grad_middle = grad_middle + grad_out
    mlp_terms = (
        grad_gain_second,
        grad_shift_second,
        grad_up_weight,
        grad_up_bias,
        grad_down_weight,
        grad_down_bias,
    )
    mlp_sums = (
        lax.psum_scatter(mlp_terms[0], "fsdp", scatter_dimension=0, tiled=True),
        lax.psum_scatter(mlp_terms[1], "fsdp", scatter_dimension=0, tiled=True),
        lax.psum_scatter(mlp_terms[2], "fsdp", scatter_dimension=0, tiled=True),
        lax.psum_scatter(mlp_terms[3], "fsdp", scatter_dimension=0, tiled=True),
        lax.psum_scatter(mlp_terms[4], "fsdp", scatter_dimension=0, tiled=True),
        lax.psum_scatter(mlp_terms[5], "fsdp", scatter_dimension=0, tiled=True),
    )
    attn_back = (
        lax.all_gather(gain_first, "fsdp", axis=0, tiled=True),
        lax.all_gather(shift_first, "fsdp", axis=0, tiled=True),
        lax.all_gather(joint_weight, "fsdp", axis=0, tiled=True),
        lax.all_gather(joint_bias, "fsdp", axis=1, tiled=True),
        lax.all_gather(output_weight, "fsdp", axis=0, tiled=True),
        lax.all_gather(output_bias, "fsdp", axis=0, tiled=True),
    )
    joint_back = attn_back[2]
    output_back = attn_back[4]
    grad_branch = grad_middle.astype(jnp.bfloat16)
    grad_output_bias = jnp.sum(grad_branch.astype(jnp.float32), axis=0)
    grad_output_weight = jnp.einsum(
        "td,te->de", mixed_heads, grad_branch, preferred_element_type=jnp.float32
    )
    grad_mixed = jnp.einsum(
        "te,de->td", grad_branch, output_back, preferred_element_type=jnp.float32
    ).astype(jnp.bfloat16)
    grad_mixed_blocks = grad_mixed.reshape(block_count, block_rows, head_count, HD)

    def attend_back(carry, inputs_block):
        grad_key_sum, grad_value_sum = carry
        query_block, crop_block, log_total, grad_block = inputs_block
        scores = masked_scores(query_block, crop_block)
        weights = jnp.exp(scores - log_total[..., None])
        weights_low = weights.astype(jnp.bfloat16)
        grad_value_sum = grad_value_sum + jnp.einsum(
            "hqk,qhd->khd", weights_low, grad_block, preferred_element_type=jnp.float32
        )
        grad_weights = jnp.einsum(
            "qhd,khd->hqk", grad_block, value_rows, preferred_element_type=jnp.float32
        )
        inner = jnp.sum(weights * grad_weights, axis=-1, keepdims=True)
        grad_scores = (weights * (grad_weights - inner)).astype(jnp.bfloat16)
        grad_query = (
            jnp.einsum("hqk,khd->qhd", grad_scores, key_rows, preferred_element_type=jnp.float32)
            * score_scale
        )
        grad_key_sum = (
            grad_key_sum
            + jnp.einsum(
                "hqk,qhd->khd", grad_scores, query_block, preferred_element_type=jnp.float32
            )
            * score_scale
        )
        return ((grad_key_sum, grad_value_sum), grad_query)

    empty_heads = jnp.zeros((row_count, head_count, HD), jnp.float32)
    (grad_keys, grad_values), grad_query_blocks = lax.scan(
        attend_back,
        (empty_heads, empty_heads),
        (query_blocks, crop_blocks, log_totals, grad_mixed_blocks),
    )
    grad_joint = jnp.concatenate(
        [
            grad_query_blocks.reshape(row_count, model_width),
            grad_keys.reshape(row_count, model_width),
            grad_values.reshape(row_count, model_width),
        ],
        axis=1,
    ).astype(jnp.bfloat16)
    grad_joint_wide = grad_joint.astype(jnp.float32)
    grad_joint_bias = jnp.stack(
        [
            jnp.sum(grad_joint_wide[:, :model_width], axis=0),
            jnp.sum(grad_joint_wide[:, 2 * model_width :], axis=0),
        ]
    )
    grad_joint_weight = jnp.einsum(
        "td,te->de", hidden_first, grad_joint, preferred_element_type=jnp.float32
    )
    grad_hidden_first = jnp.einsum(
        "te,de->td", grad_joint, joint_back, preferred_element_type=jnp.float32
    )
    grad_inputs, grad_gain_first, grad_shift_first = pull_first(grad_hidden_first)
    input_grad = grad_inputs + grad_middle
    attn_terms = (
        grad_gain_first,
        grad_shift_first,
        grad_joint_weight,
        grad_joint_bias,
        grad_output_weight,
        grad_output_bias,
    )
    attn_sums = (
        lax.psum_scatter(attn_terms[0], "fsdp", scatter_dimension=0, tiled=True),
        lax.psum_scatter(attn_terms[1], "fsdp", scatter_dimension=0, tiled=True),
        lax.psum_scatter(attn_terms[2], "fsdp", scatter_dimension=0, tiled=True),
        lax.psum_scatter(attn_terms[3], "fsdp", scatter_dimension=1, tiled=True),
        lax.psum_scatter(attn_terms[4], "fsdp", scatter_dimension=0, tiled=True),
        lax.psum_scatter(attn_terms[5], "fsdp", scatter_dimension=0, tiled=True),
    )
    totals = (
        lax.psum(attn_sums[0].astype(jnp.bfloat16), "dp").astype(jnp.float32),
        lax.psum(attn_sums[1].astype(jnp.bfloat16), "dp").astype(jnp.float32),
        lax.psum(attn_sums[2].astype(jnp.bfloat16), "dp").astype(jnp.float32),
        lax.psum(attn_sums[3].astype(jnp.bfloat16), "dp").astype(jnp.float32),
        lax.psum(attn_sums[4].astype(jnp.bfloat16), "dp").astype(jnp.float32),
        lax.psum(attn_sums[5].astype(jnp.bfloat16), "dp").astype(jnp.float32),
        lax.psum(mlp_sums[0].astype(jnp.bfloat16), "dp").astype(jnp.float32),
        lax.psum(mlp_sums[1].astype(jnp.bfloat16), "dp").astype(jnp.float32),
        lax.psum(mlp_sums[2].astype(jnp.bfloat16), "dp").astype(jnp.float32),
        lax.psum(mlp_sums[3].astype(jnp.bfloat16), "dp").astype(jnp.float32),
        lax.psum(mlp_sums[4].astype(jnp.bfloat16), "dp").astype(jnp.float32),
        lax.psum(mlp_sums[5].astype(jnp.bfloat16), "dp").astype(jnp.float32),
    )
    return (
        activations,
        input_grad,
        totals[0],
        totals[1],
        totals[2],
        totals[3],
        totals[4],
        totals[5],
        totals[6],
        totals[7],
        totals[8],
        totals[9],
        totals[10],
        totals[11],
    )


def solution(mesh):
    placed = (
        P(("fsdp", "dp"), None),
        P(("fsdp", "dp")),
        P("fsdp"),
        P("fsdp"),
        P("fsdp", None),
        P(None, "fsdp"),
        P("fsdp", None),
        P("fsdp"),
        P("fsdp"),
        P("fsdp"),
        P("fsdp", None),
        P("fsdp"),
        P("fsdp", None),
        P("fsdp"),
        P(("fsdp", "dp"), None),
    )
    return jax.shard_map(
        on_device,
        mesh=mesh,
        in_specs=placed,
        out_specs=(
            P(("fsdp", "dp"), None),
            P(("fsdp", "dp"), None),
            P("fsdp"),
            P("fsdp"),
            P("fsdp", None),
            P(None, "fsdp"),
            P("fsdp", None),
            P("fsdp"),
            P("fsdp"),
            P("fsdp"),
            P("fsdp", None),
            P("fsdp"),
            P("fsdp", None),
            P("fsdp"),
        ),
        check_vma=False,
    )
```

profile of v0, /device:TPU:0, one launch (start us, length us, event | category | flops | bytes accessed | tf_op | source)
XLA Modules:
  0.0 798.5 jit_solution(4974741141929564460)
XLA Ops:
  17.8 26.7 %all-reduce.14 = (bf16[768]{0:T(1024)(128)(2,1)S(1)}, bf16[768]{0:T(1024)(128)(2,1)S(1)}, bf16[768]{0:T(1024)(128)(2,1)S(1)}, bf16[768]{0:T(1024)(128)(2,1)S(1)}...) all-reduce(bf16[768]{0:T(1024)(128)(2,1)S(1)} %dynamic-update-slice., ...), channel_id=1, replica_groups=mesh['fsdp'=8,'dp'=4] {'fsdp'}, use_global_device_ids=true, to_apply=%add.1 | all-reduce | flops 4608 | bytes 18432
  47.0 7.8 all-gather
  54.9 8.9 %all-gather.1 = bf16[8,1,384]{2,1,0:T(2,128)(2,1)S(1)} all-gather(bf16[1,1,384]{2,1,0:T(2,128)(2,1)S(1)} %reshape.232), channel_id=1, replica_groups=mesh['fsdp'=8,'dp'=4] {'fsdp'}, dimensions={0}, use_global_device_ids=true | all-gather | bytes 6912 | tf_op jit(solution)/shard_map/all_gather | solution.py:100
  64.4 1.8 copy.83
  67.6 1.7 copy.92
  69.4 6.4 add_convert_fusion.1
  78.9 1.7 copy.86
  82.3 3.9 reshape_reshape.3
  86.2 1.7 copy.88
  87.9 72.2 %while.27 = (s32[]{:T(128)}, bf16[2,512,12,64]{1,3,2,0:T(8,128)(2,1)}, f32[2,12,512]{2,1,0:T(8,128)S(1)}, s32[2,512]{1,0:T(2,128)S(1)}, s32[1024]{0:T(1024)S(1)}...) while((s32[]{:T(128)}, ...), condition=%wide.region_5.6_spmd, body=%wide.region_2.5_spmd.sunk | while | flops 1687021568 | bytes 189499568 | solution.py:90
  88.3 11.1 %fusion.114 = (f32[12,512]{1,0:T(8,128)S(1)}, f32[12,512,1024]{2,1,0:T(8,128)}) fusion(pred[512,1024]{1,0:T(8,128)(4,1)S(1)} %broadcast_compare_fusion.4, bf16[1024,12,64]{0,2,1:T(8,128)(2,1)S(1)} %get-tuple-element.534, bf16[2,512,12,64]{1,3,2,0:T(8,128)(2,1)S(1)} %get-tuple-element.533, s32[]{:T(128)S(6)} %copy.120), kind=kOutput, calls=%fused_computation.3.clone.1 | convolution fusion | flops 824174592 | bytes 28073988 | tf_op jit(solution)/shard_map/while/body/eval_jaxpr/qhd,khd->hqk/dot_general | solution.py:71
  99.4 12.5 %fusion.115 = f32[12,512]{1,0:T(8,128)S(1)} fusion(f32[12,512,1024]{2,1,0:T(8,128)} %get-tuple-element.495, f32[12,512]{1,0:T(8,128)S(1)} %get-tuple-element.496, pred[512,1024]{1,0:T(8,128)(4,1)S(1)} %broadcast_compare_fusion.4), kind=kLoop, calls=%fused_computation.4.clone.1 | loop fusion | flops 25159680 | bytes 25739264 | tf_op jit(solution)/shard_map/while/body/eval_jaxpr/reduce_sum | solution.py:82
  111.9 3.2 copy-done
  115.2 8.5 %fusion.116 = bf16[2,512,12,64]{1,3,2,0:T(8,128)(2,1)} fusion(bf16[2,512,12,64]{1,3,2,0:T(8,128)(2,1)} %get-tuple-element.520, s32[]{:T(128)S(6)} %copy.120, bf16[1024,12,64]{0,2,1:T(8,128)(2,1)S(1)} %copy-done.6, f32[12,512,1024]{2,1,0:T(8,128)S(1)} %copy-done, f32[12,512]{1,0:T(8,128)S(1)} %fusion.115, f32[12,512]{1,0:T(8,128)S(1)} %get-tuple-element.496, ...), kind=kOutput, calls=%fused_computation.8.clone.1 | convolution fusion | flops 837156864 | bytes 28098564 | tf_op jit(solution)/shard_map/while/body/eval_jaxpr/hqk,khd->qhd/dot_general | solution.py:84
  124.1 10.7 %fusion.114 = (f32[12,512]{1,0:T(8,128)S(1)}, f32[12,512,1024]{2,1,0:T(8,128)}) fusion(pred[512,1024]{1,0:T(8,128)(4,1)S(1)} %broadcast_compare_fusion.4, bf16[1024,12,64]{0,2,1:T(8,128)(2,1)S(1)} %get-tuple-element.534, bf16[2,512,12,64]{1,3,2,0:T(8,128)(2,1)S(1)} %get-tuple-element.533, s32[]{:T(128)S(6)} %copy.120), kind=kOutput, calls=%fused_computation.3.clone.1 | convolution fusion | flops 824174592 | bytes 28073988 | tf_op jit(solution)/shard_map/while/body/eval_jaxpr/qhd,khd->hqk/dot_general | solution.py:71
  134.8 13.2 %fusion.115 = f32[12,512]{1,0:T(8,128)S(1)} fusion(f32[12,512,1024]{2,1,0:T(8,128)} %get-tuple-element.495, f32[12,512]{1,0:T(8,128)S(1)} %get-tuple-element.496, pred[512,1024]{1,0:T(8,128)(4,1)S(1)} %broadcast_compare_fusion.4), kind=kLoop, calls=%fused_computation.4.clone.1 | loop fusion | flops 25159680 | bytes 25739264 | tf_op jit(solution)/shard_map/while/body/eval_jaxpr/reduce_sum | solution.py:82
  147.9 3.3 copy-done
  151.2 8.5 %fusion.116 = bf16[2,512,12,64]{1,3,2,0:T(8,128)(2,1)} fusion(bf16[2,512,12,64]{1,3,2,0:T(8,128)(2,1)} %get-tuple-element.520, s32[]{:T(128)S(6)} %copy.120, bf16[1024,12,64]{0,2,1:T(8,128)(2,1)S(1)} %copy-done.6, f32[12,512,1024]{2,1,0:T(8,128)S(1)} %copy-done, f32[12,512]{1,0:T(8,128)S(1)} %fusion.115, f32[12,512]{1,0:T(8,128)S(1)} %get-tuple-element.496, ...), kind=kOutput, calls=%fused_computation.8.clone.1 | convolution fusion | flops 837156864 | bytes 28098564 | tf_op jit(solution)/shard_map/while/body/eval_jaxpr/hqk,khd->qhd/dot_general | solution.py:84
  160.1 4.2 copy.89
  165.9 3.8 fusion.67
  170.6 37.9 %multiply_convert_fusion.1 = (bf16[1024,3072]{1,0:T(8,128)(2,1)}, f32[1024,3072]{1,0:T(8,128)}, f32[1024,3072]{1,0:T(8,128)}) fusion(f32[3072]{0:T(1024)S(1)} %bitcast.151, bf16[768,3072]{1,0:T(8,128)(2,1)} %all-gather.11.cloned.1.call-done, f32[1024,768]{0,1:T(8,128)S(1)} %get-tuple-element.378, f32[768]{0:T(1024)S(1)} %copy-done.51, ...), kind=kOutput, calls=%fused_computation.50 | convolution fusion | flops 5043388416 | bytes 39348224 | tf_op jit(solution)/shard_map/dot_general | solution.py:109
  208.5 18.9 %convert_reduce_fusion = (f32[3072]{0:T(1024)}, bf16[1024,3072]{1,0:T(8,128)(2,1)}) fusion(f32[1024,3072]{1,0:T(8,128)} %get-tuple-element.365, bf16[1024,768]{1,0:T(8,128)(2,1)} %param.33, bf16[3072,768]{1,0:T(8,128)(2,1)} %all-gather.13.cloned.1.call-done, f32[1024,3072]{1,0:T(8,128)} %get-tuple-element.379, f32[3072]{0:T(1024)S(1)} %bitcast.152), kind=kOutput, calls=%fused_computation.48 | convolution fusion | flops 4885312512 | bytes 37773312 | tf_op jit(solution)/shard_map/td,fd->tf/dot_general | solution.py:134
  227.4 10.3 %fusion.69 = (f32[768]{0:T(1024)}, f32[1024,768]{1,0:T(8,128)}) fusion(bf16[1024,3072]{1,0:T(8,128)(2,1)} %get-tuple-element.385, bf16[768,3072]{1,0:T(8,128)(2,1)} %all-gather.11.cloned.1.call-done), kind=kOutput, calls=%fused_computation.128 | convolution fusion | flops 4832623616 | bytes 14158848 | tf_op jit(solution)/shard_map/tf,df->td/dot_general | solution.py:141
  237.7 3.5 copy.91
  241.3 3.5 multiply_reduce_fusion.1
  248.2 2.9 fusion.70
  251.1 2.7 convolution_convert_fusion
  257.4 169.1 %while.28 = (s32[]{:T(128)}, f32[1024,12,64]{0,2,1:T(8,128)}, f32[1024,12,64]{0,2,1:T(8,128)}, bf16[2,512,12,64]{1,3,2,0:T(8,128)(2,1)}, bf16[2,512,12,64]{1,3,2...) while((s32[]{:T(128)}, f32[1024,12,64]{0,2,1:T(8,128)}, ...), condition=%wide.region_12.13_spmd.clone, body=%wide.region_10.12_spmd.clone.sunk | while | flops 4125747200 | bytes 225634512 | solution.py:210
  258.3 12.3 %fusion.126 = f32[12,512,1024]{2,1,0:T(8,128)} fusion(bf16[1024,12,64]{0,2,1:T(8,128)(2,1)S(1)} %get-tuple-element.570, bf16[2,512,12,64]{1,3,2,0:T(8,128)(2,1)} %get-tuple-element.567, s32[]{:T(128)S(6)} %copy.130), kind=kOutput, calls=%fused_computation.32.clone.1 | convolution fusion | flops 805306368 | bytes 27525124 | tf_op jit(solution)/shard_map/while/body/eval_jaxpr/qhd,khd->hqk/dot_general | solution.py:71
  270.5 13.5 %bitcast_add_fusion.5 = f32[1024,12,64]{0,2,1:T(8,128)} fusion(f32[1024,12,64]{0,2,1:T(8,128)} %get-tuple-element.552, f32[12,512,1024]{2,1,0:T(8,128)} %fusion.126, f32[12,512]{1,0:T(8,128)S(1)} %dynamic-slice_bitcast_fusion.2, pred[512,1024]{1,0:T(8,128)(4,1)S(1)} %broadcast_compare_fusion.5, pred[]{:T(512)S(6)} %compare.3, ...), kind=kOutput, calls=%fused_computation.24.clone.1 | convolution fusion | flops 832045056 | bytes 32800772 | tf_op jit(solution)/shard_map/while/body/eval_jaxpr/hqk,qhd->khd/dot_general | solution.py:188
  284.0 18.3 %multiply_reduce_fusion.5 = (f32[12,512]{1,0:T(8,128)S(1)}, f32[12,512,1024]{2,1,0:T(8,128)}) fusion(f32[12,512,1024]{2,1,0:T(8,128)} %fusion.126, f32[12,512]{1,0:T(8,128)S(1)} %dynamic-slice_bitcast_fusion.2, pred[512,1024]{1,0:T(8,128)(4,1)S(1)} %broadcast_compare_fusion.5, bf16[1024,12,64]{0,2,1:T(8,128)(2,1)} %get-tuple-element.573, ...), kind=kOutput, calls=%fused_computation.19.clone.1 | convolution fusion | flops 836757504 | bytes 53264388 | tf_op jit(solution)/shard_map/while/body/eval_jaxpr/qhd,khd->hqk/dot_general | solution.py:191
  302.3 21.3 %multiply_convert_fusion.3 = bf16[12,512,1024]{2,1,0:T(8,128)(2,1)} fusion(f32[12,512,1024]{2,1,0:T(8,128)} %get-tuple-element.508, f32[12,512,1024]{2,1,0:T(8,128)} %fusion.126, f32[12,512]{1,0:T(8,128)S(1)} %get-tuple-element.509, f32[12,512]{1,0:T(8,128)S(1)} %dynamic-slice_bitcast_fusion.2, pred[512,1024]{1,0:T(8,128)(4,1)S(1)} %broadcast_compare_fusion.5), kind=kLoop, calls=%fused_computation.18.clone.1 | loop fusion | flops 37748736 | bytes 63488000 | tf_op jit(solution)/shard_map/while/body/eval_jaxpr/convert_element_type | solution.py:195
  323.6 9.5 %bitcast_dynamic-update-slice_fusion.5 = bf16[2,512,12,64]{1,3,2,0:T(8,128)(2,1)} fusion(bf16[2,512,12,64]{1,3,2,0:T(8,128)(2,1)} %get-tuple-element.553, s32[]{:T(128)S(6)} %copy.130, bf16[12,512,1024]{2,1,0:T(8,128)(2,1)} %multiply_convert_fusion.3, bf16[1024,12,64]{0,2,1:T(8,128)(2,1)S(1)} %get-tuple-element.570), kind=kOutput, calls=%fused_computation.26.clone.1 | convolution fusion | flops 805699584 | bytes 15728644 | tf_op jit(solution)/shard_map/while/body/eval_jaxpr/hqk,khd->qhd/dot_general | solution.py:197
  333.1 8.6 %bitcast_add_fusion.4 = f32[1024,12,64]{0,2,1:T(8,128)} fusion(f32[1024,12,64]{0,2,1:T(8,128)} %get-tuple-element.551, bf16[12,512,1024]{2,1,0:T(8,128)(2,1)} %multiply_convert_fusion.3, pred[]{:T(512)S(6)} %compare.3, bf16[2,512,12,64]{1,3,2,0:T(8,128)(2,1)S(1)} %copy-done.5, s32[]{:T(128)S(6)} %copy.130), kind=kOutput, calls=%fused_computation.25.clone.1 | convolution fusion | flops 807665664 | bytes 19660804 | tf_op jit(solution)/shard_map/while/body/eval_jaxpr/hqk,qhd->khd/dot_general | solution.py:202
  342.1 11.4 %fusion.126 = f32[12,512,1024]{2,1,0:T(8,128)} fusion(bf16[1024,12,64]{0,2,1:T(8,128)(2,1)S(1)} %get-tuple-element.570, bf16[2,512,12,64]{1,3,2,0:T(8,128)(2,1)} %get-tuple-element.567, s32[]{:T(128)S(6)} %copy.130), kind=kOutput, calls=%fused_computation.32.clone.1 | convolution fusion | flops 805306368 | bytes 27525124 | tf_op jit(solution)/shard_map/while/body/eval_jaxpr/qhd,khd->hqk/dot_general | solution.py:71
  353.5 14.4 %bitcast_add_fusion.5 = f32[1024,12,64]{0,2,1:T(8,128)} fusion(f32[1024,12,64]{0,2,1:T(8,128)} %get-tuple-element.552, f32[12,512,1024]{2,1,0:T(8,128)} %fusion.126, f32[12,512]{1,0:T(8,128)S(1)} %dynamic-slice_bitcast_fusion.2, pred[512,1024]{1,0:T(8,128)(4,1)S(1)} %broadcast_compare_fusion.5, pred[]{:T(512)S(6)} %compare.3, ...), kind=kOutput, calls=%fused_computation.24.clone.1 | convolution fusion | flops 832045056 | bytes 32800772 | tf_op jit(solution)/shard_map/while/body/eval_jaxpr/hqk,qhd->khd/dot_general | solution.py:188
  367.9 18.1 %multiply_reduce_fusion.5 = (f32[12,512]{1,0:T(8,128)S(1)}, f32[12,512,1024]{2,1,0:T(8,128)}) fusion(f32[12,512,1024]{2,1,0:T(8,128)} %fusion.126, f32[12,512]{1,0:T(8,128)S(1)} %dynamic-slice_bitcast_fusion.2, pred[512,1024]{1,0:T(8,128)(4,1)S(1)} %broadcast_compare_fusion.5, bf16[1024,12,64]{0,2,1:T(8,128)(2,1)} %get-tuple-element.573, ...), kind=kOutput, calls=%fused_computation.19.clone.1 | convolution fusion | flops 836757504 | bytes 53264388 | tf_op jit(solution)/shard_map/while/body/eval_jaxpr/qhd,khd->hqk/dot_general | solution.py:191
  386.0 21.3 %multiply_convert_fusion.3 = bf16[12,512,1024]{2,1,0:T(8,128)(2,1)} fusion(f32[12,512,1024]{2,1,0:T(8,128)} %get-tuple-element.508, f32[12,512,1024]{2,1,0:T(8,128)} %fusion.126, f32[12,512]{1,0:T(8,128)S(1)} %get-tuple-element.509, f32[12,512]{1,0:T(8,128)S(1)} %dynamic-slice_bitcast_fusion.2, pred[512,1024]{1,0:T(8,128)(4,1)S(1)} %broadcast_compare_fusion.5), kind=kLoop, calls=%fused_computation.18.clone.1 | loop fusion | flops 37748736 | bytes 63488000 | tf_op jit(solution)/shard_map/while/body/eval_jaxpr/convert_element_type | solution.py:195
  407.3 9.6 %bitcast_dynamic-update-slice_fusion.5 = bf16[2,512,12,64]{1,3,2,0:T(8,128)(2,1)} fusion(bf16[2,512,12,64]{1,3,2,0:T(8,128)(2,1)} %get-tuple-element.553, s32[]{:T(128)S(6)} %copy.130, bf16[12,512,1024]{2,1,0:T(8,128)(2,1)} %multiply_convert_fusion.3, bf16[1024,12,64]{0,2,1:T(8,128)(2,1)S(1)} %get-tuple-element.570), kind=kOutput, calls=%fused_computation.26.clone.1 | convolution fusion | flops 805699584 | bytes 15728644 | tf_op jit(solution)/shard_map/while/body/eval_jaxpr/hqk,khd->qhd/dot_general | solution.py:197
  416.9 9.5 %bitcast_add_fusion.4 = f32[1024,12,64]{0,2,1:T(8,128)} fusion(f32[1024,12,64]{0,2,1:T(8,128)} %get-tuple-element.551, bf16[12,512,1024]{2,1,0:T(8,128)(2,1)} %multiply_convert_fusion.3, pred[]{:T(512)S(6)} %compare.3, bf16[2,512,12,64]{1,3,2,0:T(8,128)(2,1)S(1)} %copy-done.5, s32[]{:T(128)S(6)} %copy.130), kind=kOutput, calls=%fused_computation.25.clone.1 | convolution fusion | flops 807665664 | bytes 19660804 | tf_op jit(solution)/shard_map/while/body/eval_jaxpr/hqk,qhd->khd/dot_general | solution.py:202
  426.5 3.2 copy.96
  430.4 2.7 convert.14
  434.3 7.0 fusion.55
  442.1 10.8 %fusion.60 = f32[768,3072]{1,0:T(8,128)} fusion(bf16[1024,3072]{1,0:T(8,128)(2,1)} %get-tuple-element.385, f32[1024,768]{0,1:T(8,128)} %copy-done.12, f32[768]{0:T(1024)S(1)} %copy-done.52, f32[768]{0:T(1024)S(1)} %copy-done.43, f32[1024]{0:T(1024)S(1)} %copy-done.45, f32[1024]{0:T(1024)S(1)} %copy-done.35), kind=kOutput, calls=%fused_computation.121 | convolution fusion | flops 4835770368 | bytes 18888704 | tf_op jit(solution)/shard_map/td,tf->df/dot_general | solution.py:138
  452.9 10.7 %fusion.71 = f32[3072,768]{1,0:T(8,128)} fusion(bf16[1024,3072]{1,0:T(8,128)(2,1)} %get-tuple-element.364, bf16[1024,768]{1,0:T(8,128)(2,1)} %param.33), kind=kOutput, calls=%fused_computation.130 | convolution fusion | flops 4831838208 | bytes 17301504 | tf_op jit(solution)/shard_map/tf,td->fd/dot_general | solution.py:131
  465.0 3.2 fusion.58
  469.7 10.6 %add_add_fusion.3 = f32[1024,768]{0,1:T(8,128)} fusion(f32[1024,768]{0,1:T(8,128)} %copy-done.12, bf16[1024,3072]{1,0:T(8,128)(2,1)} %get-tuple-element.364, bf16[3072,768]{1,0:T(8,128)(2,1)} %all-gather.13.cloned.1.call-done, f32[768]{0:T(1024)S(1)} %convert_element_type.160), kind=kOutput, calls=%fused_computation.90 | convolution fusion | flops 4833411072 | bytes 17304576 | tf_op jit(solution)/shard_map/dot_general | solution.py:116
  480.3 5.5 fusion.68
  485.8 3.5 copy.100
  489.3 3.5 copy.97
  494.5 12.8 %reduce-scatter.8.cloned.1.call-done = f32[96,2304]{1,0:T(8,128)} async-done(((f32[768,2304]{1,0:T(8,128)}), f32[96,2304]{1,0:T(8,128)}) %reduce-scatter.8.cloned.1.call-update) | async-done | bytes 884752 | tf_op jit(solution)/shard_map/reduce_scatter | solution.py:249
  507.4 2.0 convert_element_type.169
  509.3 78.4 %reduce-scatter.12.cloned.1.call-done = f32[96,3072]{1,0:T(8,128)} async-done(((f32[768,3072]{1,0:T(8,128)}), f32[96,3072]{1,0:T(8,128)}) %reduce-scatter.12.cloned.1.call-update) | async-done | bytes 1179664 | tf_op jit(solution)/shard_map/reduce_scatter | solution.py:157
  587.7 2.2 convert_element_type.183
  589.9 78.2 %reduce-scatter.14.cloned.1.call-done = f32[384,768]{1,0:T(8,128)} async-done(((f32[3072,768]{1,0:T(8,128)}), f32[384,768]{1,0:T(8,128)}) %reduce-scatter.14.cloned.1.call-update) | async-done | bytes 1179664 | tf_op jit(solution)/shard_map/reduce_scatter | solution.py:159
  668.1 2.1 convert_element_type.188
  670.2 2.6 fusion.50
  675.2 3.3 convert_reduce_fusion.2
  678.5 23.3 %all-reduce.13 = (bf16[768]{0:T(1024)(128)(2,1)S(1)}, bf16[768]{0:T(1024)(128)(2,1)S(1)}, bf16[768]{0:T(1024)(128)(2,1)S(1)}, bf16[768]{0:T(1024)(128)(2,1)S(1)}...) all-reduce(f32[768]{0:T(1024)S(1)} %get-tuple-element.293, ...), channel_id=2, replica_groups=mesh['fsdp'=8,'dp'=4] {'fsdp'}, use_global_device_ids=true, to_apply=%region_16.17.clone | all-reduce | flops 7680 | bytes 46080
  702.2 3.5 copy.101
  706.7 11.9 %all-reduce.15 = (bf16[96]{0:T(256)(128)(2,1)S(1)}, bf16[96]{0:T(256)(128)(2,1)S(1)}, bf16[2,96]{1,0:T(2,128)(2,1)S(1)}, bf16[96]{0:T(256)(128)(2,1)S(1)}, bf16[...) all-reduce(bf16[96]{0:T(256)(128)(2,1)S(1)} %dynamic-slice.33, ...), channel_id=1, replica_groups=mesh['fsdp'=8,'dp'=4] {'dp'}, use_global_device_ids=true, to_apply=%region_17.18 | all-reduce | flops 1152 | bytes 4608 | tf_op jit(solution)/shard_map/psum | solution.py:255
  722.9 61.4 %all-reduce.19.cloned.1.call-done = (bf16[96,2304]{1,0:T(8,128)(2,1)}, bf16[96,768]{1,0:T(8,128)(2,1)}, bf16[96,3072]{1,0:T(8,128)(2,1)}, bf16[384,768]{1,0:T(8,128)(2,1)}) async-done(((bf16[96,2304]{1,0:T(8,128)(2,1)}, bf16[96,768]{1,0:T(8,128)(2,1)}, bf16[96,3072]{1,0:T(8,128)(2,1)}, bf16[384,768]{1,0:T(8,128)(2,1)}), (bf16[96,2304]{1,0:T(8,128)(2,1)}, bf16[96,768]{1,0:T(8,128)(2,1)}, ...) | async-done | bytes 1769488 | tf_op jit(solution)/shard_map/psum | solution.py:257
  786.0 2.0 convert_element_type.170
  788.0 2.2 convert_element_type.184
  (239 shorter events, 46.4 us)
Async XLA Ops:
  7.2 62.2 %all-gather.7.cloned.1.call-start = ((), (), s32[]{:S(2)}) async-start(), calls=%async_computation.5 | async-start | bytes 3981312 | tf_op jit(solution)/shard_map/all_gather | solution.py:45
  7.9 158.0 %all-gather.9.cloned.1.call-start = ((), (), s32[]{:S(2)}) async-start(), calls=%async_computation.6 | async-start | bytes 1327104 | tf_op jit(solution)/shard_map/all_gather | solution.py:47
  8.7 161.6 %all-gather.11.cloned.1.call-start = ((), (), s32[]{:S(2)}) async-start(), calls=%async_computation.7 | async-start | bytes 5308416 | tf_op jit(solution)/shard_map/all_gather | solution.py:99
  9.4 199.1 %all-gather.13.cloned.1.call-start = ((), (), s32[]{:S(2)}) async-start(), calls=%async_computation.8 | async-start | bytes 5308416 | tf_op jit(solution)/shard_map/all_gather | solution.py:101
  10.0 482.9 %reduce-scatter.10.cloned.1.call-start = ((), (), s32[]{:S(2)}) async-start(), calls=%async_computation.10 | async-start | bytes 2654208 | tf_op jit(solution)/shard_map/reduce_scatter | solution.py:251
  44.5 24.9 %copy-start.53 = (f32[768]{0:T(1024)}, f32[768]{0:T(1024)S(1)}, u32[]{:S(2)}) copy-start(f32[768]{0:T(1024)S(1)} %convert_element_type.150) | copy-start | bytes 9220
  44.5 24.9 %copy-start.32 = (f32[768]{0:T(1024)}, f32[768]{0:T(1024)S(1)}, u32[]{:S(2)}) copy-start(f32[768]{0:T(1024)S(1)} %convert_element_type.149) | copy-start | bytes 9220
  64.4 3.2 copy-start.21
  66.3 3.2 copy-start.7
  66.5 9.3 %copy-start.30 = (f32[1024]{0:T(1024)}, f32[1024]{0:T(1024)S(1)}, u32[]{:S(2)}) copy-start(f32[1024]{0:T(1024)S(1)} %broadcast_multiply_fusion.1) | copy-start | bytes 12292
  67.6 8.3 %copy-start.36 = (f32[1024]{0:T(1024)}, f32[1024]{0:T(1024)S(1)}, u32[]{:S(2)}) copy-start(f32[1024]{0:T(1024)S(1)} %fusion.53) | copy-start | bytes 12292
  82.3 5.6 copy-start.24
  88.3 23.6 %copy-start.6 = (bf16[1024,12,64]{0,2,1:T(8,128)(2,1)S(1)}, bf16[1024,12,64]{0,2,1:T(8,128)(2,1)}, u32[]{:S(2)}) copy-start(bf16[1024,12,64]{0,2,1:T(8,128)(2,1)} %get-tuple-element.535) | copy-start | bytes 4718596 | tf_op jit(solution)/shard_map/while
  99.4 15.8 %copy-start = (f32[12,512,1024]{2,1,0:T(8,128)S(1)}, f32[12,512,1024]{2,1,0:T(8,128)}, u32[]{:S(2)}) copy-start(f32[12,512,1024]{2,1,0:T(8,128)} %get-tuple-element.495) | copy-start | bytes 75497472 | tf_op jit(solution)/shard_map/while
  124.1 23.8 %copy-start.6 = (bf16[1024,12,64]{0,2,1:T(8,128)(2,1)S(1)}, bf16[1024,12,64]{0,2,1:T(8,128)(2,1)}, u32[]{:S(2)}) copy-start(bf16[1024,12,64]{0,2,1:T(8,128)(2,1)} %get-tuple-element.535) | copy-start | bytes 4718596 | tf_op jit(solution)/shard_map/while
  134.8 16.5 %copy-start = (f32[12,512,1024]{2,1,0:T(8,128)S(1)}, f32[12,512,1024]{2,1,0:T(8,128)}, u32[]{:S(2)}) copy-start(f32[12,512,1024]{2,1,0:T(8,128)} %get-tuple-element.495) | copy-start | bytes 75497472 | tf_op jit(solution)/shard_map/while
  160.1 5.8 copy-start.1
  160.1 5.8 copy-start.4
  160.1 5.8 copy-start.26
  160.1 5.8 copy-start.28
  160.1 5.8 copy-start.55
  169.8 75.0 %copy-start.12 = (f32[1024,768]{0,1:T(8,128)}, f32[1024,768]{0,1:T(8,128)S(1)}, u32[]{:S(2)}) copy-start(f32[1024,768]{0,1:T(8,128)S(1)} %get-tuple-element.378) | copy-start | bytes 9437188
  169.8 75.0 %copy-start.34 = (f32[1024]{0:T(1024)}, f32[1024]{0:T(1024)S(1)}, u32[]{:S(2)}) copy-start(f32[1024]{0:T(1024)S(1)} %broadcast_multiply_fusion) | copy-start | bytes 12292
  170.2 74.6 %copy-start.44 = (f32[1024]{0:T(1024)}, f32[1024]{0:T(1024)S(1)}, u32[]{:S(2)}) copy-start(f32[1024]{0:T(1024)S(1)} %fusion.54) | copy-start | bytes 12292
  241.3 3.6 copy-start.13
  244.8 1.4 copy-start.15
  245.7 1.7 copy-start.10
  245.7 1.7 copy-start.38
  246.2 2.0 copy-start.22
  255.8 1.6 copy-start.2
  255.8 1.6 copy-start.25
  255.8 1.6 copy-start.27
  255.8 1.6 copy-start.29
  257.3 250.1 %reduce-scatter.8.cloned.1.call-start = ((), (), s32[]{:S(2)}) async-start(), calls=%async_computation.9 | async-start | bytes 7962624 | tf_op jit(solution)/shard_map/reduce_scatter | solution.py:249
  258.2 12.3 %copy-start.14 = (bf16[2,512,12,64]{1,3,2,0:T(8,128)(2,1)S(1)}, bf16[2,512,12,64]{1,3,2,0:T(8,128)(2,1)}, u32[]{:S(2)}) copy-start(bf16[2,512,12,64]{1,3,2,0:T(8,128)(2,1)} %get-tuple-element.572) | copy-start | bytes 4718596 | tf_op jit(solution)/shard_map/while
  323.6 9.5 %copy-start.5 = (bf16[2,512,12,64]{1,3,2,0:T(8,128)(2,1)S(1)}, bf16[2,512,12,64]{1,3,2,0:T(8,128)(2,1)}, u32[]{:S(2)}) copy-start(bf16[2,512,12,64]{1,3,2,0:T(8,128)(2,1)} %get-tuple-element.567) | copy-start | bytes 4718596 | tf_op jit(solution)/shard_map/while
  342.1 11.4 %copy-start.14 = (bf16[2,512,12,64]{1,3,2,0:T(8,128)(2,1)S(1)}, bf16[2,512,12,64]{1,3,2,0:T(8,128)(2,1)}, u32[]{:S(2)}) copy-start(bf16[2,512,12,64]{1,3,2,0:T(8,128)(2,1)} %get-tuple-element.572) | copy-start | bytes 4718596 | tf_op jit(solution)/shard_map/while
  407.3 9.6 %copy-start.5 = (bf16[2,512,12,64]{1,3,2,0:T(8,128)(2,1)S(1)}, bf16[2,512,12,64]{1,3,2,0:T(8,128)(2,1)}, u32[]{:S(2)}) copy-start(bf16[2,512,12,64]{1,3,2,0:T(8,128)(2,1)} %get-tuple-element.567) | copy-start | bytes 4718596 | tf_op jit(solution)/shard_map/while
  426.5 3.6 copy-start.3
  430.4 2.8 copy-start.17
  430.4 3.9 copy-start.8
  430.4 3.9 copy-start.31
  430.4 3.9 copy-start.33
  430.4 3.9 copy-start.37
  430.4 3.9 copy-start.54
  433.2 1.1 copy-start.19
  441.4 146.3 %reduce-scatter.12.cloned.1.call-start = ((), (), s32[]{:S(2)}) async-start(), calls=%async_computation.11 | async-start | bytes 10616832 | tf_op jit(solution)/shard_map/reduce_scatter | solution.py:157
  452.9 215.2 %reduce-scatter.14.cloned.1.call-start = ((), (), s32[]{:S(2)}) async-start(), calls=%async_computation.12 | async-start | bytes 10616832 | tf_op jit(solution)/shard_map/reduce_scatter | solution.py:159
  463.6 1.4 copy-start.56
  463.6 242.3 %reduce-scatter.16.cloned.1.call-start = ((), (), s32[]{:S(2)}) async-start(), calls=%async_computation.13 | async-start | bytes 442368
  469.6 314.7 %all-reduce.19.cloned.1.call-start = ((), (), s32[]{:S(2)}) async-start(), calls=%async_computation.14 | async-start | bytes 3538944 | tf_op jit(solution)/shard_map/psum | solution.py:257
  469.6 10.6 %copy-start.18 = (bf16[1024,12,64]{0,2,1:T(8,128)(2,1)S(1)}, bf16[1024,12,64]{0,2,1:T(8,128)(2,1)}, u32[]{:S(2)}) copy-start(bf16[1024,12,64]{0,2,1:T(8,128)(2,1)} %copy-done.17) | copy-start | bytes 4718596
  469.6 10.6 %copy-start.20 = (bf16[1024,12,64]{0,2,1:T(8,128)(2,1)S(1)}, bf16[1024,12,64]{0,2,1:T(8,128)(2,1)}, u32[]{:S(2)}) copy-start(bf16[1024,12,64]{0,2,1:T(8,128)(2,1)} %copy-done.19) | copy-start | bytes 4718596
  469.6 10.6 %copy-start.57 = (bf16[768,2304]{1,0:T(8,128)(2,1)S(1)}, bf16[768,2304]{1,0:T(8,128)(2,1)}, u32[]{:S(2)}) copy-start(bf16[768,2304]{1,0:T(8,128)(2,1)} %all-gather.7.cloned.1.call-done) | copy-start | bytes 10616836
  670.2 2.6 copy-start.41
  670.2 2.8 copy-start.9
  672.8 1.9 copy-start.11
  672.8 2.4 copy-start.16
  672.9 2.4 copy-start.39
  675.2 3.3 copy-start.46
  675.2 3.3 copy-start.47
  675.2 3.3 copy-start.49
  675.2 3.3 copy-start.50
  784.3 5.9 copy-start.23
  (8 other events, 5.6 us)
Sparse Core Ops, SparseCore 0:
  9.9 36.7 all-gather.6
  48.6 23.9 all-gather.8
  74.5 38.7 all-gather.10
  115.0 38.7 all-gather.12
  257.4 42.6 reduce-scatter.9
  441.5 65.8 reduce-scatter.7
  510.9 76.8 reduce-scatter.11
  591.2 76.8 reduce-scatter.13
  671.1 33.8 reduce-scatter.15
  708.7 75.5 all-reduce.18
where the time goes:
time: 809 us; the launch traced here: 798 us
  matrix products  291 us (36%)
  waiting for transfers between devices  234 us (29%)
  other arithmetic  112 us (14%)
  blocking collectives  78.6 us (10%)
  local copies, waits for them, and re-layouts  64.6 us (8%)
  between operations  17.3 us (2%)
    reduce_scatter x1, waiting for transfers between devices, on_device(): lax.psum_scatter(mlp_terms[2], 'fsdp', scatter_dimension=0, tiled=True)  78.4 us
    reduce_scatter x1, waiting for transfers between devices, on_device(): lax.psum_scatter(mlp_terms[4], 'fsdp', scatter_dimension=0, tiled=True)  78.2 us
    psum x1, waiting for transfers between devices, on_device(): lax.psum(attn_sums[2].astype(jnp.bfloat16), 'dp').astype(jnp.float32)  61.4 us
    unnamed x2, blocking collectives  50 us
    dot_general x4, matrix products, masked_scores(): jnp.einsum('qhd,khd->hqk', query_block, key_rows, preferred_element_type=...  45.4 us
    convert_element_type x2, other arithmetic, attend_back(): grad_scores = (weights * (grad_weights - inner)).astype(jnp.bfloat16)  42.6 us
    dot_general x1, matrix products, on_device(): jnp.dot(hidden_second, up_full, preferred_element_type=jnp.float32)  37.9 us
    dot_general x2, matrix products, attend_back(): jnp.einsum('qhd,khd->hqk', grad_block, value_rows, preferred_element_type...  36.4 us
  transfers between devices with their start and end apart: 10, of which 4 were waited for; matrix products, arithmetic and copies ran while one was open for 50% of the time, Pallas kernels for 0%

commit v1 on v0

v1 whole, which is shorter than its diff:
```python
import functools

import jax
import jax.numpy as jnp
from jax import lax
from jax.experimental import pallas as pl
from jax.experimental.pallas import tpu as pltpu
from jax.sharding import PartitionSpec as P

HD = 64
PAIR = 2 * HD
EPS = 1e-06
WIN = 256
SNAP = 16
TILE = 256
CHUNK = 512
LIMIT = 58 << 20
F32 = jnp.float32
BF16 = jnp.bfloat16
NT = (((1,), (1,)), ((), ()))
NN = (((1,), (0,)), ((), ()))


def mm(left, right, dims=NN):
    return lax.dot_general(left, right, dims, preferred_element_type=F32)


def fold(values):
    return jnp.sum(values.reshape(values.shape[0] // 8, 8, values.shape[1]), axis=0)


def swap(value, axis, size, bit):
    return lax.ppermute(value, axis, [(i, i ^ bit) for i in range(size)])


def gather_eight(shard, x_first):
    go = lambda v, bit: swap(v, "fsdp", 8, bit)
    via_x, via_y = go(shard, 2), go(shard, 4)
    far = go(via_x, 4) if x_first else go(via_y, 2)
    own = [shard, via_x, via_y, far]
    pieces = []
    for value in own:
        pieces += [value, go(value, 1)]
    return pieces


def gather_weight(shards, size):
    if size == 8:
        return [(gather_eight(shard, at % 2 == 0), True) for at, shard in enumerate(shards)]
    return [([lax.all_gather(shard, "fsdp", axis=0, tiled=True)], False) for shard in shards]


def pick(value, at, axis):
    return lax.dynamic_index_in_dim(value, at, axis, keepdims=False)


def add_low(left, right):
    return (left.astype(F32) + right.astype(F32)).astype(left.dtype)


def scatter_sum(value, size, x_first):
    if size != 8:
        return lax.psum_scatter(value, "fsdp", scatter_dimension=0, tiled=True)[0]
    me = lax.axis_index("fsdp")
    core, at_x, at_y = me & 1, (me >> 1) & 1, me >> 2
    rows, columns = value.shape[1:]
    pairs = value.reshape(4, 2, rows, columns)
    total = add_low(pick(pairs, core, 1), swap(pick(pairs, 1 - core, 1), "fsdp", 8, 1))
    total = total.reshape(2, 2, rows, columns)
    if x_first:
        total = add_low(pick(total, at_x, 1), swap(pick(total, 1 - at_x, 1), "fsdp", 8, 2))
        return add_low(pick(total, at_y, 0), swap(pick(total, 1 - at_y, 0), "fsdp", 8, 4))
    total = add_low(pick(total, at_y, 0), swap(pick(total, 1 - at_y, 0), "fsdp", 8, 4))
    return add_low(pick(total, at_x, 0), swap(pick(total, 1 - at_x, 0), "fsdp", 8, 2))


def join(mine, other, bit):
    first = jnp.where(bit == 0, mine, other)
    second = jnp.where(bit == 0, other, mine)
    return jnp.concatenate([first, second], axis=0)


def reduce_groups(value, size):
    if size != 4:
        return lax.psum(value, "dp")
    me = lax.axis_index("dp")
    low, high = me & 1, me >> 1
    rows, columns = value.shape
    if rows % 4:
        value = add_low(value, swap(value, "dp", 4, 1))
        return add_low(value, swap(value, "dp", 4, 2))
    half = value.reshape(2, rows // 2, columns)
    half = add_low(pick(half, low, 0), swap(pick(half, 1 - low, 0), "dp", 4, 1))
    part = half.reshape(2, rows // 4, columns)
    part = add_low(pick(part, high, 0), swap(pick(part, 1 - high, 0), "dp", 4, 2))
    half = join(part, swap(part, "dp", 4, 2), high)
    return join(half, swap(half, "dp", 4, 1), low)


class Weight:
    def __init__(self, shape, split, gathered, size):
        self.shape = shape
        self.arrays = []
        self.places = []
        at_row = at_column = 0
        for pieces, is_shard in gathered:
            rows, columns = pieces[0].shape
            for offset, piece in enumerate(pieces):
                if is_shard:
                    step = shape[0] // size
                    self.places.append((len(self.arrays), offset, step, at_row, rows, at_column, columns))
                else:
                    self.places.append((len(self.arrays), None, 0, at_row, rows, at_column, columns))
                self.arrays.append(piece)
            if split == "columns":
                at_column += columns
            else:
                at_row += rows

    def copies(self, me, refs, scratch, sems):
        made = []
        for at, (ref, offset, step, row, rows, column, columns) in enumerate(self.places):
            start = row if offset is None else pl.multiple_of((me ^ offset) * step + row, 16)
            target = scratch.at[pl.ds(start, rows), pl.ds(column, columns)]
            made.append(pltpu.make_async_copy(refs[ref], target, sems.at[at]))
        return made

    def scratch(self):
        return [pltpu.VMEM(self.shape, BF16), pltpu.SemaphoreType.DMA((len(self.places),))]


def any_specs(count):
    return [pl.BlockSpec(memory_space=pl.ANY)] * count


def params():
    return pltpu.CompilerParams(dimension_semantics=("arbitrary",), vmem_limit_bytes=LIMIT)


def cost(flops, reads, exps=0):
    return pl.CostEstimate(flops=int(flops), transcendentals=int(exps), bytes_accessed=int(reads))


def row_spec(columns):
    return pl.BlockSpec((TILE, columns), lambda i, *_: (i, 0))


def whole_spec(shape):
    return pl.BlockSpec(shape, lambda i, *_: (0,) * len(shape))


def normed(values):
    center = values - jnp.mean(values, axis=-1, keepdims=True)
    scale = lax.rsqrt(jnp.mean(center * center, axis=-1, keepdims=True) + EPS)
    return center * scale, scale


def norm_back(grad, unit, scale, gain):
    scaled = grad * gain
    first = jnp.mean(scaled, axis=-1, keepdims=True)
    second = jnp.mean(scaled * unit, axis=-1, keepdims=True)
    return (scaled - first - unit * second) * scale


def load_first(weights, me, refs, scratches):
    @pl.when(pl.program_id(0) == 0)
    def _():
        started = []
        at = 0
        for weight, (scratch, sems) in zip(weights, scratches):
            mine = refs[at : at + len(weight.arrays)]
            at += len(weight.arrays)
            started += weight.copies(me, mine, scratch, sems)
        for copy in started:
            copy.start()
        for copy in started:
            copy.wait()


def joint_kernel(weight, me_ref, x_ref, gain_ref, shift_ref, bias_ref, *refs):
    count = len(weight.arrays)
    out_ref, hidden_ref, scratch, sems = refs[count:]
    load_first([weight], me_ref[0], refs[:count], [(scratch, sems)])
    unit, _ = normed(x_ref[...].astype(F32))
    hidden = (unit * gain_ref[...] + shift_ref[...]).astype(BF16)
    hidden_ref[...] = hidden
    out_ref[...] = (mm(hidden, scratch[...]) + bias_ref[...]).astype(BF16)


def joint_forward(me, tokens, gain, shift, bias, weight):
    rows, width = tokens.shape
    columns = weight.shape[1]
    return pl.pallas_call(
        functools.partial(joint_kernel, weight),
        grid_spec=pltpu.PrefetchScalarGridSpec(
            num_scalar_prefetch=1,
            grid=(rows // TILE,),
            in_specs=[row_spec(width), whole_spec((1, width)), whole_spec((1, width)), whole_spec((1, columns))]
            + any_specs(len(weight.arrays)),
            out_specs=[row_spec(columns), row_spec(width)],
            scratch_shapes=weight.scratch(),
        ),
        out_shape=[jax.ShapeDtypeStruct((rows, columns), BF16), jax.ShapeDtypeStruct((rows, width), BF16)],
        compiler_params=params(),
        cost_estimate=cost(2 * rows * width * columns, 2 * (rows * (2 * width + columns) + width * columns)),
        name="joint_forward",
    )(me, tokens, gain, shift, bias, *weight.arrays)


def plan_groups(starts_ref, crops_ref, table_ref, bias_ref, rows):
    def one(state):
        at, start = state
        base = jnp.minimum((start // SNAP) * SNAP, rows - WIN)
        base = pl.multiple_of(base, SNAP)
        edge = base + WIN
        stop = jnp.where(edge >= rows, rows, starts_ref[jnp.minimum(edge, rows - 1)])
        table_ref[0, at] = base
        table_ref[1, at] = start
        down = crops_ref[pl.ds(base, WIN), :]
        across = down.T
        down = jnp.concatenate([down] * (WIN // 128), axis=1)
        across = jnp.concatenate([across] * (WIN // 128), axis=0)
        bias_ref[at] = jnp.where(down == across, 0.0, -1e30)
        return at + 1, stop

    more = lambda state: jnp.logical_and(state[1] < rows, state[0] < group_bound(rows))
    table_ref[2, 0] = lax.while_loop(more, one, (jnp.int32(0), jnp.int32(0)))[0]


def group_bound(rows):
    return 2 * (rows // (WIN - SNAP + 2)) + 2


def keep_from(ref, base, start, columns, value):
    window = (pl.ds(base, WIN), pl.ds(columns, PAIR))
    row = base + lax.broadcasted_iota(jnp.int32, (WIN, PAIR), 0)
    ref[window] = jnp.where(row >= start, value, ref[window].astype(F32)).astype(ref.dtype)


def attend_kernel(rows, starts_ref, crops_ref, joint_ref, mixed_ref, log_ref, table_ref, bias_ref):
    @pl.when(pl.program_id(0) == 0)
    def _():
        plan_groups(starts_ref, crops_ref, table_ref, bias_ref, rows)

    lane = lax.broadcasted_iota(jnp.int32, (WIN, PAIR), 1)

    def one(at, carry):
        base = pl.multiple_of(table_ref[0, at], SNAP)
        start = table_ref[1, at]
        window = pl.ds(base, WIN)
        query = joint_ref[window, 0:PAIR] * jnp.asarray(HD**-0.5, BF16)
        key = joint_ref[window, PAIR : 2 * PAIR]
        value_t = joint_ref[window, 2 * PAIR : 3 * PAIR].T
        outs = []
        for head in range(2):
            mine = (lane >= HD) if head else (lane < HD)
            scores = mm(jnp.where(mine, key, jnp.zeros_like(key)), query, NT) + bias_ref[at]
            top = jnp.max(scores, axis=0, keepdims=True)
            expo = jnp.exp(scores - top)
            total = jnp.sum(expo, axis=0, keepdims=True)
            mixed = mm(value_t[head * HD : (head + 1) * HD, :], expo.astype(BF16))
            outs.append(mixed * (1.0 / total))
            log_ref[0, at, pl.ds(head, 1), :] = top + jnp.log(total)
        keep_from(mixed_ref, base, start, 0, jnp.concatenate(outs, axis=0).T)
        return carry

    lax.fori_loop(0, table_ref[2, 0], one, 0)


def attend(starts, crops, joint):
    rows, columns = joint.shape
    pairs = columns // (3 * PAIR)
    groups = group_bound(rows)
    return pl.pallas_call(
        functools.partial(attend_kernel, rows),
        grid_spec=pltpu.PrefetchScalarGridSpec(
            num_scalar_prefetch=1,
            grid=(pairs,),
            in_specs=[whole_spec((rows, 128)), pl.BlockSpec((rows, 3 * PAIR), lambda i, *_: (0, i))],
            out_specs=[
                pl.BlockSpec((rows, PAIR), lambda i, *_: (0, i)),
                pl.BlockSpec((1, groups, 8, WIN), lambda i, *_: (i, 0, 0, 0)),
            ],
            scratch_shapes=[pltpu.SMEM((3, 16), jnp.int32), pltpu.VMEM((groups, WIN, WIN), F32)],
        ),
        out_shape=[
            jax.ShapeDtypeStruct((rows, pairs * PAIR), BF16),
            jax.ShapeDtypeStruct((pairs, groups, 8, WIN), F32),
        ],
        compiler_params=params(),
        cost_estimate=cost(pairs * 6 * 8 * WIN**3, 2 * rows * columns * 4 // 3, pairs * 12 * WIN * WIN),
        name="attend",
    )(starts, crops, joint)


def attend_back_kernel(rows, starts_ref, crops_ref, joint_ref, mixed_ref, grad_ref, log_ref, out_ref, table_ref, bias_ref):
    @pl.when(pl.program_id(0) == 0)
    def _():
        plan_groups(starts_ref, crops_ref, table_ref, bias_ref, rows)

    lane = lax.broadcasted_iota(jnp.int32, (WIN, PAIR), 1)

    def one(at, carry):
        base = pl.multiple_of(table_ref[0, at], SNAP)
        start = table_ref[1, at]
        window = pl.ds(base, WIN)
        query = joint_ref[window, 0:PAIR] * jnp.asarray(HD**-0.5, BF16)
        key = joint_ref[window, PAIR : 2 * PAIR]
        value = joint_ref[window, 2 * PAIR : 3 * PAIR]
        key_t = key.T
        grad = grad_ref[window, :]
        inner_t = (grad.astype(F32) * mixed_ref[window, :].astype(F32)).T
        d_query, d_key, d_value = [], [], []
        for head in range(2):
            mine = (lane >= HD) if head else (lane < HD)
            zero = jnp.zeros_like(key)
            scores = mm(jnp.where(mine, key, zero), query, NT) + bias_ref[at]
            weights = jnp.exp(scores - log_ref[0, at, pl.ds(head, 1), :])
            inner = jnp.sum(inner_t[head * HD : (head + 1) * HD, :], axis=0, keepdims=True)
            d_weights = mm(jnp.where(mine, value, zero), grad, NT)
            d_scores = (weights * (d_weights - inner)).astype(BF16)
            d_value.append(mm(weights.astype(BF16), grad))
            d_key.append(mm(d_scores, query))
            d_query.append(mm(key_t[head * HD : (head + 1) * HD, :], d_scores) * HD**-0.5)
        low = lane < HD
        keep_from(out_ref, base, start, 0, jnp.concatenate(d_query, axis=0).T)
        keep_from(out_ref, base, start, PAIR, jnp.where(low, d_key[0], d_key[1]))
        keep_from(out_ref, base, start, 2 * PAIR, jnp.where(low, d_value[0], d_value[1]))
        return carry

    lax.fori_loop(0, table_ref[2, 0], one, 0)


def attend_back(starts, crops, joint, mixed, grad, logs, first, count):
    rows = joint.shape[0]
    groups = group_bound(rows)
    wide = lambda columns: pl.BlockSpec((rows, columns), lambda i, *_: (0, first + i))
    return pl.pallas_call(
        functools.partial(attend_back_kernel, rows),
        grid_spec=pltpu.PrefetchScalarGridSpec(
            num_scalar_prefetch=1,
            grid=(count,),
            in_specs=[
                whole_spec((rows, 128)),
                wide(3 * PAIR),
                wide(PAIR),
                wide(PAIR),
                pl.BlockSpec((1, groups, 8, WIN), lambda i, *_: (first + i, 0, 0, 0)),
            ],
            out_specs=pl.BlockSpec((rows, 3 * PAIR), lambda i, *_: (0, i)),
            scratch_shapes=[pltpu.SMEM((3, 16), jnp.int32), pltpu.VMEM((groups, WIN, WIN), F32)],
        ),
        out_shape=jax.ShapeDtypeStruct((rows, count * 3 * PAIR), BF16),
        compiler_params=params(),
        cost_estimate=cost(count * 6 * 20 * WIN**3, 2 * rows * count * 8 * PAIR, count * 12 * WIN * WIN),
        name="attend_back",
    )(starts, crops, joint, mixed, grad, logs)


def up_kernel(out_weight, up_weight, me_ref, x_ref, mixed_ref, vec_ref, bias_ref, *refs):
    count = len(out_weight.arrays) + len(up_weight.arrays)
    middle_ref, hidden_ref, active_ref, slope_ref, out_s, out_sem, up_s, up_sem = refs[count:]
    load_first([out_weight, up_weight], me_ref[0], refs[:count], [(out_s, out_sem), (up_s, up_sem)])
    middle = x_ref[...].astype(F32) + mm(mixed_ref[...], out_s[...]) + vec_ref[0:1, :]
    middle_ref[...] = middle
    unit, _ = normed(middle)
    hidden = (unit * vec_ref[1:2, :] + vec_ref[2:3, :]).astype(BF16)
    hidden_ref[...] = hidden
    for at in range(0, up_weight.shape[1], CHUNK):
        part = pl.ds(at, CHUNK)
        value = mm(hidden, up_s[:, part]) + bias_ref[:, part]
        below = 0.5 + 0.5 * lax.erf(value * (0.5**0.5))
        active_ref[:, part] = (value * below).astype(BF16)
        bell = jnp.exp(value * value * -0.5) * 0.3989422804014327
        slope_ref[:, part] = (below + value * bell).astype(BF16)


def up_forward(me, tokens, mixed, vectors, bias, out_weight, up_weight):
    rows, width = tokens.shape
    inner = up_weight.shape[1]
    arrays = out_weight.arrays + up_weight.arrays
    return pl.pallas_call(
        functools.partial(up_kernel, out_weight, up_weight),
        grid_spec=pltpu.PrefetchScalarGridSpec(
            num_scalar_prefetch=1,
            grid=(rows // TILE,),
            in_specs=[row_spec(width), row_spec(width), whole_spec(vectors.shape), whole_spec((1, inner))]
            + any_specs(len(arrays)),
            out_specs=[row_spec(width), row_spec(width), row_spec(inner), row_spec(inner)],
            scratch_shapes=out_weight.scratch() + up_weight.scratch(),
        ),
        out_shape=[
            jax.ShapeDtypeStruct((rows, width), F32),
            jax.ShapeDtypeStruct((rows, width), BF16),
            jax.ShapeDtypeStruct((rows, inner), BF16),
            jax.ShapeDtypeStruct((rows, inner), BF16),
        ],
        compiler_params=params(),
        cost_estimate=cost(2 * rows * width * (width + inner), rows * (10 * width + 4 * inner) + 2 * width * inner, rows * inner * 2),
        name="up_forward",
    )(me, tokens, mixed, vectors, bias, *arrays)


def middle_kernel(
    out_weight, up_weight, down_weight, me_ref, middle_ref, grad_ref, active_ref, slope_ref, vec_ref, *refs
):
    weights = [out_weight, up_weight, down_weight]
    count = sum(len(weight.arrays) for weight in weights)
    refs, rest = refs[:count], refs[count:]
    acts_ref, ga_ref, gmid_ref, glow_ref, gmix_ref, sums_ref, upsum_ref = rest[:7]
    out_s, out_sem, up_s, up_sem, down_s, down_sem = rest[7:]
    load_first(weights, me_ref[0], refs, [(out_s, out_sem), (up_s, up_sem), (down_s, down_sem)])

    @pl.when(pl.program_id(0) == 0)
    def _():
        sums_ref[...] = jnp.zeros_like(sums_ref)
        upsum_ref[...] = jnp.zeros_like(upsum_ref)

    middle = middle_ref[...]
    grad = grad_ref[...]
    acts_ref[...] = middle + mm(active_ref[...], down_s[...]) + vec_ref[3:4, :]
    total = None
    for at in range(0, up_weight.shape[1], CHUNK):
        part = pl.ds(at, CHUNK)
        inner = (mm(grad, down_s[part, :], NT) * slope_ref[:, part].astype(F32)).astype(BF16)
        ga_ref[:, part] = inner
        upsum_ref[:, part] += fold(inner.astype(F32))
        term = mm(inner, up_s[:, part], NT)
        total = term if total is None else total + term
    unit, scale = normed(middle)
    wide = grad.astype(F32)
    sums_ref[0] += fold(total * unit)
    sums_ref[1] += fold(total)
    sums_ref[2] += fold(wide)
    gmid = wide + norm_back(total, unit, scale, vec_ref[1:2, :])
    gmid_ref[...] = gmid
    low = gmid.astype(BF16)
    glow_ref[...] = low
    sums_ref[3] += fold(low.astype(F32))
    gmix_ref[...] = mm(low, out_s[...], NT).astype(BF16)


def middle_back(me, middle, grad, active, slope, vectors, out_weight, up_weight, down_weight):
    rows, width = middle.shape
    inner = active.shape[1]
    arrays = out_weight.arrays + up_weight.arrays + down_weight.arrays
    return pl.pallas_call(
        functools.partial(middle_kernel, out_weight, up_weight, down_weight),
        grid_spec=pltpu.PrefetchScalarGridSpec(
            num_scalar_prefetch=1,
            grid=(rows // TILE,),
            in_specs=[row_spec(width), row_spec(width), row_spec(inner), row_spec(inner), whole_spec(vectors.shape)]
            + any_specs(len(arrays)),
            out_specs=[
                row_spec(width),
                row_spec(inner),
                row_spec(width),
                row_spec(width),
                row_spec(width),
                whole_spec((4, 8, width)),
                whole_spec((8, inner)),
            ],
            scratch_shapes=out_weight.scratch() + up_weight.scratch() + down_weight.scratch(),
        ),
        out_shape=[
            jax.ShapeDtypeStruct((rows, width), F32),
            jax.ShapeDtypeStruct((rows, inner), BF16),
            jax.ShapeDtypeStruct((rows, width), F32),
            jax.ShapeDtypeStruct((rows, width), BF16),
            jax.ShapeDtypeStruct((rows, width), BF16),
            jax.ShapeDtypeStruct((4, 8, width), F32),
            jax.ShapeDtypeStruct((8, inner), F32),
        ],
        compiler_params=params(),
        cost_estimate=cost(2 * rows * width * (width + 3 * inner), rows * (18 * width + 6 * inner) + 4 * width * inner),
        name="middle_back",
    )(me, middle, grad, active, slope, vectors, *arrays)


def first_kernel(weight, me_ref, x_ref, gmid_ref, part_a_ref, part_b_ref, gain_ref, *refs):
    count = len(weight.arrays)
    out_ref, sums_ref, joint_sum_ref, scratch, sems = refs[count:]
    load_first([weight], me_ref[0], refs[:count], [(scratch, sems)])

    @pl.when(pl.program_id(0) == 0)
    def _():
        sums_ref[...] = jnp.zeros_like(sums_ref)
        joint_sum_ref[...] = jnp.zeros_like(joint_sum_ref)

    grad = jnp.concatenate([part_a_ref[...], part_b_ref[...]], axis=1)
    joint_sum_ref[...] += fold(grad.astype(F32))
    total = mm(grad, scratch[...], NT)
    unit, scale = normed(x_ref[...].astype(F32))
    sums_ref[0] += fold(total * unit)
    sums_ref[1] += fold(total)
    out_ref[...] = gmid_ref[...] + norm_back(total, unit, scale, gain_ref[...])


def first_back(me, tokens, gmid, part_a, part_b, gain, weight):
    rows, width = tokens.shape
    columns = weight.shape[1]
    return pl.pallas_call(
        functools.partial(first_kernel, weight),
        grid_spec=pltpu.PrefetchScalarGridSpec(
            num_scalar_prefetch=1,
            grid=(rows // TILE,),
            in_specs=[row_spec(width), row_spec(width), row_spec(columns // 2), row_spec(columns // 2), whole_spec((1, width))]
            + any_specs(len(weight.arrays)),
            out_specs=[row_spec(width), whole_spec((2, 8, width)), whole_spec((8, columns))],
            scratch_shapes=weight.scratch(),
        ),
        out_shape=[
            jax.ShapeDtypeStruct((rows, width), F32),
            jax.ShapeDtypeStruct((2, 8, width), F32),
            jax.ShapeDtypeStruct((8, columns), F32),
        ],
        compiler_params=params(),
        cost_estimate=cost(2 * rows * width * columns, rows * (10 * width + 2 * columns) + 2 * width * columns),
        name="first_back",
    )(me, tokens, gmid, part_a, part_b, gain, *weight.arrays)


def by_pair(matrix, parts):
    rows, columns = matrix.shape
    pairs = columns // (parts * PAIR)
    return matrix.reshape(rows, parts, pairs, PAIR).transpose(0, 2, 1, 3).reshape(rows, columns)


def by_part(matrix, parts):
    rows, columns = matrix.shape
    pairs = columns // (parts * PAIR)
    return matrix.reshape(rows, pairs, parts, PAIR).transpose(0, 2, 1, 3).reshape(rows, columns)


def weight_grad(left, right):
    return lax.dot_general(left, right, (((0,), (0,)), ((), ())), preferred_element_type=F32).astype(BF16)


def on_device(
    fsdp,
    dp,
    tokens,
    crop_ids,
    gain_first,
    shift_first,
    joint_weight,
    joint_bias,
    output_weight,
    output_bias,
    gain_second,
    shift_second,
    up_weight,
    up_bias,
    down_weight,
    down_bias,
    cotangent,
):
    rows, width = tokens.shape
    inner = up_bias.shape[0] * fsdp
    joint_width = joint_weight.shape[1]
    rank = lax.axis_index("fsdp")
    me = rank.astype(jnp.int32).reshape(1)
    own = width // fsdp
    own_up = inner // fsdp

    pack = jnp.concatenate(
        [
            gain_first,
            shift_first,
            joint_bias.reshape(-1),
            output_bias,
            gain_second,
            shift_second,
            down_bias,
            up_bias,
        ]
    ).reshape(1, -1)
    if fsdp == 8:
        pieces = jnp.concatenate([pack] + [swap(pack, "fsdp", 8, k) for k in range(1, 8)], axis=0)
        order = (jnp.arange(8)[:, None] ^ rank) == jnp.arange(8)[None, :]
        vectors = mm(order.astype(BF16), pieces)
    else:
        vectors = lax.all_gather(pack, "fsdp", axis=0, tiled=True).astype(F32)
    small = vectors[:, : 8 * own].reshape(fsdp, 8, own).transpose(1, 0, 2).reshape(8, width)
    up_row = vectors[:, 8 * own :].reshape(1, inner)
    gain_one, shift_one = small[0:1], small[1:2]
    bias_joint = jnp.concatenate([small[2:3], jnp.zeros((1, width), F32), small[3:4]], axis=1)
    bias_joint = by_pair(bias_joint, 3)
    second = jnp.stack([small[4], small[5], small[6], small[7]] + [jnp.zeros((width,), F32)] * 4)

    paired = by_pair(joint_weight, 3)
    half = joint_width // 2
    joint_parts = gather_weight([paired[:, :half], paired[:, half:]], fsdp)
    joint_full = Weight((width, joint_width), "columns", joint_parts, fsdp)
    gate = joint_full.arrays[-1]
    output_in, up_in, gate = lax.optimization_barrier((output_weight, up_weight, gate))
    out_full = Weight((width, width), "columns", gather_weight([output_in], fsdp), fsdp)
    cut = inner // 2
    up_full = Weight((width, inner), "columns", gather_weight([up_in[:, :cut], up_in[:, cut:]], fsdp), fsdp)
    down_in, gate = lax.optimization_barrier((down_weight, up_full.arrays[-1]))
    if fsdp == 8:
        cut = own_up // 2
        down_parts = gather_weight([down_in[:cut], down_in[cut:]], fsdp)
    else:
        down_parts = gather_weight([down_in], fsdp)
    down_full = Weight((inner, width), "rows", down_parts, fsdp)

    starts = jnp.sum((crop_ids[None, :] < crop_ids[:, None]).astype(jnp.int32), axis=1)
    crops = jnp.broadcast_to(crop_ids.astype(F32)[:, None], (rows, 128))

    joint, hidden_first = joint_forward(me, tokens, gain_one, shift_one, bias_joint, joint_full)
    mixed, logs = attend(starts, crops, joint)
    middle, hidden_second, active, slope = up_forward(me, tokens, mixed, second, up_row, out_full, up_full)
    acts, grad_up, grad_middle, grad_low, grad_mixed, sums, up_sums = middle_back(
        me, middle, cotangent, active, slope, second, out_full, up_full, down_full
    )

    def finish(slabs, x_first):
        return reduce_groups(scatter_sum(slabs, fsdp, x_first), dp)

    down_sum = finish(weight_grad(active, cotangent).reshape(fsdp, own_up, width), False)
    up_sum = finish(weight_grad(hidden_second, grad_up).reshape(fsdp, own, inner), True)
    out_sum = finish(weight_grad(mixed, grad_low).reshape(fsdp, own, width), False)

    pairs = joint_width // (3 * PAIR)
    near = pairs // 2
    grad_a = attend_back(starts, crops, joint, mixed, grad_mixed, logs, 0, near)
    sum_a = finish(weight_grad(hidden_first, grad_a).reshape(fsdp, own, -1), True)
    grad_b = attend_back(starts, crops, joint, mixed, grad_mixed, logs, near, pairs - near)
    sum_b = finish(weight_grad(hidden_first, grad_b).reshape(fsdp, own, -1), False)
    input_grad, first_sums, joint_sums = first_back(me, tokens, grad_middle, grad_a, grad_b, gain_one, joint_full)

    joint_row = by_part(jnp.sum(joint_sums, axis=0, keepdims=True), 3)
    rows_out = jnp.stack(
        [
            jnp.sum(first_sums[0], axis=0),
            jnp.sum(first_sums[1], axis=0),
            joint_row[0, :width],
            joint_row[0, 2 * width :],
            jnp.sum(sums[3], axis=0),
            jnp.sum(sums[0], axis=0),
            jnp.sum(sums[1], axis=0),
            jnp.sum(sums[2], axis=0),
        ]
    )
    packed = jnp.concatenate(
        [
            rows_out.reshape(8, fsdp, own).transpose(1, 0, 2).reshape(fsdp, 8 * own),
            jnp.sum(up_sums, axis=0).reshape(fsdp, own_up),
        ],
        axis=1,
    )
    total = finish(packed.reshape(fsdp, 1, -1), True)[0]
    vec = lambda at: total[at * own : (at + 1) * own]
    grad_joint = by_part(jnp.concatenate([sum_a, sum_b], axis=1), 3)
    return (
        acts,
        input_grad,
        vec(0),
        vec(1),
        grad_joint.astype(F32),
        jnp.stack([vec(2), vec(3)]),
        out_sum.astype(F32),
        vec(4),
        vec(5),
        vec(6),
        up_sum.astype(F32),
        total[8 * own :],
        down_sum.astype(F32),
        vec(7),
    )


def solution(mesh):
    rows, line, flat = P(("fsdp", "dp"), None), P("fsdp"), P("fsdp", None)
    both = P(None, "fsdp")
    return jax.shard_map(
        functools.partial(on_device, mesh.shape["fsdp"], mesh.shape["dp"]),
        mesh=mesh,
        in_specs=(rows, P(("fsdp", "dp")), line, line, flat, both, flat, line, line, line, flat, line, flat, line, rows),
        out_specs=(rows, rows, line, line, flat, both, flat, line, line, line, flat, line, flat, line),
        check_vma=False,
    )
```

time: 809 us -> 409 us (0.51)
  matrix products: 291 us -> 29.1 us
  Pallas kernels: 0 us -> 126 us
  waiting for transfers between devices: 234 us -> 133 us
  other arithmetic: 112 us -> 13.2 us
  starting transfers between devices: 0.4 us -> 80.4 us
  blocking collectives: 78.6 us -> 0 us
  local copies, waits for them, and re-layouts: 64.6 us -> 20 us
  between operations: 17.3 us -> 2.54 us
    dot_general x26 -> x6, matrix products: 291 us -> 29.1 us  [the longest x5 28.9 us: weight_grad(): lax.dot_general(left, right, (((0,), (0,)), ((), ())), preferred_element_...]
    reduce_scatter x4 -> x0, waiting for transfers between devices: 169 us -> none  [the longest x1 78.4 us: on_device(): lax.psum_scatter(mlp_terms[2], 'fsdp', scatter_dimension=0, tiled=True)]
    ppermute x0 -> x96, waiting for transfers between devices: none -> 133 us  [swap(): return lax.ppermute(value, axis, [(i, i ^ bit) for i in range(size)])]
    pallas_call x0 -> x7, Pallas kernels: none -> 126 us  [the longest x2 29.4 us: attend_back(): pl.pallas_call(functools.partial(attend_back_kernel, rows), grid_spec=plt...]
    ppermute x0 -> x96, starting transfers between devices: none -> 80.4 us  [swap(): return lax.ppermute(value, axis, [(i, i ^ bit) for i in range(size)])]
    psum x1 -> x0, waiting for transfers between devices: 61.4 us -> none  [on_device(): lax.psum(attn_sums[2].astype(jnp.bfloat16), 'dp').astype(jnp.float32)]
    convert_element_type x27 -> x30, other arithmetic: 67.3 us -> 9 us  [the longest x25 6 us: add_low(): return (left.astype(F32) + right.astype(F32)).astype(left.dtype)]
    unnamed x2 -> x0, blocking collectives: 50 us -> none
  transfers between devices with their start and end apart: 10 -> 96, of which waited for: 4 -> 41; matrix products, arithmetic and copies ran while one was open for 50% -> 14% of each run, Pallas kernels for 0% -> 31%
where the time goes in v1:
time: 409 us; the launch traced here: 403 us
  waiting for transfers between devices  133 us (33%)
  Pallas kernels  126 us (31%)
  starting transfers between devices  80.4 us (20%)
  matrix products  29.1 us (7%)
  local copies, waits for them, and re-layouts  20 us (5%)
  other arithmetic  13.2 us (3%)
    ppermute x96, waiting for transfers between devices, swap(): return lax.ppermute(value, axis, [(i, i ^ bit) for i in range(size)])  133 us
    ppermute x96, starting transfers between devices, swap(): return lax.ppermute(value, axis, [(i, i ^ bit) for i in range(size)])  80.4 us
    pallas_call x2, Pallas kernels, attend_back(): pl.pallas_call(functools.partial(attend_back_kernel, rows), grid_spec=plt...  29.4 us
    pallas_call x1, Pallas kernels, middle_back(): pl.pallas_call(functools.partial(middle_kernel, out_weight, up_weight, do...  29 us
    dot_general x5, matrix products, weight_grad(): lax.dot_general(left, right, (((0,), (0,)), ((), ())), preferred_element_...  28.9 us
    pallas_call x1, Pallas kernels, attend(): pl.pallas_call(functools.partial(attend_kernel, rows), grid_spec=pltpu.Pr...  27 us
    pallas_call x1, Pallas kernels, up_forward(): pl.pallas_call(functools.partial(up_kernel, out_weight, up_weight), grid_...  18.9 us
    pallas_call x1, Pallas kernels, first_back(): pl.pallas_call(functools.partial(first_kernel, weight), grid_spec=pltpu.P...  11.3 us
  transfers between devices with their start and end apart: 96, of which 41 were waited for; matrix products, arithmetic and copies ran while one was open for 14% of the time, Pallas kernels for 31%

profile of v1, /device:TPU:0, one launch (start us, length us, event | category | flops | bytes accessed | tf_op | source)
XLA Modules:
  0.0 403.4 jit_solution(16509906935265740019)
XLA Ops:
  3.0 3.1 collective-permute-start.17
  6.1 5.4 %collective-permute-done.17.refs_12_ = bf16[96,1152]{1,0:T(8,128)(2,1)S(1)} collective-permute-done((bf16[96,1152]{1,0:T(8,128)(2,1)S(1)}, bf16[96,1152]{1,0:T(8,128)(2,1)S(1)}, u32[]{:S(2)}, u32[]{:S(2)}) %collective-permute-start.17) | collective-permute-done | bytes 221216 | tf_op jit(solution)/shard_map/ppermute | solution.py:33
  11.5 1.7 collective-permute-start.19
  13.2 4.9 %collective-permute-done.19.refs_14_ = bf16[96,1152]{1,0:T(8,128)(2,1)S(1)} collective-permute-done((bf16[96,1152]{1,0:T(8,128)(2,1)S(1)}, bf16[96,1152]{1,0:T(8,128)(2,1)S(1)}, u32[]{:S(2)}, u32[]{:S(2)}) %collective-permute-start.19) | collective-permute-done | bytes 221216 | tf_op jit(solution)/shard_map/ppermute | solution.py:33
  23.3 3.1 collective-permute-done.1
  26.7 2.7 collective-permute-done.2
  30.5 2.5 collective-permute-done.3
  33.0 3.0 collective-permute-done.4
  36.0 2.1 collective-permute-start.5
  38.2 2.4 collective-permute-done.5
  40.5 1.6 collective-permute-done.6
  45.8 2.7 collective-permute-done.15.refs_10_
  49.0 2.1 collective-permute-done.12.refs_6_
  55.0 2.6 collective-permute-done.22.refs_2_
  61.2 1.6 collective-permute-done.25.refs_5_
  64.2 2.3 collective-permute-done.26.refs_6_
  66.5 1.9 collective-permute-start.36
  71.0 2.9 collective-permute-done.29.refs_10_
  76.5 3.2 collective-permute-done.36.refs_18_
  80.3 9.9 %joint_forward.1 = (bf16[1024,2304]{1,0:T(8,128)(2,1)}, bf16[1024,768]{1,0:T(8,128)(2,1)}) custom-call(s32[1]{0:T(128)} %bitcast.me_ref, bf16[1024,768]{1,0:T(8,128)(2,1)} %x_ref.5, f32[1,768]{1,0:T(1,128)} %slice.144.gain_ref, f32[1,768]{1,0:T(1,128)} %slice.146.shift_ref, f32[1,2304]{1,0:T(1,128)} %reshape.218.bias_ref, bf16[96,1152]{1,0:T(8,128)(2,1)} %copy-done.12, ...), custom_call_target="tpu_custom_call" | custom-call | flops 3623878656 | bytes 11403264 | tf_op jit(solution)/shard_map/joint_forward/pallas_call | solution.py:193
  95.6 27.0 %attend.1 = (bf16[1024,768]{1,0:T(8,128)(2,1)}, f32[6,10,8,256]{3,2,1,0:T(8,128)}) custom-call(s32[1024]{0:T(1024)} %convert_reduce_fusion.starts_ref, f32[1024,128]{1,0:T(8,128)} %broadcast_in_dim.4.crops_ref, bf16[1024,2304]{1,0:T(8,128)(2,1)} %get-tuple-element.35.joint_ref), custom_call_target="tpu_custom_call" | custom-call | flops 4831838208 | bytes 6291456 | tf_op jit(solution)/shard_map/attend/pallas_call | solution.py:274
  122.6 4.4 %collective-permute-start.49 = (bf16[192,768]{1,0:T(8,128)(2,1)S(1)}, bf16[192,768]{1,0:T(8,128)(2,1)S(1)}, u32[]{:S(2)}, u32[]{:S(2)}) collective-permute-start(bf16[192,768]{1,0:T(8,128)(2,1)S(1)} %get-tuple-element.68.refs_32_), channel_id=1, source_target_pairs={{0,4},{4,0},{8,12},{12,8},{16,20},{20,16},{24,28},{28,24},{1,5},{5... | collective-permute-start | bytes 884744 | tf_op jit(solution)/shard_map/ppermute | solution.py:33
  129.8 18.9 %up_forward.1 = (f32[1024,768]{1,0:T(8,128)}, bf16[1024,768]{1,0:T(8,128)(2,1)}, bf16[1024,3072]{1,0:T(8,128)(2,1)}, bf16[1024,3072]{1,0:T(8,128)(2,1)}) custom-call(s32[1]{0:T(128)} %bitcast.me_ref, bf16[1024,768]{1,0:T(8,128)(2,1)} %x_ref.5, bf16[1024,768]{1,0:T(8,128)(2,1)} %get-tuple-element.36.mixed_ref, f32[8,768]{1,0:T(8,128)} %stack.37.vec_ref, ...), custom_call_target="tpu_custom_call" | custom-call | flops 6039797760 | bytes 25165824 | tf_op jit(solution)/shard_map/up_forward/pallas_call | solution.py:382
  150.0 8.5 %convolution_convert_fusion = bf16[3072,768]{1,0:T(8,128)(2,1)S(1)} fusion(bf16[1024,3072]{1,0:T(8,128)(2,1)} %get-tuple-element.40.active_ref, bf16[1024,768]{1,0:T(8,128)(2,1)S(1)} %copy-done.23), kind=kOutput, calls=%fused_computation | convolution fusion | flops 4834197504 | bytes 12582912 | tf_op jit(solution)/shard_map/dot_general | solution.py:536
  158.5 1.7 dynamic-slice_bitcast_fusion
  162.7 29.0 %middle_back.1 = (f32[1024,768]{1,0:T(8,128)}, bf16[1024,3072]{1,0:T(8,128)(2,1)}, f32[1024,768]{1,0:T(8,128)}, bf16[1024,768]{1,0:T(8,128)(2,1)}, bf16[1024,768...) custom-call(s32[1]{0:T(128)} %bitcast.me_ref, f32[1024,768]{1,0:T(8,128)} %get-tuple-element.39.middle_ref, ...), custom_call_target="tpu_custom_call" | custom-call | flops 15703474176 | bytes 42467328 | tf_op jit(solution)/shard_map/middle_back/pallas_call | solution.py:447
  191.8 14.8 %attend_back.2.part_a_ref = bf16[1024,1152]{1,0:T(8,128)(2,1)} custom-call(s32[1024]{0:T(1024)} %convert_reduce_fusion.starts_ref, f32[1024,128]{1,0:T(8,128)} %broadcast_in_dim.4.crops_ref, bf16[1024,2304]{1,0:T(8,128)(2,1)} %get-tuple-element.35.joint_ref, bf16[1024,768]{1,0:T(8,128)(2,1)} %get-tuple-element.36.mixed_ref, ...), custom_call_target="tpu_custom_call" | custom-call | flops 6039797760 | bytes 6291456 | tf_op jit(solution)/shard_map/attend_back/pallas_call | solution.py:338
  206.6 14.6 %attend_back.3.part_b_ref = bf16[1024,1152]{1,0:T(8,128)(2,1)} custom-call(s32[1024]{0:T(1024)} %convert_reduce_fusion.starts_ref, f32[1024,128]{1,0:T(8,128)} %broadcast_in_dim.4.crops_ref, bf16[1024,2304]{1,0:T(8,128)(2,1)} %get-tuple-element.35.joint_ref, bf16[1024,768]{1,0:T(8,128)(2,1)} %get-tuple-element.36.mixed_ref, ...), custom_call_target="tpu_custom_call" | custom-call | flops 6039797760 | bytes 6291456 | tf_op jit(solution)/shard_map/attend_back/pallas_call | solution.py:338
  221.2 5.8 %convolution_convert_fusion.2 = bf16[768,1152]{1,0:T(8,128)(2,1)} fusion(bf16[1024,768]{1,0:T(8,128)(2,1)} %get-tuple-element.52, bf16[1024,1152]{1,0:T(8,128)(2,1)} %attend_back.3.part_b_ref), kind=kOutput, calls=%fused_computation.7 | convolution fusion | flops 1812824064 | bytes 5701632 | tf_op jit(solution)/shard_map/dot_general | solution.py:536
  227.0 3.5 convolution_convert_fusion.3
  230.5 11.3 %first_back.1 = (f32[1024,768]{1,0:T(8,128)}, f32[2,8,768]{2,1,0:T(8,128)}, f32[8,2304]{1,0:T(8,128)}) custom-call(s32[1]{0:T(128)} %bitcast.me_ref, bf16[1024,768]{1,0:T(8,128)(2,1)} %x_ref.5, f32[1024,768]{1,0:T(8,128)} %get-tuple-element.44.gmid_ref, bf16[1024,1152]{1,0:T(8,128)(2,1)} %attend_back.2.part_a_ref, bf16[1024,1152]{1,0:T(8,128)(2,1)} %attend_back.3.part_b_ref, ...), custom_call_target="tpu_custom_call" | custom-call | flops 3623878656 | bytes 16121856 | tf_op jit(solution)/shard_map/first_back/pallas_call | solution.py:502
  244.5 4.6 %collective-permute-start.56 = (f32[4,1,1152]{2,1,0:T(1,128)S(1)}, f32[4,1,1152]{2,1,0:T(1,128)S(1)}, u32[]{:S(2)}, u32[]{:S(2)}) collective-permute-start(f32[4,1,1152]{2,1,0:T(1,128)S(1)} %dynamic-slice_bitcast_fusion.25), channel_id=1, source_target_pairs={{0,4},{4,0},{8,12},{12,8},{16,20},{20,16},{24,28},{28,24},{1,5},{5... | collective-permute-start | bytes 55304 | tf_op jit(solution)/shard_map/ppermute | solution.py:33
  252.8 3.0 convolution_convert_fusion.4
  257.1 2.4 collective-permute-done.58
  260.0 8.1 %convolution_convert_fusion.1 = bf16[768,3072]{1,0:T(8,128)(2,1)S(1)} fusion(bf16[1024,768]{1,0:T(8,128)(2,1)S(1)} %copy-done.63, bf16[1024,3072]{1,0:T(8,128)(2,1)} %get-tuple-element.55), kind=kOutput, calls=%fused_computation.1 | convolution fusion | flops 4834197504 | bytes 12582912 | tf_op jit(solution)/shard_map/dot_general | solution.py:536
  268.2 3.2 collective-permute-start.60
  271.5 2.0 collective-permute-start.76
  274.4 4.5 %collective-permute-done.76 = bf16[2,96,768]{2,1,0:T(8,128)(2,1)S(1)} collective-permute-done((bf16[2,96,768]{2,1,0:T(8,128)(2,1)S(1)}, bf16[2,96,768]{2,1,0:T(8,128)(2,1)S(1)}, u32[]{:S(2)}, u32[]{:S(2)}) %collective-permute-start.76) | collective-permute-done | bytes 294944 | tf_op jit(solution)/shard_map/ppermute | solution.py:33
  281.6 2.6 collective-permute-done.77
  285.4 3.7 collective-permute-done.78
  289.5 1.8 collective-permute-start.69
  291.3 3.0 collective-permute-done.79
  294.8 4.5 %collective-permute-done.80 = bf16[24,768]{1,0:T(8,128)(2,1)S(1)} collective-permute-done((bf16[24,768]{1,0:T(8,128)(2,1)S(1)}, bf16[24,768]{1,0:T(8,128)(2,1)S(1)}, u32[]{:S(2)}, u32[]{:S(2)}) %collective-permute-start.80) | collective-permute-done | bytes 36896 | tf_op jit(solution)/shard_map/ppermute | solution.py:33
  300.7 3.0 collective-permute-done.81
  305.8 2.1 collective-permute-done.62
  311.0 1.9 collective-permute-start.71
  312.9 3.5 collective-permute-done.63
  316.5 1.9 collective-permute-start.64
  318.8 3.6 collective-permute-done.64
  322.4 1.8 collective-permute-start.65
  325.7 1.9 collective-permute-done.65
  327.6 1.8 collective-permute-start.66
  330.1 2.6 collective-permute-done.66
  332.7 1.8 collective-permute-start.67
  339.7 14.4 %collective-permute-done.83 = bf16[2,96,3072]{2,1,0:T(8,128)(2,1)S(1)} collective-permute-done((bf16[2,96,3072]{2,1,0:T(8,128)(2,1)S(1)}, bf16[2,96,3072]{2,1,0:T(8,128)(2,1)S(1)}, u32[]{:S(2)}, u32[]{:S(2)}) %collective-permute-start.83) | collective-permute-done | bytes 1179680 | tf_op jit(solution)/shard_map/ppermute | solution.py:33
  358.4 2.2 collective-permute-done.91
  362.2 3.5 collective-permute-done.84
  367.3 5.6 %collective-permute-done.92 = bf16[192,768]{1,0:T(8,128)(2,1)S(1)} collective-permute-done((bf16[192,768]{1,0:T(8,128)(2,1)S(1)}, bf16[192,768]{1,0:T(8,128)(2,1)S(1)}, u32[]{:S(2)}, u32[]{:S(2)}) %collective-permute-start.92) | collective-permute-done | bytes 294944 | tf_op jit(solution)/shard_map/ppermute | solution.py:33
  373.1 7.7 %collective-permute-done.85 = bf16[48,3072]{1,0:T(8,128)(2,1)S(1)} collective-permute-done((bf16[48,3072]{1,0:T(8,128)(2,1)S(1)}, bf16[48,3072]{1,0:T(8,128)(2,1)S(1)}, u32[]{:S(2)}, u32[]{:S(2)}) %collective-permute-start.85) | collective-permute-done | bytes 294944 | tf_op jit(solution)/shard_map/ppermute | solution.py:33
  381.1 3.0 collective-permute-start.94
  384.1 4.6 %collective-permute-done.86 = bf16[24,3072]{1,0:T(8,128)(2,1)S(1)} collective-permute-done((bf16[24,3072]{1,0:T(8,128)(2,1)S(1)}, bf16[24,3072]{1,0:T(8,128)(2,1)S(1)}, u32[]{:S(2)}, u32[]{:S(2)}) %collective-permute-start.86) | collective-permute-done | bytes 147488 | tf_op jit(solution)/shard_map/ppermute | solution.py:33
  390.4 4.5 %collective-permute-done.87 = bf16[24,3072]{1,0:T(8,128)(2,1)S(1)} collective-permute-done((bf16[24,3072]{1,0:T(8,128)(2,1)S(1)}, bf16[24,3072]{1,0:T(8,128)(2,1)S(1)}, u32[]{:S(2)}, u32[]{:S(2)}) %collective-permute-start.87) | collective-permute-done | bytes 147488 | tf_op jit(solution)/shard_map/ppermute | solution.py:33
  395.0 2.9 collective-permute-done.95
  399.1 2.6 collective-permute-done.88
  (414 shorter events, 79.6 us)
Async XLA Ops:
  3.0 8.5 %collective-permute-start.17 = (bf16[96,1152]{1,0:T(8,128)(2,1)S(1)}, bf16[96,1152]{1,0:T(8,128)(2,1)S(1)}, u32[]{:S(2)}, u32[]{:S(2)}) collective-permute-start(bf16[96,1152]{1,0:T(8,128)(2,1)S(1)} %get-tuple-element.72.refs_8_), channel_id=1, source_target_pairs={{0,16},{4,20},{8,24},{12,28},{16,0},{20,4},{24,8},{28,12},{1,17},{... | collective-permute-start | bytes 663560 | tf_op jit(solution)/shard_map/ppermute | solution.py:33
  11.5 6.6 %collective-permute-start.19 = (bf16[96,1152]{1,0:T(8,128)(2,1)S(1)}, bf16[96,1152]{1,0:T(8,128)(2,1)S(1)}, u32[]{:S(2)}, u32[]{:S(2)}) collective-permute-start(bf16[96,1152]{1,0:T(8,128)(2,1)S(1)} %collective-permute-done.17.refs_12_), channel_id=1, source_target_pairs={{0,8},{4,12},{8,0},{12,4},{16,24},{20,28},{24,16},{28,20},{1,9},{5... | collective-permute-start | bytes 663560 | tf_op jit(solution)/shard_map/ppermute | solution.py:33
  18.1 20.0 %collective-permute-start.20 = (bf16[96,1152]{1,0:T(8,128)(2,1)S(1)}, bf16[96,1152]{1,0:T(8,128)(2,1)S(1)}, u32[]{:S(2)}, u32[]{:S(2)}) collective-permute-start(bf16[96,1152]{1,0:T(8,128)(2,1)S(1)} %collective-permute-done.19.refs_14_), channel_id=1, source_target_pairs={{0,4},{4,0},{8,12},{12,8},{16,20},{20,16},{24,28},{28,24},{1,5},{5... | collective-permute-start | bytes 663560 | tf_op jit(solution)/shard_map/ppermute | solution.py:33
  18.1 24.6 %collective-permute-start.8 = (bf16[96,1152]{1,0:T(8,128)(2,1)S(1)}, bf16[96,1152]{1,0:T(8,128)(2,1)S(1)}, u32[]{:S(2)}, u32[]{:S(2)}) collective-permute-start(bf16[96,1152]{1,0:T(8,128)(2,1)S(1)} %get-tuple-element.73.refs_0_), channel_id=1, source_target_pairs={{0,8},{4,12},{8,0},{12,4},{16,24},{20,28},{24,16},{28,20},{1,9},{5... | collective-permute-start | bytes 663560 | tf_op jit(solution)/shard_map/ppermute | solution.py:33
  19.5 23.1 %collective-permute-start.7 = (bf16[96,1152]{1,0:T(8,128)(2,1)S(1)}, bf16[96,1152]{1,0:T(8,128)(2,1)S(1)}, u32[]{:S(2)}, u32[]{:S(2)}) collective-permute-start(bf16[96,1152]{1,0:T(8,128)(2,1)S(1)} %get-tuple-element.73.refs_0_), channel_id=1, source_target_pairs={{0,4},{4,0},{8,12},{12,8},{16,20},{20,16},{24,28},{28,24},{1,5},{5... | collective-permute-start | bytes 663560 | tf_op jit(solution)/shard_map/ppermute | solution.py:33
  19.7 23.9 %collective-permute-start.10 = (bf16[96,1152]{1,0:T(8,128)(2,1)S(1)}, bf16[96,1152]{1,0:T(8,128)(2,1)S(1)}, u32[]{:S(2)}, u32[]{:S(2)}) collective-permute-start(bf16[96,1152]{1,0:T(8,128)(2,1)S(1)} %get-tuple-element.73.refs_0_), channel_id=1, source_target_pairs={{0,16},{4,20},{8,24},{12,28},{16,0},{20,4},{24,8},{28,12},{1,17},{... | collective-permute-start | bytes 663560 | tf_op jit(solution)/shard_map/ppermute | solution.py:33
  42.1 6.4 %collective-permute-start.15 = (bf16[96,1152]{1,0:T(8,128)(2,1)S(1)}, bf16[96,1152]{1,0:T(8,128)(2,1)}, u32[]{:S(2)}, u32[]{:S(2)}) collective-permute-start(bf16[96,1152]{1,0:T(8,128)(2,1)S(1)} %get-tuple-element.72.refs_8_), channel_id=1, source_target_pairs={{0,8},{4,12},{8,0},{12,4},{16,24},{20,28},{24,16},{28,20},{1,9},{5... | collective-permute-start | bytes 663560 | tf_op jit(solution)/shard_map/ppermute | solution.py:33
  42.7 8.5 %collective-permute-start.12 = (bf16[96,1152]{1,0:T(8,128)(2,1)S(1)}, bf16[96,1152]{1,0:T(8,128)(2,1)}, u32[]{:S(2)}, u32[]{:S(2)}) collective-permute-start(bf16[96,1152]{1,0:T(8,128)(2,1)S(1)} %collective-permute-done.8.refs_2_), channel_id=1, source_target_pairs={{0,16},{4,20},{8,24},{12,28},{16,0},{20,4},{24,8},{28,12},{1,17},{... | collective-permute-start | bytes 663560 | tf_op jit(solution)/shard_map/ppermute | solution.py:33
  43.6 7.5 %collective-permute-start.11 = (bf16[96,1152]{1,0:T(8,128)(2,1)S(1)}, bf16[96,1152]{1,0:T(8,128)(2,1)}, u32[]{:S(2)}, u32[]{:S(2)}) collective-permute-start(bf16[96,1152]{1,0:T(8,128)(2,1)S(1)} %collective-permute-done.10.refs_4_), channel_id=1, source_target_pairs={{0,4},{4,0},{8,12},{12,8},{16,20},{20,16},{24,28},{28,24},{1,5},{5... | collective-permute-start | bytes 663560 | tf_op jit(solution)/shard_map/ppermute | solution.py:33
  44.6 13.0 %collective-permute-start.38 = (bf16[96,1536]{1,0:T(8,128)(2,1)S(1)}, bf16[96,1536]{1,0:T(8,128)(2,1)S(1)}, u32[]{:S(2)}, u32[]{:S(2)}) collective-permute-start(bf16[96,1536]{1,0:T(8,128)(2,1)S(1)} %get-tuple-element.70.refs_16_), channel_id=1, source_target_pairs={{0,16},{4,20},{8,24},{12,28},{16,0},{20,4},{24,8},{28,12},{1,17},{... | collective-permute-start | bytes 884744 | tf_op jit(solution)/shard_map/ppermute | solution.py:33
  51.2 6.4 %collective-permute-start.22 = (bf16[96,768]{1,0:T(8,128)(2,1)S(1)}, bf16[96,768]{1,0:T(8,128)(2,1)}, u32[]{:S(2)}, u32[]{:S(2)}) collective-permute-start(bf16[96,768]{1,0:T(8,128)(2,1)S(1)} %copy-done.57), channel_id=1, source_target_pairs={{0,8},{4,12},{8,0},{12,4},{16,24},{20,28},{24,16},{28,20},{1,9},{5... | collective-permute-start | bytes 442376 | tf_op jit(solution)/shard_map/ppermute | solution.py:33
  54.9 11.6 %collective-permute-start.28 = (bf16[96,1536]{1,0:T(8,128)(2,1)S(1)}, bf16[96,1536]{1,0:T(8,128)(2,1)S(1)}, u32[]{:S(2)}, u32[]{:S(2)}) collective-permute-start(bf16[96,1536]{1,0:T(8,128)(2,1)S(1)} %get-tuple-element.71.refs_8_), channel_id=1, source_target_pairs={{0,4},{4,0},{8,12},{12,8},{16,20},{20,16},{24,28},{28,24},{1,5},{5... | collective-permute-start | bytes 884744 | tf_op jit(solution)/shard_map/ppermute | solution.py:33
  57.6 10.8 %collective-permute-start.40 = (bf16[96,1536]{1,0:T(8,128)(2,1)S(1)}, bf16[96,1536]{1,0:T(8,128)(2,1)S(1)}, u32[]{:S(2)}, u32[]{:S(2)}) collective-permute-start(bf16[96,1536]{1,0:T(8,128)(2,1)S(1)} %collective-permute-done.38.refs_20_), channel_id=1, source_target_pairs={{0,8},{4,12},{8,0},{12,4},{16,24},{20,28},{24,16},{28,20},{1,9},{5... | collective-permute-start | bytes 884744 | tf_op jit(solution)/shard_map/ppermute | solution.py:33
  59.5 14.4 %collective-permute-start.29 = (bf16[96,1536]{1,0:T(8,128)(2,1)S(1)}, bf16[96,1536]{1,0:T(8,128)(2,1)S(1)}, u32[]{:S(2)}, u32[]{:S(2)}) collective-permute-start(bf16[96,1536]{1,0:T(8,128)(2,1)S(1)} %get-tuple-element.71.refs_8_), channel_id=1, source_target_pairs={{0,8},{4,12},{8,0},{12,4},{16,24},{20,28},{24,16},{28,20},{1,9},{5... | collective-permute-start | bytes 884744 | tf_op jit(solution)/shard_map/ppermute | solution.py:33
  62.7 12.5 %collective-permute-start.31 = (bf16[96,1536]{1,0:T(8,128)(2,1)S(1)}, bf16[96,1536]{1,0:T(8,128)(2,1)S(1)}, u32[]{:S(2)}, u32[]{:S(2)}) collective-permute-start(bf16[96,1536]{1,0:T(8,128)(2,1)S(1)} %get-tuple-element.71.refs_8_), channel_id=1, source_target_pairs={{0,16},{4,20},{8,24},{12,28},{16,0},{20,4},{24,8},{28,12},{1,17},{... | collective-permute-start | bytes 884744 | tf_op jit(solution)/shard_map/ppermute | solution.py:33
  66.5 9.2 %collective-permute-start.35 = (bf16[96,1536]{1,0:T(8,128)(2,1)S(1)}, bf16[96,1536]{1,0:T(8,128)(2,1)S(1)}, u32[]{:S(2)}, u32[]{:S(2)}) collective-permute-start(bf16[96,1536]{1,0:T(8,128)(2,1)S(1)} %get-tuple-element.70.refs_16_), channel_id=1, source_target_pairs={{0,4},{4,0},{8,12},{12,8},{16,20},{20,16},{24,28},{28,24},{1,5},{5... | collective-permute-start | bytes 884744 | tf_op jit(solution)/shard_map/ppermute | solution.py:33
  66.5 13.2 %collective-permute-start.36 = (bf16[96,1536]{1,0:T(8,128)(2,1)S(1)}, bf16[96,1536]{1,0:T(8,128)(2,1)S(1)}, u32[]{:S(2)}, u32[]{:S(2)}) collective-permute-start(bf16[96,1536]{1,0:T(8,128)(2,1)S(1)} %get-tuple-element.70.refs_16_), channel_id=1, source_target_pairs={{0,8},{4,12},{8,0},{12,4},{16,24},{20,28},{24,16},{28,20},{1,9},{5... | collective-permute-start | bytes 884744 | tf_op jit(solution)/shard_map/ppermute | solution.py:33
  68.5 11.8 %collective-permute-start.41 = (bf16[96,1536]{1,0:T(8,128)(2,1)S(1)}, bf16[96,1536]{1,0:T(8,128)(2,1)}, u32[]{:S(2)}, u32[]{:S(2)}) collective-permute-start(bf16[96,1536]{1,0:T(8,128)(2,1)S(1)} %collective-permute-done.40.refs_22_), channel_id=1, source_target_pairs={{0,4},{4,0},{8,12},{12,8},{16,20},{20,16},{24,28},{28,24},{1,5},{5... | collective-permute-start | bytes 884744 | tf_op jit(solution)/shard_map/ppermute | solution.py:33
  75.2 15.7 %collective-permute-start.30 = (bf16[96,1536]{1,0:T(8,128)(2,1)S(1)}, bf16[96,1536]{1,0:T(8,128)(2,1)S(1)}, u32[]{:S(2)}, u32[]{:S(2)}) collective-permute-start(bf16[96,1536]{1,0:T(8,128)(2,1)S(1)} %collective-permute-done.29.refs_10_), channel_id=1, source_target_pairs={{0,4},{4,0},{8,12},{12,8},{16,20},{20,16},{24,28},{28,24},{1,5},{5... | collective-permute-start | bytes 884744 | tf_op jit(solution)/shard_map/ppermute | solution.py:33
  75.7 14.8 %collective-permute-start.33 = (bf16[96,1536]{1,0:T(8,128)(2,1)S(1)}, bf16[96,1536]{1,0:T(8,128)(2,1)S(1)}, u32[]{:S(2)}, u32[]{:S(2)}) collective-permute-start(bf16[96,1536]{1,0:T(8,128)(2,1)S(1)} %collective-permute-done.29.refs_10_), channel_id=1, source_target_pairs={{0,16},{4,20},{8,24},{12,28},{16,0},{20,4},{24,8},{28,12},{1,17},{... | collective-permute-start | bytes 884744 | tf_op jit(solution)/shard_map/ppermute | solution.py:33
  79.7 13.3 %collective-permute-start.39 = (bf16[96,1536]{1,0:T(8,128)(2,1)S(1)}, bf16[96,1536]{1,0:T(8,128)(2,1)S(1)}, u32[]{:S(2)}, u32[]{:S(2)}) collective-permute-start(bf16[96,1536]{1,0:T(8,128)(2,1)S(1)} %collective-permute-done.38.refs_20_), channel_id=1, source_target_pairs={{0,4},{4,0},{8,12},{12,8},{16,20},{20,16},{24,28},{28,24},{1,5},{5... | collective-permute-start | bytes 884744 | tf_op jit(solution)/shard_map/ppermute | solution.py:33
  79.7 11.3 %collective-permute-start.32 = (bf16[96,1536]{1,0:T(8,128)(2,1)S(1)}, bf16[96,1536]{1,0:T(8,128)(2,1)S(1)}, u32[]{:S(2)}, u32[]{:S(2)}) collective-permute-start(bf16[96,1536]{1,0:T(8,128)(2,1)S(1)} %collective-permute-done.31.refs_12_), channel_id=1, source_target_pairs={{0,4},{4,0},{8,12},{12,8},{16,20},{20,16},{24,28},{28,24},{1,5},{5... | collective-permute-start | bytes 884744 | tf_op jit(solution)/shard_map/ppermute | solution.py:33
  80.3 12.3 %collective-permute-start.37 = (bf16[96,1536]{1,0:T(8,128)(2,1)S(1)}, bf16[96,1536]{1,0:T(8,128)(2,1)S(1)}, u32[]{:S(2)}, u32[]{:S(2)}) collective-permute-start(bf16[96,1536]{1,0:T(8,128)(2,1)S(1)} %collective-permute-done.36.refs_18_), channel_id=1, source_target_pairs={{0,4},{4,0},{8,12},{12,8},{16,20},{20,16},{24,28},{28,24},{1,5},{5... | collective-permute-start | bytes 884744 | tf_op jit(solution)/shard_map/ppermute | solution.py:33
  90.4 32.1 %collective-permute-start.34 = (bf16[96,1536]{1,0:T(8,128)(2,1)S(1)}, bf16[96,1536]{1,0:T(8,128)(2,1)S(1)}, u32[]{:S(2)}, u32[]{:S(2)}) collective-permute-start(bf16[96,1536]{1,0:T(8,128)(2,1)S(1)} %collective-permute-done.33.refs_14_), channel_id=1, source_target_pairs={{0,4},{4,0},{8,12},{12,8},{16,20},{20,16},{24,28},{28,24},{1,5},{5... | collective-permute-start | bytes 884744 | tf_op jit(solution)/shard_map/ppermute | solution.py:33
  90.9 36.1 %collective-permute-start.42 = (bf16[192,768]{1,0:T(8,128)(2,1)S(1)}, bf16[192,768]{1,0:T(8,128)(2,1)S(1)}, u32[]{:S(2)}, u32[]{:S(2)}) collective-permute-start(bf16[192,768]{1,0:T(8,128)(2,1)S(1)} %get-tuple-element.69.refs_24_), channel_id=1, source_target_pairs={{0,4},{4,0},{8,12},{12,8},{16,20},{20,16},{24,28},{28,24},{1,5},{5... | collective-permute-start | bytes 884744 | tf_op jit(solution)/shard_map/ppermute | solution.py:33
  91.0 37.1 %collective-permute-start.43 = (bf16[192,768]{1,0:T(8,128)(2,1)S(1)}, bf16[192,768]{1,0:T(8,128)(2,1)S(1)}, u32[]{:S(2)}, u32[]{:S(2)}) collective-permute-start(bf16[192,768]{1,0:T(8,128)(2,1)S(1)} %get-tuple-element.69.refs_24_), channel_id=1, source_target_pairs={{0,8},{4,12},{8,0},{12,4},{16,24},{20,28},{24,16},{28,20},{1,9},{5... | collective-permute-start | bytes 884744 | tf_op jit(solution)/shard_map/ppermute | solution.py:33
  92.5 35.8 %collective-permute-start.45 = (bf16[192,768]{1,0:T(8,128)(2,1)S(1)}, bf16[192,768]{1,0:T(8,128)(2,1)S(1)}, u32[]{:S(2)}, u32[]{:S(2)}) collective-permute-start(bf16[192,768]{1,0:T(8,128)(2,1)S(1)} %get-tuple-element.69.refs_24_), channel_id=1, source_target_pairs={{0,16},{4,20},{8,24},{12,28},{16,0},{20,4},{24,8},{28,12},{1,17},{... | collective-permute-start | bytes 884744 | tf_op jit(solution)/shard_map/ppermute | solution.py:33
  93.1 36.1 %collective-permute-start.52 = (bf16[192,768]{1,0:T(8,128)(2,1)S(1)}, bf16[192,768]{1,0:T(8,128)(2,1)S(1)}, u32[]{:S(2)}, u32[]{:S(2)}) collective-permute-start(bf16[192,768]{1,0:T(8,128)(2,1)S(1)} %get-tuple-element.68.refs_32_), channel_id=1, source_target_pairs={{0,16},{4,20},{8,24},{12,28},{16,0},{20,4},{24,8},{28,12},{1,17},{... | collective-permute-start | bytes 884744 | tf_op jit(solution)/shard_map/ppermute | solution.py:33
  122.6 26.1 %collective-permute-start.49 = (bf16[192,768]{1,0:T(8,128)(2,1)S(1)}, bf16[192,768]{1,0:T(8,128)(2,1)S(1)}, u32[]{:S(2)}, u32[]{:S(2)}) collective-permute-start(bf16[192,768]{1,0:T(8,128)(2,1)S(1)} %get-tuple-element.68.refs_32_), channel_id=1, source_target_pairs={{0,4},{4,0},{8,12},{12,8},{16,20},{20,16},{24,28},{28,24},{1,5},{5... | collective-permute-start | bytes 884744 | tf_op jit(solution)/shard_map/ppermute | solution.py:33
  127.0 21.8 %collective-permute-start.50 = (bf16[192,768]{1,0:T(8,128)(2,1)S(1)}, bf16[192,768]{1,0:T(8,128)(2,1)}, u32[]{:S(2)}, u32[]{:S(2)}) collective-permute-start(bf16[192,768]{1,0:T(8,128)(2,1)S(1)} %get-tuple-element.68.refs_32_), channel_id=1, source_target_pairs={{0,8},{4,12},{8,0},{12,4},{16,24},{20,28},{24,16},{28,20},{1,9},{5... | collective-permute-start | bytes 884744 | tf_op jit(solution)/shard_map/ppermute | solution.py:33
  128.1 21.2 %collective-permute-start.44 = (bf16[192,768]{1,0:T(8,128)(2,1)S(1)}, bf16[192,768]{1,0:T(8,128)(2,1)S(1)}, u32[]{:S(2)}, u32[]{:S(2)}) collective-permute-start(bf16[192,768]{1,0:T(8,128)(2,1)S(1)} %collective-permute-done.43.refs_26_), channel_id=1, source_target_pairs={{0,4},{4,0},{8,12},{12,8},{16,20},{20,16},{24,28},{28,24},{1,5},{5... | collective-permute-start | bytes 884744 | tf_op jit(solution)/shard_map/ppermute | solution.py:33
  128.3 21.1 %collective-permute-start.47 = (bf16[192,768]{1,0:T(8,128)(2,1)S(1)}, bf16[192,768]{1,0:T(8,128)(2,1)}, u32[]{:S(2)}, u32[]{:S(2)}) collective-permute-start(bf16[192,768]{1,0:T(8,128)(2,1)S(1)} %collective-permute-done.43.refs_26_), channel_id=1, source_target_pairs={{0,16},{4,20},{8,24},{12,28},{16,0},{20,4},{24,8},{28,12},{1,17},{... | collective-permute-start | bytes 884744 | tf_op jit(solution)/shard_map/ppermute | solution.py:33
  129.2 20.7 %collective-permute-start.54 = (bf16[192,768]{1,0:T(8,128)(2,1)S(1)}, bf16[192,768]{1,0:T(8,128)(2,1)}, u32[]{:S(2)}, u32[]{:S(2)}) collective-permute-start(bf16[192,768]{1,0:T(8,128)(2,1)S(1)} %collective-permute-done.52.refs_36_), channel_id=1, source_target_pairs={{0,8},{4,12},{8,0},{12,4},{16,24},{20,28},{24,16},{28,20},{1,9},{5... | collective-permute-start | bytes 884744 | tf_op jit(solution)/shard_map/ppermute | solution.py:33
  148.8 13.0 %collective-permute-start.53 = (bf16[192,768]{1,0:T(8,128)(2,1)S(1)}, bf16[192,768]{1,0:T(8,128)(2,1)S(1)}, u32[]{:S(2)}, u32[]{:S(2)}) collective-permute-start(bf16[192,768]{1,0:T(8,128)(2,1)S(1)} %collective-permute-done.52.refs_36_), channel_id=1, source_target_pairs={{0,4},{4,0},{8,12},{12,8},{16,20},{20,16},{24,28},{28,24},{1,5},{5... | collective-permute-start | bytes 884744 | tf_op jit(solution)/shard_map/ppermute | solution.py:33
  148.9 12.5 %collective-permute-start.46 = (bf16[192,768]{1,0:T(8,128)(2,1)S(1)}, bf16[192,768]{1,0:T(8,128)(2,1)S(1)}, u32[]{:S(2)}, u32[]{:S(2)}) collective-permute-start(bf16[192,768]{1,0:T(8,128)(2,1)S(1)} %collective-permute-done.45.refs_28_), channel_id=1, source_target_pairs={{0,4},{4,0},{8,12},{12,8},{16,20},{20,16},{24,28},{28,24},{1,5},{5... | collective-permute-start | bytes 884744 | tf_op jit(solution)/shard_map/ppermute | solution.py:33
  149.3 12.5 %collective-permute-start.51 = (bf16[192,768]{1,0:T(8,128)(2,1)}, bf16[192,768]{1,0:T(8,128)(2,1)S(1)}, u32[]{:S(2)}, u32[]{:S(2)}) collective-permute-start(bf16[192,768]{1,0:T(8,128)(2,1)} %collective-permute-done.50.refs_34_), channel_id=1, source_target_pairs={{0,4},{4,0},{8,12},{12,8},{16,20},{20,16},{24,28},{28,24},{1,5},{5... | collective-permute-start | bytes 884744 | tf_op jit(solution)/shard_map/ppermute | solution.py:33
  149.4 12.4 %collective-permute-start.48 = (bf16[192,768]{1,0:T(8,128)(2,1)}, bf16[192,768]{1,0:T(8,128)(2,1)S(1)}, u32[]{:S(2)}, u32[]{:S(2)}) collective-permute-start(bf16[192,768]{1,0:T(8,128)(2,1)} %collective-permute-done.47.refs_30_), channel_id=1, source_target_pairs={{0,4},{4,0},{8,12},{12,8},{16,20},{20,16},{24,28},{28,24},{1,5},{5... | collective-permute-start | bytes 884744 | tf_op jit(solution)/shard_map/ppermute | solution.py:33
  149.9 12.0 %collective-permute-start.55 = (bf16[192,768]{1,0:T(8,128)(2,1)}, bf16[192,768]{1,0:T(8,128)(2,1)}, u32[]{:S(2)}, u32[]{:S(2)}) collective-permute-start(bf16[192,768]{1,0:T(8,128)(2,1)} %collective-permute-done.54.refs_38_), channel_id=1, source_target_pairs={{0,4},{4,0},{8,12},{12,8},{16,20},{20,16},{24,28},{28,24},{1,5},{5... | collective-permute-start | bytes 884744 | tf_op jit(solution)/shard_map/ppermute | solution.py:33
  161.4 148.1 %collective-permute-start.89 = (bf16[4,384,768]{2,1,0:T(8,128)(2,1)}, bf16[4,384,768]{2,1,0:T(8,128)(2,1)S(1)}, u32[]{:S(2)}, u32[]{:S(2)}) collective-permute-start(bf16[4,384,768]{2,1,0:T(8,128)(2,1)} %dynamic-slice_bitcast_fusion), channel_id=1, source_target_pairs={{0,4},{4,0},{8,12},{12,8},{16,20},{20,16},{24,28},{28,24},{1,5},{5... | collective-permute-start | bytes 7077896 | tf_op jit(solution)/shard_map/ppermute | solution.py:33
  244.5 6.7 %collective-permute-start.56 = (f32[4,1,1152]{2,1,0:T(1,128)S(1)}, f32[4,1,1152]{2,1,0:T(1,128)S(1)}, u32[]{:S(2)}, u32[]{:S(2)}) collective-permute-start(f32[4,1,1152]{2,1,0:T(1,128)S(1)} %dynamic-slice_bitcast_fusion.25), channel_id=1, source_target_pairs={{0,4},{4,0},{8,12},{12,8},{16,20},{20,16},{24,28},{28,24},{1,5},{5... | collective-permute-start | bytes 55304 | tf_op jit(solution)/shard_map/ppermute | solution.py:33
  250.5 34.6 %collective-permute-start.68 = (bf16[4,96,1152]{2,1,0:T(8,128)(2,1)S(1)}, bf16[4,96,1152]{2,1,0:T(8,128)(2,1)S(1)}, u32[]{:S(2)}, u32[]{:S(2)}) collective-permute-start(bf16[4,96,1152]{2,1,0:T(8,128)(2,1)S(1)} %dynamic-slice_bitcast_fusion.4), channel_id=1, source_target_pairs={{0,4},{4,0},{8,12},{12,8},{16,20},{20,16},{24,28},{28,24},{1,5},{5... | collective-permute-start | bytes 2654216 | tf_op jit(solution)/shard_map/ppermute | solution.py:33
  250.7 43.8 %collective-permute-start.61 = (bf16[4,96,1152]{2,1,0:T(8,128)(2,1)S(1)}, bf16[4,96,1152]{2,1,0:T(8,128)(2,1)S(1)}, u32[]{:S(2)}, u32[]{:S(2)}) collective-permute-start(bf16[4,96,1152]{2,1,0:T(8,128)(2,1)S(1)} %dynamic-slice_bitcast_fusion.5), channel_id=1, source_target_pairs={{0,4},{4,0},{8,12},{12,8},{16,20},{20,16},{24,28},{28,24},{1,5},{5... | collective-permute-start | bytes 2654216 | tf_op jit(solution)/shard_map/ppermute | solution.py:33
  257.0 14.3 %collective-permute-start.75 = (bf16[4,96,768]{2,1,0:T(8,128)(2,1)S(1)}, bf16[4,96,768]{2,1,0:T(8,128)(2,1)S(1)}, u32[]{:S(2)}, u32[]{:S(2)}) collective-permute-start(bf16[4,96,768]{2,1,0:T(8,128)(2,1)S(1)} %dynamic-slice_bitcast_fusion.8), channel_id=1, source_target_pairs={{0,4},{4,0},{8,12},{12,8},{16,20},{20,16},{24,28},{28,24},{1,5},{5... | collective-permute-start | bytes 1769480 | tf_op jit(solution)/shard_map/ppermute | solution.py:33
  259.5 8.6 %collective-permute-start.59 = (f32[1,1152]{1,0:T(1,128)S(1)}, f32[1,1152]{1,0:T(1,128)S(1)}, u32[]{:S(2)}, u32[]{:S(2)}) collective-permute-start(f32[1,1152]{1,0:T(1,128)S(1)} %fusion.29), channel_id=1, source_target_pairs={{0,1},{1,0},{2,3},{3,2},{4,5},{5,4},{6,7},{7,6},{8,9},{9,8},{10,11... | collective-permute-start | bytes 13832 | tf_op jit(solution)/shard_map/ppermute | solution.py:33
  271.5 7.4 %collective-permute-start.76 = (bf16[2,96,768]{2,1,0:T(8,128)(2,1)S(1)}, bf16[2,96,768]{2,1,0:T(8,128)(2,1)S(1)}, u32[]{:S(2)}, u32[]{:S(2)}) collective-permute-start(bf16[2,96,768]{2,1,0:T(8,128)(2,1)S(1)} %dynamic-slice_bitcast_fusion.13), channel_id=1, source_target_pairs={{0,16},{4,20},{8,24},{12,28},{16,0},{20,4},{24,8},{28,12},{1,17},{... | collective-permute-start | bytes 884744 | tf_op jit(solution)/shard_map/ppermute | solution.py:33
  273.7 60.8 %collective-permute-start.82 = (bf16[4,96,3072]{2,1,0:T(8,128)(2,1)S(1)}, bf16[4,96,3072]{2,1,0:T(8,128)(2,1)S(1)}, u32[]{:S(2)}, u32[]{:S(2)}) collective-permute-start(bf16[4,96,3072]{2,1,0:T(8,128)(2,1)S(1)} %dynamic-slice_bitcast_fusion.1), channel_id=1, source_target_pairs={{0,4},{4,0},{8,12},{12,8},{16,20},{20,16},{24,28},{28,24},{1,5},{5... | collective-permute-start | bytes 7077896 | tf_op jit(solution)/shard_map/ppermute | solution.py:33
  289.5 14.9 %collective-permute-start.69 = (bf16[2,96,1152]{2,1,0:T(8,128)(2,1)S(1)}, bf16[2,96,1152]{2,1,0:T(8,128)(2,1)S(1)}, u32[]{:S(2)}, u32[]{:S(2)}) collective-permute-start(bf16[2,96,1152]{2,1,0:T(8,128)(2,1)S(1)} %dynamic-slice_bitcast_fusion.9), channel_id=1, source_target_pairs={{0,16},{4,20},{8,24},{12,28},{16,0},{20,4},{24,8},{28,12},{1,17},{... | collective-permute-start | bytes 1327112 | tf_op jit(solution)/shard_map/ppermute | solution.py:33
  299.6 8.4 %collective-permute-start.62 = (bf16[2,96,1152]{2,1,0:T(8,128)(2,1)S(1)}, bf16[2,96,1152]{2,1,0:T(8,128)(2,1)S(1)}, u32[]{:S(2)}, u32[]{:S(2)}) collective-permute-start(bf16[2,96,1152]{2,1,0:T(8,128)(2,1)S(1)} %dynamic-slice_bitcast_fusion.10), channel_id=1, source_target_pairs={{0,8},{4,12},{8,0},{12,4},{16,24},{20,28},{24,16},{28,20},{1,9},{5... | collective-permute-start | bytes 1327112 | tf_op jit(solution)/shard_map/ppermute | solution.py:33
  304.6 6.3 %collective-permute-start.70 = (bf16[96,1152]{1,0:T(8,128)(2,1)S(1)}, bf16[96,1152]{1,0:T(8,128)(2,1)S(1)}, u32[]{:S(2)}, u32[]{:S(2)}) collective-permute-start(bf16[96,1152]{1,0:T(8,128)(2,1)S(1)} %dynamic-slice_bitcast_fusion.14), channel_id=1, source_target_pairs={{0,8},{4,12},{8,0},{12,4},{16,24},{20,28},{24,16},{28,20},{1,9},{5... | collective-permute-start | bytes 663560 | tf_op jit(solution)/shard_map/ppermute | solution.py:33
  308.1 8.4 %collective-permute-start.63 = (bf16[96,1152]{1,0:T(8,128)(2,1)S(1)}, bf16[96,1152]{1,0:T(8,128)(2,1)S(1)}, u32[]{:S(2)}, u32[]{:S(2)}) collective-permute-start(bf16[96,1152]{1,0:T(8,128)(2,1)S(1)} %dynamic-slice_bitcast_fusion.15), channel_id=1, source_target_pairs={{0,16},{4,20},{8,24},{12,28},{16,0},{20,4},{24,8},{28,12},{1,17},{... | collective-permute-start | bytes 663560 | tf_op jit(solution)/shard_map/ppermute | solution.py:33
  310.2 27.4 %collective-permute-start.90 = (bf16[2,384,768]{2,1,0:T(8,128)(2,1)S(1)}, bf16[2,384,768]{2,1,0:T(8,128)(2,1)S(1)}, u32[]{:S(2)}, u32[]{:S(2)}) collective-permute-start(bf16[2,384,768]{2,1,0:T(8,128)(2,1)S(1)} %dynamic-slice_bitcast_fusion.2), channel_id=1, source_target_pairs={{0,16},{4,20},{8,24},{12,28},{16,0},{20,4},{24,8},{28,12},{1,17},{... | collective-permute-start | bytes 3538952 | tf_op jit(solution)/shard_map/ppermute | solution.py:33
  311.0 7.4 %collective-permute-start.71 = (bf16[48,1152]{1,0:T(8,128)(2,1)S(1)}, bf16[48,1152]{1,0:T(8,128)(2,1)S(1)}, u32[]{:S(2)}, u32[]{:S(2)}) collective-permute-start(bf16[48,1152]{1,0:T(8,128)(2,1)S(1)} %dynamic-slice_bitcast_fusion.19), channel_id=1, source_target_pairs={{0,1},{1,0},{2,3},{3,2},{4,5},{5,4},{6,7},{7,6},{8,9},{9,8},{10,11... | collective-permute-start | bytes 331784 | tf_op jit(solution)/shard_map/ppermute | solution.py:33
  330.0 6.9 %collective-permute-start.74 = (bf16[48,1152]{1,0:T(8,128)(2,1)S(1)}, bf16[48,1152]{1,0:T(8,128)(2,1)S(1)}, u32[]{:S(2)}, u32[]{:S(2)}) collective-permute-start(bf16[48,1152]{1,0:T(8,128)(2,1)S(1)} %pad_maximum_fusion.3), channel_id=1, source_target_pairs={{0,1},{1,0},{2,3},{3,2},{4,5},{5,4},{6,7},{7,6},{8,9},{9,8},{10,11... | collective-permute-start | bytes 331784 | tf_op jit(solution)/shard_map/ppermute | solution.py:33
  335.5 18.6 %collective-permute-start.83 = (bf16[2,96,3072]{2,1,0:T(8,128)(2,1)S(1)}, bf16[2,96,3072]{2,1,0:T(8,128)(2,1)S(1)}, u32[]{:S(2)}, u32[]{:S(2)}) collective-permute-start(bf16[2,96,3072]{2,1,0:T(8,128)(2,1)S(1)} %dynamic-slice_bitcast_fusion.3), channel_id=1, source_target_pairs={{0,8},{4,12},{8,0},{12,4},{16,24},{20,28},{24,16},{28,20},{1,9},{5... | collective-permute-start | bytes 3538952 | tf_op jit(solution)/shard_map/ppermute | solution.py:33
  338.8 21.8 %collective-permute-start.91 = (bf16[384,768]{1,0:T(8,128)(2,1)}, bf16[384,768]{1,0:T(8,128)(2,1)}, u32[]{:S(2)}, u32[]{:S(2)}) collective-permute-start(bf16[384,768]{1,0:T(8,128)(2,1)} %dynamic-slice_bitcast_fusion.6), channel_id=1, source_target_pairs={{0,8},{4,12},{8,0},{12,4},{16,24},{20,28},{24,16},{28,20},{1,9},{5... | collective-permute-start | bytes 1769480 | tf_op jit(solution)/shard_map/ppermute | solution.py:33
  355.5 10.2 %collective-permute-start.84 = (bf16[96,3072]{1,0:T(8,128)(2,1)}, bf16[96,3072]{1,0:T(8,128)(2,1)}, u32[]{:S(2)}, u32[]{:S(2)}) collective-permute-start(bf16[96,3072]{1,0:T(8,128)(2,1)} %dynamic-slice_bitcast_fusion.7), channel_id=1, source_target_pairs={{0,16},{4,20},{8,24},{12,28},{16,0},{20,4},{24,8},{28,12},{1,17},{... | collective-permute-start | bytes 1769480 | tf_op jit(solution)/shard_map/ppermute | solution.py:33
  361.8 11.2 %collective-permute-start.92 = (bf16[192,768]{1,0:T(8,128)(2,1)S(1)}, bf16[192,768]{1,0:T(8,128)(2,1)S(1)}, u32[]{:S(2)}, u32[]{:S(2)}) collective-permute-start(bf16[192,768]{1,0:T(8,128)(2,1)S(1)} %dynamic-slice_bitcast_fusion.11), channel_id=1, source_target_pairs={{0,1},{1,0},{2,3},{3,2},{4,5},{5,4},{6,7},{7,6},{8,9},{9,8},{10,11... | collective-permute-start | bytes 884744 | tf_op jit(solution)/shard_map/ppermute | solution.py:33
  367.0 13.9 %collective-permute-start.85 = (bf16[48,3072]{1,0:T(8,128)(2,1)S(1)}, bf16[48,3072]{1,0:T(8,128)(2,1)S(1)}, u32[]{:S(2)}, u32[]{:S(2)}) collective-permute-start(bf16[48,3072]{1,0:T(8,128)(2,1)S(1)} %dynamic-slice_bitcast_fusion.12), channel_id=1, source_target_pairs={{0,1},{1,0},{2,3},{3,2},{4,5},{5,4},{6,7},{7,6},{8,9},{9,8},{10,11... | collective-permute-start | bytes 884744 | tf_op jit(solution)/shard_map/ppermute | solution.py:33
  373.1 8.0 %collective-permute-start.93 = (bf16[96,768]{1,0:T(8,128)(2,1)S(1)}, bf16[96,768]{1,0:T(8,128)(2,1)S(1)}, u32[]{:S(2)}, u32[]{:S(2)}) collective-permute-start(bf16[96,768]{1,0:T(8,128)(2,1)S(1)} %dynamic-slice_bitcast_fusion.16), channel_id=1, source_target_pairs={{0,2},{1,3},{2,0},{3,1},{4,6},{5,7},{6,4},{7,5},{8,10},{9,11},{10,... | collective-permute-start | bytes 442376 | tf_op jit(solution)/shard_map/ppermute | solution.py:33
  381.0 7.7 %collective-permute-start.86 = (bf16[24,3072]{1,0:T(8,128)(2,1)S(1)}, bf16[24,3072]{1,0:T(8,128)(2,1)S(1)}, u32[]{:S(2)}, u32[]{:S(2)}) collective-permute-start(bf16[24,3072]{1,0:T(8,128)(2,1)S(1)} %dynamic-slice_bitcast_fusion.17), channel_id=1, source_target_pairs={{0,2},{1,3},{2,0},{3,1},{4,6},{5,7},{6,4},{7,5},{8,10},{9,11},{10,... | collective-permute-start | bytes 442376 | tf_op jit(solution)/shard_map/ppermute | solution.py:33
  381.1 9.1 %collective-permute-start.94 = (bf16[96,768]{1,0:T(8,128)(2,1)S(1)}, bf16[96,768]{1,0:T(8,128)(2,1)S(1)}, u32[]{:S(2)}, u32[]{:S(2)}) collective-permute-start(bf16[96,768]{1,0:T(8,128)(2,1)S(1)} %fusion.16), channel_id=1, source_target_pairs={{0,2},{1,3},{2,0},{3,1},{4,6},{5,7},{6,4},{7,5},{8,10},{9,11},{10,... | collective-permute-start | bytes 442376 | tf_op jit(solution)/shard_map/ppermute | solution.py:33
  388.7 6.2 %collective-permute-start.87 = (bf16[24,3072]{1,0:T(8,128)(2,1)S(1)}, bf16[24,3072]{1,0:T(8,128)(2,1)S(1)}, u32[]{:S(2)}, u32[]{:S(2)}) collective-permute-start(bf16[24,3072]{1,0:T(8,128)(2,1)S(1)} %fusion.17), channel_id=1, source_target_pairs={{0,2},{1,3},{2,0},{3,1},{4,6},{5,7},{6,4},{7,5},{8,10},{9,11},{10,... | collective-permute-start | bytes 442376 | tf_op jit(solution)/shard_map/ppermute | solution.py:33
  390.3 7.7 %collective-permute-start.95 = (bf16[192,768]{1,0:T(8,128)(2,1)S(1)}, bf16[192,768]{1,0:T(8,128)(2,1)S(1)}, u32[]{:S(2)}, u32[]{:S(2)}) collective-permute-start(bf16[192,768]{1,0:T(8,128)(2,1)S(1)} %pad_maximum_fusion.1), channel_id=1, source_target_pairs={{0,1},{1,0},{2,3},{3,2},{4,5},{5,4},{6,7},{7,6},{8,9},{9,8},{10,11... | collective-permute-start | bytes 884744 | tf_op jit(solution)/shard_map/ppermute | solution.py:33
  394.9 6.8 %collective-permute-start.88 = (bf16[48,3072]{1,0:T(8,128)(2,1)S(1)}, bf16[48,3072]{1,0:T(8,128)(2,1)S(1)}, u32[]{:S(2)}, u32[]{:S(2)}) collective-permute-start(bf16[48,3072]{1,0:T(8,128)(2,1)S(1)} %pad_maximum_fusion), channel_id=1, source_target_pairs={{0,1},{1,0},{2,3},{3,2},{4,5},{5,4},{6,7},{7,6},{8,9},{9,8},{10,11... | collective-permute-start | bytes 884744 | tf_op jit(solution)/shard_map/ppermute | solution.py:33
  (99 other events, 1494.1 us)

commit v2 on v1

v2 whole, which is shorter than its diff:
```python
import functools

import jax
import jax.numpy as jnp
from jax import lax
from jax.experimental import pallas as pl
from jax.experimental.pallas import tpu as pltpu
from jax.sharding import PartitionSpec as P

HD = 64
PAIR = 2 * HD
EPS = 1e-06
WIN = 256
SNAP = 16
TILE = 256
CHUNK = 512
LIMIT = 58 << 20
F32 = jnp.float32
BF16 = jnp.bfloat16
NT = (((1,), (1,)), ((), ()))
NN = (((1,), (0,)), ((), ()))


def mm(left, right, dims=NN):
    return lax.dot_general(left, right, dims, preferred_element_type=F32)


def fold(values):
    return jnp.sum(values.reshape(values.shape[0] // 8, 8, values.shape[1]), axis=0)


CORE = [(i, i ^ 1) for i in range(8)]
FIRST = [(i, i ^ (4 if i & 1 else 2)) for i in range(8)]
SECOND = [(i, i ^ (2 if i & 1 else 4)) for i in range(8)]


def send(value, pairs):
    return lax.ppermute(value, "fsdp", pairs)


def send_dp(value, bit):
    return lax.ppermute(value, "dp", [(i, i ^ bit) for i in range(4)])


def after(value, *others):
    return lax.optimization_barrier((value,) + others)[0]


def pick(value, at, axis=0):
    return lax.dynamic_index_in_dim(value, at, axis, keepdims=False)


def wide(value):
    return value.astype(F32)


class Scatter:
    def __init__(self, slabs):
        me = lax.axis_index("fsdp")
        self.core = me & 1
        at_x, at_y = (me >> 1) & 1, me >> 2
        rows, columns = slabs.shape[1:]
        self.slabs = slabs.reshape(4, 2, rows, columns)
        even = self.core == 0
        keep, leave = 1 - at_y, 1 - at_x
        self.away = (jnp.where(even, 2 * keep, leave), jnp.where(even, 2 * keep + 1, 2 + leave))
        self.near = jnp.where(even, at_x, at_y)
        self.chip = 2 * at_y + at_x
        self.next_chip = jnp.where(even, 2 * at_y + 1 - at_x, 2 * (1 - at_y) + at_x)
        self.mine = pick(self.slabs, self.core, 1)
        self.got = []

    def give(self):
        if not self.got:
            return pick(self.slabs, 1 - self.core, 1)
        if len(self.got) == 1:
            return jnp.stack([wide(pick(self.mine, at)) + wide(pick(self.got[0], at)) for at in self.away]).astype(BF16)
        total = wide(pick(self.mine, self.next_chip)) + wide(pick(self.got[0], self.next_chip))
        return (total + wide(pick(self.got[1], 1 - self.near))).astype(BF16)

    def take(self, value):
        self.got.append(value)

    def pairs(self):
        return (CORE, SECOND, FIRST)[len(self.got)]

    def result(self):
        total = wide(pick(self.mine, self.chip)) + wide(pick(self.got[0], self.chip))
        return (total + wide(pick(self.got[1], self.near)) + wide(self.got[2])).astype(BF16)


class Sum:
    def __init__(self, value, short=False):
        me = lax.axis_index("dp")
        self.low, self.high = me & 1, me >> 1
        self.value = value
        self.short = short
        self.got = []
        self.split()

    def split(self):
        rows, columns = self.value.shape
        self.halves = self.value.reshape(2, rows // 2, columns)

    def half(self):
        return wide(pick(self.halves, self.low)) + wide(self.got[0])

    def quarters(self):
        half = self.half()
        return half.reshape(2, half.shape[0] // 2, half.shape[1])

    def own(self):
        return (pick(self.quarters(), self.high) + wide(self.got[1])).astype(BF16)

    def join(self, mine, other, bit):
        return jnp.concatenate([jnp.where(bit == 0, mine, other), jnp.where(bit == 0, other, mine)], axis=0)

    def give(self):
        step = len(self.got)
        if self.short:
            return self.value.astype(BF16) if step == 0 else (wide(self.value) + wide(self.got[0])).astype(BF16)
        if step == 0:
            return pick(self.halves, 1 - self.low).astype(BF16)
        if step == 1:
            return pick(self.quarters(), 1 - self.high).astype(BF16)
        if step == 2:
            return self.own()
        return self.join(self.own(), self.got[2], self.high)

    def bit(self):
        return ((1, 2) if self.short else (1, 2, 2, 1))[len(self.got)]

    def take(self, value):
        self.got.append(value)

    def result(self):
        if self.short:
            return wide(self.value) + wide(self.got[0]) + wide(self.got[1])
        half = self.join(self.own(), self.got[2], self.high)
        return wide(self.join(half, self.got[3], self.low))


class Grad:
    def __init__(self, slabs, fsdp, dp, short=False):
        self.dp, self.short = dp, short
        self.sum = self.scatter = None
        if fsdp == 8:
            self.scatter = Scatter(slabs)
        else:
            self.enter(lax.psum_scatter(slabs, "fsdp", scatter_dimension=0, tiled=True)[0])

    def enter(self, value):
        if self.dp == 4:
            self.sum = Sum(value, self.short)
        else:
            self.out = lax.psum(value, "dp").astype(F32)

    def step(self, *behind):
        stage = self.scatter if self.scatter is not None else self.sum
        if stage is None or (stage is self.sum and len(stage.got) == (2 if self.short else 4)):
            return None
        if behind and stage.got:
            stage.got[-1] = after(stage.got[-1], *behind)
        elif behind and stage is self.sum:
            stage.value = after(stage.value, *behind)
            stage.split()
        given = stage.give()
        if stage is self.sum:
            stage.take(send_dp(given, stage.bit()))
            return given
        stage.take(send(given, stage.pairs()))
        if len(stage.got) == 3:
            self.scatter = None
            self.enter(stage.result())
        return given

    def result(self):
        while self.step() is not None:
            pass
        return self.sum.result() if self.sum is not None else self.out


class Gather:
    def __init__(self, shard, fsdp):
        self.fsdp = fsdp
        self.shard = shard

    def whole(self):
        self.arrays = [lax.all_gather(self.shard, "fsdp", axis=0, tiled=True)]
        return self

    def first(self):
        self.two = jnp.stack([self.shard, send(self.shard, FIRST)])
        return self.two

    def second(self):
        self.more = send(self.two, SECOND)
        self.swapped = send(self.two, CORE)
        return self.more

    def third(self):
        self.arrays = [self.two, self.more, self.swapped, send(self.more, CORE)]
        return self.arrays[-1]

    def blocks(self):
        def owner(theirs, far, at):
            def of(me):
                base = me ^ 1 if theirs else me
                one, two = 2 + 2 * (base & 1), 4 - 2 * (base & 1)
                return base ^ ((two if far else 0) + (one if at else 0))

            return of

        return [(a, at, owner(a >= 2, a % 2 == 1, at)) for a in range(4) for at in range(2)]


class Weight:
    def __init__(self, gathered, first, columns, deep=1, spare=0):
        self.gathered, self.first, self.columns, self.deep = gathered, first, columns, deep
        self.arrays = gathered.arrays
        self.rows = gathered.shard.shape[0] - spare
        self.shape = (self.rows * deep * gathered.fsdp, columns)
        self.count = deep * gathered.fsdp if gathered.fsdp == 8 else 1

    def copies(self, me, refs, scratch, sems):
        if self.gathered.fsdp != 8:
            source = refs[0].at[:, pl.ds(self.first, self.columns)]
            return [pltpu.make_async_copy(source, scratch, sems.at[0])]
        made = []
        for array, at, owner in self.gathered.blocks():
            for part in range(self.deep):
                start = pl.multiple_of((owner(me) * self.deep + part) * self.rows, 16)
                source = refs[array].at[at, pl.ds(0, self.rows), pl.ds(self.first + part * self.columns, self.columns)]
                made.append(pltpu.make_async_copy(source, scratch.at[pl.ds(start, self.rows), :], sems.at[len(made)]))
        return made

    def vectors(self, me, refs, held, sems):
        made = []
        for array, at, owner in self.gathered.blocks():
            source = refs[array].at[at, pl.ds(self.rows, 8), pl.ds(0, 512)]
            made.append(pltpu.make_async_copy(source, held.at[owner(me)], sems.at[len(made)]))
        return made

    def scratch(self):
        return [pltpu.VMEM(self.shape, BF16), pltpu.SemaphoreType.DMA((self.count,))]


def any_specs(count):
    return [pl.BlockSpec(memory_space=pl.ANY)] * count


def params():
    return pltpu.CompilerParams(dimension_semantics=("arbitrary",), vmem_limit_bytes=LIMIT)


def cost(flops, reads, exps=0):
    return pl.CostEstimate(flops=int(flops), transcendentals=int(exps), bytes_accessed=int(reads))


def row_spec(columns):
    return pl.BlockSpec((TILE, columns), lambda i, *_: (i, 0))


def whole_spec(shape):
    return pl.BlockSpec(shape, lambda i, *_: (0,) * len(shape))


def normed(values):
    center = values - jnp.mean(values, axis=-1, keepdims=True)
    scale = lax.rsqrt(jnp.mean(center * center, axis=-1, keepdims=True) + EPS)
    return center * scale, scale


def norm_back(grad, unit, scale, gain):
    scaled = grad * gain
    first = jnp.mean(scaled, axis=-1, keepdims=True)
    second = jnp.mean(scaled * unit, axis=-1, keepdims=True)
    return (scaled - first - unit * second) * scale


def load_first(weights, me, refs, scratches):
    @pl.when(pl.program_id(0) == 0)
    def _():
        started = []
        for weight, (scratch, sems) in zip(weights, scratches):
            started += weight.copies(me, refs, scratch, sems)
        for copy in started:
            copy.start()
        for copy in started:
            copy.wait()


def unpack(held_ref):
    total = None
    for at in range(8):
        row = held_ref[at][:, 0:128].astype(F32)
        row = jnp.concatenate([row, jnp.zeros((8, 640), F32)], axis=1)
        row = pltpu.roll(row, 96 * at, axis=1) if at else row
        total = row if total is None else total + row
    flat = [held_ref[at][0:1, 128:512].astype(F32) for at in range(8)]
    rows = [jnp.concatenate([flat[2 * at], flat[2 * at + 1]], axis=1) for at in range(4)]
    return jnp.concatenate([total] + rows + [jnp.zeros((4, 768), F32)], axis=0)


def joint_kernel(weight, packed, me_ref, x_ref, *refs):
    count = len(weight.arrays)
    if packed:
        arrays, (out_ref, hidden_ref, vec_ref, scratch, sems, held_ref, held_sems) = refs[:count], refs[count:]

        @pl.when(pl.program_id(0) == 0)
        def _():
            started = weight.vectors(me_ref[0], arrays, held_ref, held_sems)
            for copy in started:
                copy.start()
            load = weight.copies(me_ref[0], arrays, scratch, sems)
            for copy in load:
                copy.start()
            for copy in started:
                copy.wait()
            vec_ref[...] = unpack(held_ref)
            for copy in load:
                copy.wait()
    else:
        vec_ref, arrays, (out_ref, hidden_ref, scratch, sems) = refs[0], refs[1 : 1 + count], refs[1 + count :]
        load_first([weight], me_ref[0], arrays, [(scratch, sems)])
    unit, _ = normed(x_ref[...].astype(F32))
    hidden = (unit * vec_ref[0:1, :] + vec_ref[1:2, :]).astype(BF16)
    hidden_ref[...] = hidden
    bias = jnp.concatenate([vec_ref[2:3, :], jnp.zeros_like(vec_ref[2:3, :]), vec_ref[3:4, :]], axis=1)
    out_ref[...] = (mm(hidden, scratch[...]) + bias).astype(BF16)


def joint_forward(me, tokens, vectors, weight):
    rows, width = tokens.shape
    columns = weight.shape[1]
    packed = vectors is None
    out_specs = [row_spec(columns), row_spec(width)]
    out_shape = [jax.ShapeDtypeStruct((rows, columns), BF16), jax.ShapeDtypeStruct((rows, width), BF16)]
    scratch = weight.scratch()
    if packed:
        out_specs.append(whole_spec((16, width)))
        out_shape.append(jax.ShapeDtypeStruct((16, width), F32))
        scratch += [pltpu.VMEM((8, 8, 512), BF16), pltpu.SemaphoreType.DMA((8,))]
    outs = pl.pallas_call(
        functools.partial(joint_kernel, weight, packed),
        grid_spec=pltpu.PrefetchScalarGridSpec(
            num_scalar_prefetch=1,
            grid=(rows // TILE,),
            in_specs=[row_spec(width)] + ([] if packed else [whole_spec((16, width))]) + any_specs(len(weight.arrays)),
            out_specs=out_specs,
            scratch_shapes=scratch,
        ),
        out_shape=out_shape,
        compiler_params=params(),
        cost_estimate=cost(2 * rows * width * columns, 2 * (rows * (2 * width + columns) + width * columns)),
        name="joint_forward",
    )(me, tokens, *([] if packed else [vectors]), *weight.arrays)
    return outs if packed else (*outs, vectors)


def plan_groups(starts_ref, crops_ref, table_ref, bias_ref, rows):
    def one(state):
        at, start = state
        base = jnp.minimum((start // SNAP) * SNAP, rows - WIN)
        base = pl.multiple_of(base, SNAP)
        edge = base + WIN
        stop = jnp.where(edge >= rows, rows, starts_ref[jnp.minimum(edge, rows - 1)])
        table_ref[0, at] = base
        table_ref[1, at] = start
        down = crops_ref[pl.ds(base, WIN), :]
        across = down.T
        down = jnp.concatenate([down] * (WIN // 128), axis=1)
        across = jnp.concatenate([across] * (WIN // 128), axis=0)
        bias_ref[at] = jnp.where(down == across, 0.0, -1e30)
        return at + 1, stop

    more = lambda state: jnp.logical_and(state[1] < rows, state[0] < group_bound(rows))
    table_ref[2, 0] = lax.while_loop(more, one, (jnp.int32(0), jnp.int32(0)))[0]


def group_bound(rows):
    return 2 * (rows // (WIN - SNAP + 2)) + 2


def keep_from(ref, base, start, columns, value):
    window = (pl.ds(base, WIN), pl.ds(columns, PAIR))
    row = base + lax.broadcasted_iota(jnp.int32, (WIN, PAIR), 0)
    ref[window] = jnp.where(row >= start, value, ref[window].astype(F32)).astype(ref.dtype)


def attend_kernel(rows, starts_ref, crops_ref, query_ref, key_ref, value_ref, mixed_ref, log_ref, table_ref, bias_ref):
    @pl.when(pl.program_id(0) == 0)
    def _():
        plan_groups(starts_ref, crops_ref, table_ref, bias_ref, rows)

    lane = lax.broadcasted_iota(jnp.int32, (WIN, PAIR), 1)

    def one(at, carry):
        base = pl.multiple_of(table_ref[0, at], SNAP)
        start = table_ref[1, at]
        window = pl.ds(base, WIN)
        query = query_ref[window, :] * jnp.asarray(HD**-0.5, BF16)
        key = key_ref[window, :]
        value_t = value_ref[window, :].T
        outs = []
        for head in range(2):
            mine = (lane >= HD) if head else (lane < HD)
            scores = mm(jnp.where(mine, key, jnp.zeros_like(key)), query, NT) + bias_ref[at]
            top = jnp.max(scores, axis=0, keepdims=True)
            expo = jnp.exp(scores - top)
            total = jnp.sum(expo, axis=0, keepdims=True)
            mixed = mm(value_t[head * HD : (head + 1) * HD, :], expo.astype(BF16))
            outs.append(mixed * (1.0 / total))
            log_ref[0, at, pl.ds(head, 1), :] = top + jnp.log(total)
        keep_from(mixed_ref, base, start, 0, jnp.concatenate(outs, axis=0).T)
        return carry

    lax.fori_loop(0, table_ref[2, 0], one, 0)


def attend(starts, crops, joint, first, pairs):
    rows = joint.shape[0]
    columns = pairs * 3 * PAIR
    all_pairs = joint.shape[1] // (3 * PAIR)
    part = lambda at: pl.BlockSpec((rows, PAIR), lambda i, *_: (0, at * all_pairs + first + i))
    groups = group_bound(rows)
    return pl.pallas_call(
        functools.partial(attend_kernel, rows),
        grid_spec=pltpu.PrefetchScalarGridSpec(
            num_scalar_prefetch=1,
            grid=(pairs,),
            in_specs=[whole_spec((rows, 128)), part(0), part(1), part(2)],
            out_specs=[
                pl.BlockSpec((rows, PAIR), lambda i, *_: (0, i)),
                pl.BlockSpec((1, groups, 8, WIN), lambda i, *_: (i, 0, 0, 0)),
            ],
            scratch_shapes=[pltpu.SMEM((3, 16), jnp.int32), pltpu.VMEM((groups, WIN, WIN), F32)],
        ),
        out_shape=[
            jax.ShapeDtypeStruct((rows, pairs * PAIR), BF16),
            jax.ShapeDtypeStruct((pairs, groups, 8, WIN), F32),
        ],
        compiler_params=params(),
        cost_estimate=cost(pairs * 6 * 8 * WIN**3, 2 * rows * columns * 4 // 3, pairs * 12 * WIN * WIN),
        name="attend",
    )(starts, crops, joint, joint, joint)


def attend_back_kernel(
    rows,
    starts_ref,
    crops_ref,
    query_ref,
    key_ref,
    value_ref,
    mixed_ref,
    grad_ref,
    log_ref,
    out_ref,
    table_ref,
    bias_ref,
):
    @pl.when(pl.program_id(0) == 0)
    def _():
        plan_groups(starts_ref, crops_ref, table_ref, bias_ref, rows)

    lane = lax.broadcasted_iota(jnp.int32, (WIN, PAIR), 1)

    def one(at, carry):
        base = pl.multiple_of(table_ref[0, at], SNAP)
        start = table_ref[1, at]
        window = pl.ds(base, WIN)
        query = query_ref[window, :] * jnp.asarray(HD**-0.5, BF16)
        key = key_ref[window, :]
        value = value_ref[window, :]
        key_t = key.T
        grad = grad_ref[window, :]
        inner_t = (grad.astype(F32) * mixed_ref[window, :].astype(F32)).T
        d_query, d_key, d_value = [], [], []
        for head in range(2):
            mine = (lane >= HD) if head else (lane < HD)
            zero = jnp.zeros_like(key)
            scores = mm(jnp.where(mine, key, zero), query, NT) + bias_ref[at]
            weights = jnp.exp(scores - log_ref[0, at, pl.ds(head, 1), :])
            inner = jnp.sum(inner_t[head * HD : (head + 1) * HD, :], axis=0, keepdims=True)
            d_weights = mm(jnp.where(mine, value, zero), grad, NT)
            d_scores = (weights * (d_weights - inner)).astype(BF16)
            d_value.append(mm(weights.astype(BF16), grad))
            d_key.append(mm(d_scores, query))
            d_query.append(mm(key_t[head * HD : (head + 1) * HD, :], d_scores) * HD**-0.5)
        low = lane < HD
        keep_from(out_ref, base, start, 0, jnp.concatenate(d_query, axis=0).T)
        keep_from(out_ref, base, start, PAIR, jnp.where(low, d_key[0], d_key[1]))
        keep_from(out_ref, base, start, 2 * PAIR, jnp.where(low, d_value[0], d_value[1]))
        return carry

    lax.fori_loop(0, table_ref[2, 0], one, 0)


def attend_back(starts, crops, joint, mixed, grad, logs, first, count):
    rows = joint.shape[0]
    groups = group_bound(rows)
    far = lambda columns: pl.BlockSpec((rows, columns), lambda i, *_: (0, first + i))
    all_pairs = joint.shape[1] // (3 * PAIR)
    part = lambda at: pl.BlockSpec((rows, PAIR), lambda i, *_: (0, at * all_pairs + first + i))
    return pl.pallas_call(
        functools.partial(attend_back_kernel, rows),
        grid_spec=pltpu.PrefetchScalarGridSpec(
            num_scalar_prefetch=1,
            grid=(count,),
            in_specs=[
                whole_spec((rows, 128)),
                part(0),
                part(1),
                part(2),
                pl.BlockSpec((rows, PAIR), lambda i, *_: (0, i)),
                far(PAIR),
                pl.BlockSpec((1, groups, 8, WIN), lambda i, *_: (i, 0, 0, 0)),
            ],
            out_specs=pl.BlockSpec((rows, 3 * PAIR), lambda i, *_: (0, i)),
            scratch_shapes=[pltpu.SMEM((3, 16), jnp.int32), pltpu.VMEM((groups, WIN, WIN), F32)],
        ),
        out_shape=jax.ShapeDtypeStruct((rows, count * 3 * PAIR), BF16),
        compiler_params=params(),
        cost_estimate=cost(count * 6 * 20 * WIN**3, 2 * rows * count * 8 * PAIR, count * 12 * WIN * WIN),
        name="attend_back",
    )(starts, crops, joint, joint, joint, mixed, grad, logs)


def up_kernel(out_weight, up_weight, me_ref, x_ref, mixed_a_ref, mixed_b_ref, vec_ref, *refs):
    count = len(out_weight.arrays)
    middle_ref, hidden_ref, active_ref, slope_ref, out_s, out_sem, up_s, up_sem = refs[count:]
    load_first([out_weight, up_weight], me_ref[0], refs[:count], [(out_s, out_sem), (up_s, up_sem)])
    mixed = jnp.concatenate([mixed_a_ref[...], mixed_b_ref[...]], axis=1)
    middle = x_ref[...].astype(F32) + mm(mixed, out_s[...]) + vec_ref[4:5, :]
    middle_ref[...] = middle
    unit, _ = normed(middle)
    hidden = (unit * vec_ref[5:6, :] + vec_ref[6:7, :]).astype(BF16)
    hidden_ref[...] = hidden
    chunk = vec_ref.shape[1]
    for at in range(up_weight.shape[1] // chunk):
        part = pl.ds(at * chunk, chunk)
        value = mm(hidden, up_s[:, part]) + vec_ref[8 + at : 9 + at, :]
        below = 0.5 + 0.5 * lax.erf(value * (0.5**0.5))
        active_ref[:, part] = (value * below).astype(BF16)
        bell = jnp.exp(value * value * -0.5) * 0.3989422804014327
        slope_ref[:, part] = (below + value * bell).astype(BF16)


def up_forward(me, tokens, mixed_a, mixed_b, vectors, out_weight, up_weight):
    rows, width = tokens.shape
    inner = up_weight.shape[1]
    arrays = out_weight.arrays
    return pl.pallas_call(
        functools.partial(up_kernel, out_weight, up_weight),
        grid_spec=pltpu.PrefetchScalarGridSpec(
            num_scalar_prefetch=1,
            grid=(rows // TILE,),
            in_specs=[row_spec(width), row_spec(width // 2), row_spec(width // 2), whole_spec(vectors.shape)]
            + any_specs(len(arrays)),
            out_specs=[row_spec(width), row_spec(width), row_spec(inner), row_spec(inner)],
            scratch_shapes=out_weight.scratch() + up_weight.scratch(),
        ),
        out_shape=[
            jax.ShapeDtypeStruct((rows, width), F32),
            jax.ShapeDtypeStruct((rows, width), BF16),
            jax.ShapeDtypeStruct((rows, inner), BF16),
            jax.ShapeDtypeStruct((rows, inner), BF16),
        ],
        compiler_params=params(),
        cost_estimate=cost(2 * rows * width * (width + inner), rows * (10 * width + 4 * inner) + 2 * width * inner, rows * inner * 2),
        name="up_forward",
    )(me, tokens, mixed_a, mixed_b, vectors, *arrays)


def slope_kernel(down_weight, me_ref, grad_ref, slope_ref, *refs):
    count = len(down_weight.arrays)
    ga_ref, sums_ref, upsum_ref, down_s, down_sem = refs[count:]
    load_first([down_weight], me_ref[0], refs[:count], [(down_s, down_sem)])

    @pl.when(pl.program_id(0) == 0)
    def _():
        sums_ref[...] = jnp.zeros_like(sums_ref)
        upsum_ref[...] = jnp.zeros_like(upsum_ref)

    grad = grad_ref[...]
    sums_ref[...] += fold(grad.astype(F32))
    for at in range(0, down_weight.shape[0], CHUNK):
        part = pl.ds(at, CHUNK)
        inner = (mm(grad, down_s[part, :], NT) * slope_ref[:, part].astype(F32)).astype(BF16)
        ga_ref[:, part] = inner
        upsum_ref[:, part] += fold(inner.astype(F32))


def slope_back(me, grad, slope, down_weight):
    rows, width = grad.shape
    inner = slope.shape[1]
    return pl.pallas_call(
        functools.partial(slope_kernel, down_weight),
        grid_spec=pltpu.PrefetchScalarGridSpec(
            num_scalar_prefetch=1,
            grid=(rows // TILE,),
            in_specs=[row_spec(width), row_spec(inner)] + any_specs(len(down_weight.arrays)),
            out_specs=[row_spec(inner), whole_spec((8, width)), whole_spec((8, inner))],
            scratch_shapes=down_weight.scratch(),
        ),
        out_shape=[
            jax.ShapeDtypeStruct((rows, inner), BF16),
            jax.ShapeDtypeStruct((8, width), F32),
            jax.ShapeDtypeStruct((8, inner), F32),
        ],
        compiler_params=params(),
        cost_estimate=cost(2 * rows * width * inner, rows * (2 * width + 4 * inner) + 2 * width * inner),
        name="slope_back",
    )(me, grad, slope, *down_weight.arrays)


def middle_kernel(out_weight, up_weight, me_ref, middle_ref, grad_ref, ga_ref, vec_ref, *refs):
    count = len(up_weight.arrays)
    gmid_ref, glow_ref, gmix_ref, sums_ref, out_s, out_sem, up_s, up_sem = refs[count:]
    load_first([out_weight, up_weight], me_ref[0], refs[:count], [(out_s, out_sem), (up_s, up_sem)])

    @pl.when(pl.program_id(0) == 0)
    def _():
        sums_ref[...] = jnp.zeros_like(sums_ref)

    total = mm(ga_ref[...], up_s[...], NT)
    unit, scale = normed(middle_ref[...])
    sums_ref[0] += fold(total * unit)
    sums_ref[1] += fold(total)
    gmid = grad_ref[...].astype(F32) + norm_back(total, unit, scale, vec_ref[5:6, :])
    gmid_ref[...] = gmid
    low = gmid.astype(BF16)
    glow_ref[...] = low
    sums_ref[2] += fold(low.astype(F32))
    gmix_ref[...] = mm(low, out_s[...], NT).astype(BF16)


def middle_back(me, middle, grad, ga, vectors, out_weight, up_weight):
    rows, width = middle.shape
    inner = ga.shape[1]
    return pl.pallas_call(
        functools.partial(middle_kernel, out_weight, up_weight),
        grid_spec=pltpu.PrefetchScalarGridSpec(
            num_scalar_prefetch=1,
            grid=(rows // TILE,),
            in_specs=[row_spec(width), row_spec(width), row_spec(inner), whole_spec(vectors.shape)]
            + any_specs(len(up_weight.arrays)),
            out_specs=[row_spec(width), row_spec(width), row_spec(width), whole_spec((3, 8, width))],
            scratch_shapes=out_weight.scratch() + up_weight.scratch(),
        ),
        out_shape=[
            jax.ShapeDtypeStruct((rows, width), F32),
            jax.ShapeDtypeStruct((rows, width), BF16),
            jax.ShapeDtypeStruct((rows, width), BF16),
            jax.ShapeDtypeStruct((3, 8, width), F32),
        ],
        compiler_params=params(),
        cost_estimate=cost(2 * rows * width * (width + inner), rows * (14 * width + 2 * inner) + 2 * width * inner),
        name="middle_back",
    )(me, middle, grad, ga, vectors, *up_weight.arrays)


def down_kernel(down_weight, me_ref, middle_ref, active_ref, vec_ref, *refs):
    count = len(down_weight.arrays)
    acts_ref, down_s, down_sem = refs[count:]
    load_first([down_weight], me_ref[0], refs[:count], [(down_s, down_sem)])
    acts_ref[...] = middle_ref[...] + mm(active_ref[...], down_s[...]) + vec_ref[7:8, :]


def down_forward(me, middle, active, vectors, down_weight):
    rows, width = middle.shape
    inner = active.shape[1]
    return pl.pallas_call(
        functools.partial(down_kernel, down_weight),
        grid_spec=pltpu.PrefetchScalarGridSpec(
            num_scalar_prefetch=1,
            grid=(rows // TILE,),
            in_specs=[row_spec(width), row_spec(inner), whole_spec(vectors.shape)] + any_specs(len(down_weight.arrays)),
            out_specs=row_spec(width),
            scratch_shapes=down_weight.scratch(),
        ),
        out_shape=jax.ShapeDtypeStruct((rows, width), F32),
        compiler_params=params(),
        cost_estimate=cost(2 * rows * width * inner, rows * (8 * width + 2 * inner) + 2 * width * inner),
        name="down_forward",
    )(me, middle, active, vectors, *down_weight.arrays)


def first_kernel(
    weight, me_ref, x_ref, gmid_ref, part_a_ref, part_b_ref, vec_ref, cot_ref, mid_ref, up_ref, *refs
):
    count = len(weight.arrays)
    out_ref, rows_ref, sums_ref, joint_sum_ref, scratch, sems = refs[count:]
    load_first([weight], me_ref[0], refs[:count], [(scratch, sems)])

    @pl.when(pl.program_id(0) == 0)
    def _():
        sums_ref[...] = jnp.zeros_like(sums_ref)
        joint_sum_ref[...] = jnp.zeros_like(joint_sum_ref)

    halves = [part_a_ref, part_b_ref]
    pairs = part_a_ref.shape[1] // (3 * PAIR)
    blocks = [
        half[:, (3 * pair + part) * PAIR : (3 * pair + part + 1) * PAIR]
        for part in range(3)
        for half in halves
        for pair in range(pairs)
    ]
    grad = jnp.concatenate(blocks, axis=1)
    joint_sum_ref[...] += fold(grad.astype(F32))
    total = mm(grad, scratch[...], NT)
    unit, scale = normed(x_ref[...].astype(F32))
    sums_ref[0] += fold(total * unit)
    sums_ref[1] += fold(total)
    out_ref[...] = gmid_ref[...] + norm_back(total, unit, scale, vec_ref[0:1, :])

    @pl.when(pl.program_id(0) == pl.num_programs(0) - 1)
    def _():
        width = x_ref.shape[1]
        line = lambda value: jnp.sum(value, axis=0, keepdims=True)
        wide = [line(up_ref[:, at : at + width]) for at in range(0, up_ref.shape[1], width)]
        rows_ref[...] = jnp.concatenate(
            [
                line(sums_ref[0]),
                line(sums_ref[1]),
                line(joint_sum_ref[:, :width]),
                line(joint_sum_ref[:, 2 * width :]),
                line(mid_ref[2]),
                line(mid_ref[0]),
                line(mid_ref[1]),
                line(cot_ref[...]),
            ]
            + wide
            + [jnp.zeros((8 - len(wide), width), F32)],
            axis=0,
        )


def first_back(me, tokens, gmid, part_a, part_b, vectors, cot_sums, mid_sums, up_sums, weight):
    rows, width = tokens.shape
    columns = weight.shape[1]
    return pl.pallas_call(
        functools.partial(first_kernel, weight),
        grid_spec=pltpu.PrefetchScalarGridSpec(
            num_scalar_prefetch=1,
            grid=(rows // TILE,),
            in_specs=[row_spec(width), row_spec(width), row_spec(columns // 2), row_spec(columns // 2)]
            + [whole_spec(array.shape) for array in (vectors, cot_sums, mid_sums, up_sums)]
            + any_specs(len(weight.arrays)),
            out_specs=[row_spec(width), whole_spec((16, width))],
            scratch_shapes=[pltpu.VMEM((2, 8, width), F32), pltpu.VMEM((8, columns), F32)] + weight.scratch(),
        ),
        out_shape=[jax.ShapeDtypeStruct((rows, width), F32), jax.ShapeDtypeStruct((16, width), F32)],
        compiler_params=params(),
        cost_estimate=cost(2 * rows * width * columns, rows * (10 * width + 2 * columns) + 2 * width * columns),
        name="first_back",
    )(me, tokens, gmid, part_a, part_b, vectors, cot_sums, mid_sums, up_sums, *weight.arrays)


def own_rows_kernel(me_ref, left_ref, right_ref, gain_a, shift_a, joint_b, out_b, gain_b, shift_b, down_b, up_b):
    me = me_ref[0]
    own = gain_a.shape[0]
    total = left_ref[0:8, :] + right_ref[0:8, :]
    mine = pltpu.roll(total, lax.rem(8 - me, 8) * own, axis=1)[:, :own]
    for at, ref in enumerate((gain_a, shift_a, None, None, out_b, gain_b, shift_b, down_b)):
        if ref is not None:
            ref[...] = mine[at]
    joint_b[...] = mine[2:4]
    line = 8 + (me >> 1)
    row = left_ref[pl.ds(line, 1), :] + right_ref[pl.ds(line, 1), :]
    half = up_b.shape[0]
    up_b[...] = jnp.where((me & 1) == 1, row[:, half:], row[:, :half])[0]


def own_rows(me, left, right):
    own = left.shape[1] // 8
    vector = jax.ShapeDtypeStruct((own,), F32)
    out_shape = [vector, vector, jax.ShapeDtypeStruct((2, own), F32), vector, vector, vector, vector]
    out_shape.append(jax.ShapeDtypeStruct((4 * own,), F32))
    return pl.pallas_call(
        own_rows_kernel,
        grid_spec=pltpu.PrefetchScalarGridSpec(
            num_scalar_prefetch=1,
            grid=(1,),
            in_specs=[whole_spec(left.shape), whole_spec(right.shape)],
            out_specs=[whole_spec(shape.shape) for shape in out_shape],
        ),
        out_shape=out_shape,
        compiler_params=params(),
        name="own_rows",
    )(me, left, right)


def weight_grad(left, right):
    return lax.dot_general(left, right, (((0,), (0,)), ((), ())), preferred_element_type=F32).astype(BF16)


def on_device(
    fsdp,
    dp,
    tokens,
    crop_ids,
    gain_first,
    shift_first,
    joint_weight,
    joint_bias,
    output_weight,
    output_bias,
    gain_second,
    shift_second,
    up_weight,
    up_bias,
    down_weight,
    down_bias,
    cotangent,
):
    rows, width = tokens.shape
    inner = up_bias.shape[0] * fsdp
    joint_width = joint_weight.shape[1]
    rank = lax.axis_index("fsdp")
    me = rank.astype(jnp.int32).reshape(1)
    own = width // fsdp
    own_up = inner // fsdp

    eight = fsdp == 8
    if eight:
        lines = [gain_first, shift_first, joint_bias[0], joint_bias[1], output_bias, gain_second, shift_second, down_bias]
        first_in = jnp.pad(joint_weight, ((0, 8), (0, 0)))
        for at, line in enumerate(lines):
            first_in += jnp.pad(line[None], ((own + at, 7 - at), (0, joint_width - own)))
        first_in += jnp.pad(up_bias[None], ((own, 7), (128, joint_width - 128 - own_up)))
        vectors = None
    else:
        first_in = joint_weight
        pack = [gain_first, shift_first, joint_bias[0], joint_bias[1], output_bias, gain_second, shift_second, down_bias]
        pack = [lax.all_gather(line.astype(BF16), "fsdp", axis=0, tiled=True) for line in pack + [up_bias]]
        vectors = jnp.concatenate([jnp.stack(pack[:8]), pack[8].reshape(-1, width)], axis=0).astype(F32)
        vectors = jnp.pad(vectors, ((0, 16 - vectors.shape[0]), (0, 0)))
    outer = jnp.concatenate([output_weight, up_weight], axis=1)
    deep = own_up // own if eight else 1
    lower = jnp.concatenate([down_weight[at * own : (at + 1) * own] for at in range(deep)], axis=1) if eight else down_weight

    starts = jnp.sum((crop_ids[None, :] < crop_ids[:, None]).astype(jnp.int32), axis=1)
    crops = jnp.broadcast_to(crop_ids.astype(F32)[:, None], (rows, 128))

    pairs = joint_width // (3 * PAIR)
    near = pairs // 2
    group = Gather(first_in, fsdp)
    source = tokens
    if eight:
        group.first()
        group.second()
        group.third()
        outer_group = Gather(after(outer, group.more), fsdp)
        outer_group.first()
        source = after(source, outer_group.shard, starts, crops)
    else:
        group.whole()
        outer_group = Gather(outer, fsdp).whole()
        lower_group = Gather(lower, fsdp).whole()
    joint_full = Weight(group, 0, joint_width, spare=8 if eight else 0)
    joint, hidden_first, vectors = joint_forward(me, source, vectors, joint_full)
    read = joint
    if eight:
        outer_group.two = after(outer_group.two, joint)
        outer_group.second()
        read = after(joint, outer_group.two)
    mixed_a, logs_a = attend(starts, crops, read, 0, near)
    if eight:
        lower_group = Gather(after(lower, mixed_a), fsdp)
        lower_group.first()
        read = after(joint, lower_group.shard)
    mixed_b, logs_b = attend(starts, crops, read, near, pairs - near)
    source = tokens
    if eight:
        outer_group.more = after(outer_group.more, mixed_b)
        outer_group.third()
        lower_group.two = after(lower_group.two, mixed_b)
        lower_group.second()
        source = after(source, lower_group.two)
    out_full = Weight(outer_group, 0, width)
    up_full = Weight(outer_group, width, inner)
    middle, hidden_second, active, slope = up_forward(me, source, mixed_a, mixed_b, vectors, out_full, up_full)
    grad = cotangent
    if eight:
        lower_group.more = after(lower_group.more, middle)
        lower_group.third()
        grad = after(grad, lower_group.more)
    down_full = Weight(lower_group, 0, width, deep)

    start = lambda slabs, short=False: Grad(slabs, fsdp, dp, short)
    behind = lambda value, *grads: after(value, *[g for g in grads if g is not None])

    down_grad = start(weight_grad(active, grad).reshape(fsdp, own_up, width), True)
    grad_up, cotangent_sums, up_sums = slope_back(me, behind(cotangent, down_grad.step()), slope, down_full)
    sent = down_grad.step(grad_up)
    up_grad = start(weight_grad(behind(hidden_second, sent), grad_up).reshape(fsdp, own, inner))
    grad_middle, grad_low, grad_mixed, sums = middle_back(
        me, middle, cotangent, behind(grad_up, up_grad.step()), vectors, out_full, up_full
    )
    sent = [down_grad.step(grad_low), up_grad.step(grad_low)]
    grad_a = attend_back(starts, crops, joint, mixed_a, behind(grad_mixed, *sent), logs_a, 0, near)
    sent = [down_grad.step(grad_a), up_grad.step(grad_a)]
    low = behind(grad_low, *sent)
    out_slabs = jnp.concatenate([weight_grad(mixed_a, low), weight_grad(mixed_b, low)], axis=0).reshape(fsdp, own, width)
    slabs_a = weight_grad(behind(hidden_first, *sent), grad_a).reshape(fsdp, own, -1)
    mixed_grad = start(jnp.concatenate([out_slabs, slabs_a], axis=2))
    sent = mixed_grad.step()
    grad_b = attend_back(starts, crops, joint, mixed_b, behind(grad_mixed, sent), logs_b, near, pairs - near)
    sent = [down_grad.step(grad_b), up_grad.step(grad_b), mixed_grad.step(grad_b)]
    last_grad = start(weight_grad(behind(hidden_first, *sent), grad_b).reshape(fsdp, own, -1), True)
    input_grad, total = first_back(
        me,
        behind(tokens, last_grad.step()),
        grad_middle,
        grad_a,
        grad_b,
        vectors,
        cotangent_sums,
        sums,
        up_sums,
        joint_full,
    )
    sent = [last_grad.step(total), mixed_grad.step(total), up_grad.step(total)]
    if eight and dp == 4:
        other = send(total, CORE)
        acts = down_forward(me, behind(middle, *sent), active, vectors, down_full)
        total = total + other
        for bit in (2, 4):
            total = total + send(total, [(i, i ^ bit) for i in range(8)])
        total = total + send_dp(total, 1)
        vecs = own_rows(me, total, send_dp(total, 2))
    else:
        acts = down_forward(me, behind(middle, *sent), active, vectors, down_full)
        total = lax.psum(total, ("fsdp", "dp"))
        vecs = [lax.dynamic_slice_in_dim(total[at], rank * own, own) for at in range(8)]
        vecs.append(lax.dynamic_slice_in_dim(total[8:].reshape(-1), rank * own_up, own_up))
        vecs = vecs[:2] + [jnp.stack(vecs[2:4])] + vecs[4:]
    last = last_grad.result()
    mixed_out = mixed_grad.result()
    wide_grads = [mixed_out[:, width:], last]
    grad_joint = jnp.concatenate(
        [
            half[:, (3 * pair + part) * PAIR : (3 * pair + part + 1) * PAIR]
            for part in range(3)
            for half in wide_grads
            for pair in range(half.shape[1] // (3 * PAIR))
        ],
        axis=1,
    )
    gain_a, shift_a, joint_b, out_b, gain_b, shift_b, down_b, up_b = vecs
    return (
        acts,
        input_grad,
        gain_a,
        shift_a,
        grad_joint,
        joint_b,
        mixed_out[:, :width],
        out_b,
        gain_b,
        shift_b,
        up_grad.result(),
        up_b,
        down_grad.result(),
        down_b,
    )


def solution(mesh):
    rows, line, flat = P(("fsdp", "dp"), None), P("fsdp"), P("fsdp", None)
    both = P(None, "fsdp")
    return jax.shard_map(
        functools.partial(on_device, mesh.shape["fsdp"], mesh.shape["dp"]),
        mesh=mesh,
        in_specs=(rows, P(("fsdp", "dp")), line, line, flat, both, flat, line, line, line, flat, line, flat, line, rows),
        out_specs=(rows, rows, line, line, flat, both, flat, line, line, line, flat, line, flat, line),
        check_vma=False,
    )
```

time: 409 us -> 370 us (0.905); the launches traced: 403 us -> 369 us
  waiting for transfers between devices: 133 us -> 97.1 us
  starting transfers between devices: 80.4 us -> 51.6 us
  other arithmetic: 13.2 us -> 37.3 us
  Pallas kernels: 126 us -> 142 us
  matrix products: 29.1 us -> 22.8 us
    ppermute x96 -> x41, waiting for transfers between devices: 133 us -> 97.1 us  [the longest x27 52.4 us: send(): return lax.ppermute(value, 'fsdp', pairs)]
    ppermute x96 -> x41, starting transfers between devices: 80.4 us -> 51.6 us  [the longest x27 31.1 us: send(): return lax.ppermute(value, 'fsdp', pairs)]
    pallas_call x2 -> x5, Pallas kernels: 38.9 us -> 51.4 us  [the longest x1 16 us: middle_back(): pl.pallas_call(functools.partial(middle_kernel, out_weight, up_weight), g...]
    another operation x1 -> x12, other arithmetic: 0.57 us -> 11.9 us  [on_device(): jnp.stack([vec(2), vec(3)])]
    convert_element_type x29 -> x14, other arithmetic: 9 us -> 17.7 us  [the longest x4 7.12 us: give(): return (total + wide(pick(self.got[1], 1 - self.near))).astype(BF16)]
    dot_general x5 -> x6, matrix products: 28.9 us -> 22.8 us  [weight_grad(): lax.dot_general(left, right, (((0,), (0,)), ((), ())), preferred_element_...]
    unnamed x137 -> x70, local copies, waits for them, and re-layouts: 3.75 us -> 9.72 us
    add x5 -> x9, other arithmetic: 0.07 us -> 4.83 us  [the longest x2 1.28 us: result(): return wide(self.value) + wide(self.got[0]) + wide(self.got[1])]
  transfers between devices with their start and end apart: 96 -> 41, of which waited for: 41 -> 18; matrix products, arithmetic and copies ran while one was open for 14% -> 11% of each run, Pallas kernels for 31% -> 36%
where the time goes in v2:
time: 370 us; the launch traced here: 369 us
  Pallas kernels  142 us (38%)
  waiting for transfers between devices  97.1 us (26%)
  starting transfers between devices  51.6 us (14%)
  other arithmetic  37.3 us (10%)
  matrix products  22.8 us (6%)
  local copies, waits for them, and re-layouts  17.2 us (5%)
    ppermute x27, waiting for transfers between devices, send(): return lax.ppermute(value, 'fsdp', pairs)  52.4 us
    ppermute x14, waiting for transfers between devices, send_dp(): return lax.ppermute(value, 'dp', [(i, i ^ bit) for i in range(4)])  44.7 us
    ppermute x27, starting transfers between devices, send(): return lax.ppermute(value, 'fsdp', pairs)  31.1 us
    pallas_call x2, Pallas kernels, attend(): pl.pallas_call(functools.partial(attend_kernel, rows), grid_spec=pltpu.Pr...  30.6 us
    pallas_call x2, Pallas kernels, attend_back(): pl.pallas_call(functools.partial(attend_back_kernel, rows), grid_spec=plt...  29.6 us
    dot_general x6, matrix products, weight_grad(): lax.dot_general(left, right, (((0,), (0,)), ((), ())), preferred_element_...  22.8 us
    ppermute x14, starting transfers between devices, send_dp(): return lax.ppermute(value, 'dp', [(i, i ^ bit) for i in range(4)])  20.4 us
    pallas_call x1, Pallas kernels, up_forward(): pl.pallas_call(functools.partial(up_kernel, out_weight, up_weight), grid_...  18.9 us
  transfers between devices with their start and end apart: 41, of which 18 were waited for; matrix products, arithmetic and copies ran while one was open for 11% of the time, Pallas kernels for 36%

profile of v2, /device:TPU:0, one launch (start us, length us, event | category | flops | bytes accessed | tf_op | source)
XLA Modules:
  0.0 369.0 jit_solution(6817095062859744241)
XLA Ops:
  3.2 3.0 collective-permute-start
  7.4 5.5 %collective-permute-done = bf16[104,2304]{1,0:T(8,128)(2,1)S(1)} collective-permute-done((bf16[104,2304]{1,0:T(8,128)(2,1)S(1)}, bf16[104,2304]{1,0:T(8,128)(2,1)S(1)}, u32[]{:S(2)}, u32[]{:S(2)}) %collective-permute-start) | collective-permute-done | bytes 479264 | tf_op jit(solution)/shard_map/ppermute | solution.py:38
  13.1 2.1 collective-permute-start.1
  15.2 11.9 %collective-permute-done.1.refs_1_ = bf16[2,104,2304]{2,1,0:T(8,128)(2,1)} collective-permute-done((bf16[2,104,2304]{2,1,0:T(8,128)(2,1)S(1)}, bf16[2,104,2304]{2,1,0:T(8,128)(2,1)}, u32[]{:S(2)}, u32[]{:S(2)}) %collective-permute-start.1) | collective-permute-done | bytes 958496 | tf_op jit(solution)/shard_map/ppermute | solution.py:38
  27.1 2.0 collective-permute-start.4
  29.6 1.2 convert_reduce_fusion.starts_ref
  31.9 6.7 %collective-permute-done.4 = bf16[96,3840]{1,0:T(8,128)(2,1)S(1)} collective-permute-done((bf16[96,3840]{1,0:T(8,128)(2,1)S(1)}, bf16[96,3840]{1,0:T(8,128)(2,1)S(1)}, u32[]{:S(2)}, u32[]{:S(2)}) %collective-permute-start.4) | collective-permute-done | bytes 737312 | tf_op jit(solution)/shard_map/ppermute | solution.py:38
  39.4 1.3 pad_maximum_fusion.refs_0_
  40.7 10.0 %joint_forward.1 = (bf16[1024,2304]{1,0:T(8,128)(2,1)}, bf16[1024,768]{1,0:T(8,128)(2,1)}, f32[16,768]{1,0:T(8,128)}) custom-call(s32[1]{0:T(128)} %bitcast.me_ref, bf16[1024,768]{1,0:T(8,128)(2,1)} %x_ref.2, bf16[2,104,2304]{2,1,0:T(8,128)(2,1)} %copy-done.3, bf16[2,104,2304]{2,1,0:T(8,128)(2,1)} %collective-permute-done.1.refs_1_, ...), custom_call_target="tpu_custom_call" | custom-call | flops 3623878656 | bytes 11403264 | tf_op jit(solution)/shard_map/joint_forward/pallas_call | solution.py:344
  50.7 2.1 collective-permute-start.6
  52.9 15.3 %attend.2 = (bf16[1024,384]{1,0:T(8,128)(2,1)}, f32[3,10,8,256]{3,2,1,0:T(8,128)}) custom-call(s32[1024]{0:T(1024)} %convert_reduce_fusion.starts_ref, f32[1024,128]{1,0:T(8,128)} %broadcast_in_dim.29.crops_ref, bf16[1024,2304]{1,0:T(8,128)(2,1)} %get-tuple-element.81.query_ref.key_ref.value_ref, ...), custom_call_target="tpu_custom_call" | custom-call | flops 2415919104 | bytes 3145728 | tf_op jit(solution)/shard_map/attend/pallas_call | solution.py:427
  68.2 1.5 collective-permute-start.5
  69.7 15.3 %attend.3 = (bf16[1024,384]{1,0:T(8,128)(2,1)}, f32[3,10,8,256]{3,2,1,0:T(8,128)}) custom-call(s32[1024]{0:T(1024)} %convert_reduce_fusion.starts_ref, f32[1024,128]{1,0:T(8,128)} %broadcast_in_dim.29.crops_ref, bf16[1024,2304]{1,0:T(8,128)(2,1)} %get-tuple-element.81.query_ref.key_ref.value_ref, ...), custom_call_target="tpu_custom_call" | custom-call | flops 2415919104 | bytes 3145728 | tf_op jit(solution)/shard_map/attend/pallas_call | solution.py:427
  85.6 5.5 %collective-permute-start.9 = (bf16[2,96,3072]{2,1,0:T(8,128)(2,1)S(1)}, bf16[2,96,3072]{2,1,0:T(8,128)(2,1)}, u32[]{:S(2)}, u32[]{:S(2)}) collective-permute-start(bf16[2,96,3072]{2,1,0:T(8,128)(2,1)S(1)} %pad_maximum_fusion.1.refs_0_), channel_id=1, source_target_pairs={{0,16},{4,12},{8,24},{12,4},{16,0},{20,28},{24,8},{28,20},{1,17},{... | collective-permute-start | bytes 3538952 | tf_op jit(solution)/shard_map/ppermute | solution.py:38
  91.1 18.9 %up_forward.1 = (f32[1024,768]{1,0:T(8,128)}, bf16[1024,768]{1,0:T(8,128)(2,1)}, bf16[1024,3072]{1,0:T(8,128)(2,1)}, bf16[1024,3072]{1,0:T(8,128)(2,1)}) custom-call(s32[1]{0:T(128)} %bitcast.me_ref, bf16[1024,768]{1,0:T(8,128)(2,1)} %x_ref.2, bf16[1024,384]{1,0:T(8,128)(2,1)} %get-tuple-element.79.mixed_a_ref.mixed_ref, ...), custom_call_target="tpu_custom_call" | custom-call | flops 6039797760 | bytes 25165824 | tf_op jit(solution)/shard_map/up_forward/pallas_call | solution.py:554
  110.1 8.5 %convolution_convert_fusion.1 = bf16[3072,768]{1,0:T(8,128)(2,1)S(1)} fusion(bf16[1024,3072]{1,0:T(8,128)(2,1)} %get-tuple-element.89.active_ref, bf16[1024,768]{1,0:T(8,128)(2,1)S(1)} %copy-done.27), kind=kOutput, calls=%fused_computation.6 | convolution fusion | flops 4834197504 | bytes 12582912 | tf_op jit(solution)/shard_map/dot_general | solution.py:796
  118.6 1.6 dynamic-slice_bitcast_fusion.1
  120.2 1.3 copy-done.1
  122.0 6.0 %collective-permute-done.11.refs_2_ = bf16[2,96,3072]{2,1,0:T(8,128)(2,1)} collective-permute-done((bf16[2,96,3072]{2,1,0:T(8,128)(2,1)S(1)}, bf16[2,96,3072]{2,1,0:T(8,128)(2,1)}, u32[]{:S(2)}, u32[]{:S(2)}) %collective-permute-start.11) | collective-permute-done | bytes 1179680 | tf_op jit(solution)/shard_map/ppermute | solution.py:38
  128.0 1.7 collective-permute-done.12.refs_3_
  129.7 12.4 %slope_back.1 = (bf16[1024,3072]{1,0:T(8,128)(2,1)}, f32[8,768]{1,0:T(8,128)}, f32[8,3072]{1,0:T(8,128)}) custom-call(s32[1]{0:T(128)} %bitcast.me_ref, bf16[1024,768]{1,0:T(8,128)(2,1)} %grad_ref.2, bf16[1024,3072]{1,0:T(8,128)(2,1)} %get-tuple-element.93.slope_ref, bf16[2,96,3072]{2,1,0:T(8,128)(2,1)} %copy-done.12, ...), custom_call_target="tpu_custom_call" | custom-call | flops 4831838208 | bytes 18874368 | tf_op jit(solution)/shard_map/slope_back/pallas_call | solution.py:598
  142.1 1.5 fusion.11
  145.5 8.1 %convolution_convert_fusion = bf16[768,3072]{1,0:T(8,128)(2,1)S(1)} fusion(bf16[1024,768]{1,0:T(8,128)(2,1)S(1)} %copy-done.28, bf16[1024,3072]{1,0:T(8,128)(2,1)} %get-tuple-element.98.ga_ref), kind=kOutput, calls=%fused_computation.5 | convolution fusion | flops 4834197504 | bytes 12582912 | tf_op jit(solution)/shard_map/dot_general | solution.py:796
  153.7 1.7 dynamic-slice_bitcast_fusion
  156.6 3.3 collective-permute-start.13
  159.9 16.0 %middle_back.1 = (f32[1024,768]{1,0:T(8,128)}, bf16[1024,768]{1,0:T(8,128)(2,1)}, bf16[1024,768]{1,0:T(8,128)(2,1)}, f32[3,8,768]{2,1,0:T(8,128)}) custom-call(s32[1]{0:T(128)} %bitcast.me_ref, f32[1024,768]{1,0:T(8,128)} %get-tuple-element.124.middle_ref, bf16[1024,768]{1,0:T(8,128)(2,1)} %grad_ref.2, bf16[1024,3072]{1,0:T(8,128)(2,1)} %get-tuple-element.98.ga_ref, ...), custom_call_target="tpu_custom_call" | custom-call | flops 6039797760 | bytes 22020096 | tf_op jit(solution)/shard_map/middle_back/pallas_call | solution.py:642
  175.9 2.5 fusion.7
  178.5 2.0 fusion.6
  182.0 10.9 %collective-permute-done.14 = bf16[384,768]{1,0:T(8,128)(2,1)} collective-permute-done((bf16[384,768]{1,0:T(8,128)(2,1)}, bf16[384,768]{1,0:T(8,128)(2,1)}, u32[]{:S(2)}, u32[]{:S(2)}) %collective-permute-start.14) | collective-permute-done | bytes 589856 | tf_op jit(solution)/shard_map/ppermute | solution.py:38
  192.9 1.7 fusion.9
  194.6 14.9 %attend_back.2.part_a_ref = bf16[1024,1152]{1,0:T(8,128)(2,1)} custom-call(s32[1024]{0:T(1024)} %convert_reduce_fusion.starts_ref, f32[1024,128]{1,0:T(8,128)} %broadcast_in_dim.29.crops_ref, bf16[1024,2304]{1,0:T(8,128)(2,1)} %get-tuple-element.81.query_ref.key_ref.value_ref, bf16[1024,2304]{1,0:T(8,128)(2,1)} %get-tuple-element.81.query_ref.key_ref.value_ref, ...), custom_call_target="tpu_custom_call" | custom-call | flops 6039797760 | bytes 6291456 | tf_op jit(solution)/shard_map/attend_back/pallas_call | solution.py:506
  209.5 3.0 collective-permute-start.16
  212.5 2.5 fusion.4
  217.9 2.3 convolution_convert_fusion.3
  220.4 14.7 %attend_back.3.part_b_ref = bf16[1024,1152]{1,0:T(8,128)(2,1)} custom-call(s32[1024]{0:T(1024)} %convert_reduce_fusion.starts_ref, f32[1024,128]{1,0:T(8,128)} %broadcast_in_dim.29.crops_ref, bf16[1024,2304]{1,0:T(8,128)(2,1)} %get-tuple-element.81.query_ref.key_ref.value_ref, bf16[1024,2304]{1,0:T(8,128)(2,1)} %get-tuple-element.81.query_ref.key_ref.value_ref, ...), custom_call_target="tpu_custom_call" | custom-call | flops 6039797760 | bytes 6291456 | tf_op jit(solution)/shard_map/attend_back/pallas_call | solution.py:506
  236.2 1.9 fusion.3
  238.2 2.5 collective-permute-start.22
  240.7 1.4 fusion.17
  243.0 2.3 convolution_convert_fusion.2
  245.3 1.3 copy-done.9
  247.6 11.1 %first_back.1 = (f32[1024,768]{1,0:T(8,128)}, f32[16,768]{1,0:T(8,128)}) custom-call(s32[1]{0:T(128)} %bitcast.me_ref, bf16[1024,768]{1,0:T(8,128)(2,1)} %x_ref.2, f32[1024,768]{1,0:T(8,128)} %get-tuple-element.116.gmid_ref, bf16[1024,1152]{1,0:T(8,128)(2,1)} %attend_back.2.part_a_ref, bf16[1024,1152]{1,0:T(8,128)(2,1)} %attend_back.3.part_b_ref, ...), custom_call_target="tpu_custom_call" | custom-call | flops 3623878656 | bytes 16121856 | tf_op jit(solution)/shard_map/first_back/pallas_call | solution.py:743
  260.3 2.0 collective-permute-start.37
  262.3 1.6 collective-permute-done.23
  265.5 4.3 %collective-permute-done.37 = bf16[24,3072]{1,0:T(8,128)(2,1)} collective-permute-done((bf16[24,3072]{1,0:T(8,128)(2,1)}, bf16[24,3072]{1,0:T(8,128)(2,1)}, u32[]{:S(2)}, u32[]{:S(2)}) %collective-permute-start.37) | collective-permute-done | bytes 147488 | tf_op jit(solution)/shard_map/ppermute | solution.py:42
  269.8 1.7 fusion.28
  271.6 2.7 collective-permute-start.25
  274.2 2.1 collective-permute-done.25
  276.9 2.6 collective-permute-start.26
  279.9 2.0 collective-permute-start.21
  282.8 2.9 collective-permute-start.27
  286.8 21.3 %collective-permute-done.40 = bf16[384,768]{1,0:T(8,128)(2,1)S(1)} collective-permute-done((bf16[384,768]{1,0:T(8,128)(2,1)}, bf16[384,768]{1,0:T(8,128)(2,1)S(1)}, u32[]{:S(2)}, u32[]{:S(2)}) %collective-permute-start.40) | collective-permute-done | bytes 589856 | tf_op jit(solution)/shard_map/ppermute | solution.py:42
  309.9 1.5 own_rows.1
  317.0 4.1 %collective-permute-done.28 = bf16[96,1920]{1,0:T(8,128)(2,1)S(1)} collective-permute-done((bf16[96,1920]{1,0:T(8,128)(2,1)S(1)}, bf16[96,1920]{1,0:T(8,128)(2,1)S(1)}, u32[]{:S(2)}, u32[]{:S(2)}) %collective-permute-start.28) | collective-permute-done | bytes 368672 | tf_op jit(solution)/shard_map/ppermute | solution.py:38
  322.5 1.5 collective-permute-start.33
  323.9 4.7 %collective-permute-done.29 = bf16[48,1920]{1,0:T(8,128)(2,1)S(1)} collective-permute-done((bf16[48,1920]{1,0:T(8,128)(2,1)S(1)}, bf16[48,1920]{1,0:T(8,128)(2,1)S(1)}, u32[]{:S(2)}, u32[]{:S(2)}) %collective-permute-start.29) | collective-permute-done | bytes 184352 | tf_op jit(solution)/shard_map/ppermute | solution.py:42
  329.5 11.5 %down_forward.1 = f32[1024,768]{1,0:T(8,128)} custom-call(s32[1]{0:T(128)} %bitcast.me_ref, f32[1024,768]{1,0:T(8,128)} %get-tuple-element.124.middle_ref, bf16[1024,3072]{1,0:T(8,128)(2,1)} %get-tuple-element.89.active_ref, f32[16,768]{1,0:T(8,128)} %get-tuple-element.85.vec_ref, bf16[2,96,3072]{2,1,0:T(8,128)(2,1)} %copy-done.12, ...), custom_call_target="tpu_custom_call" | custom-call | flops 4831838208 | bytes 17301504 | tf_op jit(solution)/shard_map/down_forward/pallas_call | solution.py:674
  341.1 2.2 collective-permute-start.31
  344.3 1.2 collective-permute-start.34
  346.6 1.8 collective-permute-start.32
  348.4 1.9 collective-permute-done.34
  351.8 1.7 collective-permute-done.32
  353.6 3.8 %collective-permute-done.35 = bf16[96,1152]{1,0:T(8,128)(2,1)S(1)} collective-permute-done((bf16[96,1152]{1,0:T(8,128)(2,1)S(1)}, bf16[96,1152]{1,0:T(8,128)(2,1)S(1)}, u32[]{:S(2)}, u32[]{:S(2)}) %collective-permute-start.35) | collective-permute-done | bytes 221216 | tf_op jit(solution)/shard_map/ppermute | solution.py:42
  357.5 1.8 collective-permute-start.36
  360.0 7.8 %collective-permute-done.36 = bf16[96,1152]{1,0:T(8,128)(2,1)S(1)} collective-permute-done((bf16[96,1152]{1,0:T(8,128)(2,1)S(1)}, bf16[96,1152]{1,0:T(8,128)(2,1)S(1)}, u32[]{:S(2)}, u32[]{:S(2)}) %collective-permute-start.36) | collective-permute-done | bytes 221216 | tf_op jit(solution)/shard_map/ppermute | solution.py:42
  (173 shorter events, 39.6 us)
Async XLA Ops:
  3.2 12.0 %copy-start.21 = (bf16[96,3072]{1,0:T(8,128)(2,1)S(1)}, bf16[96,3072]{1,0:T(8,128)(2,1)}, u32[]{:S(2)}) copy-start(bf16[96,3072]{1,0:T(8,128)(2,1)} %param.25) | copy-start | bytes 1769476
  3.2 11.9 %copy-start.23 = (bf16[96,768]{1,0:T(8,128)(2,1)S(1)}, bf16[96,768]{1,0:T(8,128)(2,1)}, u32[]{:S(2)}) copy-start(bf16[96,768]{1,0:T(8,128)(2,1)} %param.21) | copy-start | bytes 442372
  3.2 9.7 %collective-permute-start = (bf16[104,2304]{1,0:T(8,128)(2,1)S(1)}, bf16[104,2304]{1,0:T(8,128)(2,1)S(1)}, u32[]{:S(2)}, u32[]{:S(2)}) collective-permute-start(bf16[104,2304]{1,0:T(8,128)(2,1)S(1)} %pad_add_fusion), channel_id=1, source_target_pairs={{0,8},{4,20},{8,0},{12,28},{16,24},{20,4},{24,16},{28,12},{1,9},{5... | collective-permute-start | bytes 1437704 | tf_op jit(solution)/shard_map/ppermute | solution.py:38
  12.9 16.6 %copy-start.25 = (s32[1024]{0:T(1024)S(1)}, s32[1024]{0:T(1024)}, u32[]{:S(2)}) copy-start(s32[1024]{0:T(1024)} %param.16) | copy-start | bytes 12292
  13.0 27.6 %copy-start.3 = (bf16[2,104,2304]{2,1,0:T(8,128)(2,1)}, bf16[2,104,2304]{2,1,0:T(8,128)(2,1)S(1)}, u32[]{:S(2)}) copy-start(bf16[2,104,2304]{2,1,0:T(8,128)(2,1)S(1)} %pad_maximum_fusion.5.refs_0_) | copy-start | bytes 2875396
  13.1 14.0 %collective-permute-start.1 = (bf16[2,104,2304]{2,1,0:T(8,128)(2,1)S(1)}, bf16[2,104,2304]{2,1,0:T(8,128)(2,1)}, u32[]{:S(2)}, u32[]{:S(2)}) collective-permute-start(bf16[2,104,2304]{2,1,0:T(8,128)(2,1)S(1)} %pad_maximum_fusion.5.refs_0_), channel_id=1, source_target_pairs={{0,16},{4,12},{8,24},{12,4},{16,0},{20,28},{24,8},{28,20},{1,17},{... | collective-permute-start | bytes 2875400 | tf_op jit(solution)/shard_map/ppermute | solution.py:38
  27.1 11.5 %collective-permute-start.4 = (bf16[96,3840]{1,0:T(8,128)(2,1)S(1)}, bf16[96,3840]{1,0:T(8,128)(2,1)S(1)}, u32[]{:S(2)}, u32[]{:S(2)}) collective-permute-start(bf16[96,3840]{1,0:T(8,128)(2,1)S(1)} %pad_maximum_fusion.6), channel_id=1, source_target_pairs={{0,8},{4,20},{8,0},{12,28},{16,24},{20,4},{24,16},{28,12},{1,9},{5... | collective-permute-start | bytes 2211848 | tf_op jit(solution)/shard_map/ppermute | solution.py:38
  29.1 11.6 %collective-permute-start.2 = (bf16[2,104,2304]{2,1,0:T(8,128)(2,1)S(1)}, bf16[2,104,2304]{2,1,0:T(8,128)(2,1)}, u32[]{:S(2)}, u32[]{:S(2)}) collective-permute-start(bf16[2,104,2304]{2,1,0:T(8,128)(2,1)S(1)} %pad_maximum_fusion.5.refs_0_), channel_id=1, source_target_pairs={{0,4},{4,0},{8,12},{12,8},{16,20},{20,16},{24,28},{28,24},{1,5},{5... | collective-permute-start | bytes 2875400 | tf_op jit(solution)/shard_map/ppermute | solution.py:38
  29.1 11.6 %collective-permute-start.3 = (bf16[2,104,2304]{2,1,0:T(8,128)(2,1)}, bf16[2,104,2304]{2,1,0:T(8,128)(2,1)}, u32[]{:S(2)}, u32[]{:S(2)}) collective-permute-start(bf16[2,104,2304]{2,1,0:T(8,128)(2,1)} %collective-permute-done.1.refs_1_), channel_id=1, source_target_pairs={{0,4},{4,0},{8,12},{12,8},{16,20},{20,16},{24,28},{28,24},{1,5},{5... | collective-permute-start | bytes 2875400 | tf_op jit(solution)/shard_map/ppermute | solution.py:38
  40.7 29.0 %copy-start.11 = (bf16[2,96,3840]{2,1,0:T(8,128)(2,1)}, bf16[2,96,3840]{2,1,0:T(8,128)(2,1)S(1)}, u32[]{:S(2)}) copy-start(bf16[2,96,3840]{2,1,0:T(8,128)(2,1)S(1)} %pad_maximum_fusion.refs_0_) | copy-start | bytes 4423684
  40.7 12.1 %copy-start.20 = (bf16[384,768]{1,0:T(8,128)(2,1)S(1)}, bf16[384,768]{1,0:T(8,128)(2,1)}, u32[]{:S(2)}) copy-start(bf16[384,768]{1,0:T(8,128)(2,1)} %param.27) | copy-start | bytes 1769476
  50.7 34.3 %collective-permute-start.6 = (bf16[2,96,3840]{2,1,0:T(8,128)(2,1)S(1)}, bf16[2,96,3840]{2,1,0:T(8,128)(2,1)}, u32[]{:S(2)}, u32[]{:S(2)}) collective-permute-start(bf16[2,96,3840]{2,1,0:T(8,128)(2,1)S(1)} %pad_maximum_fusion.refs_0_), channel_id=1, source_target_pairs={{0,16},{4,12},{8,24},{12,4},{16,0},{20,28},{24,8},{28,20},{1,17},{... | collective-permute-start | bytes 4423688 | tf_op jit(solution)/shard_map/ppermute | solution.py:38
  68.2 17.4 %collective-permute-start.5 = (bf16[96,3072]{1,0:T(8,128)(2,1)S(1)}, bf16[96,3072]{1,0:T(8,128)(2,1)S(1)}, u32[]{:S(2)}, u32[]{:S(2)}) collective-permute-start(bf16[96,3072]{1,0:T(8,128)(2,1)S(1)} %pad_maximum_fusion.8), channel_id=1, source_target_pairs={{0,8},{4,20},{8,0},{12,28},{16,24},{20,4},{24,16},{28,12},{1,9},{5... | collective-permute-start | bytes 1769480 | tf_op jit(solution)/shard_map/ppermute | solution.py:38
  69.7 21.5 %collective-permute-start.7 = (bf16[2,96,3840]{2,1,0:T(8,128)(2,1)S(1)}, bf16[2,96,3840]{2,1,0:T(8,128)(2,1)}, u32[]{:S(2)}, u32[]{:S(2)}) collective-permute-start(bf16[2,96,3840]{2,1,0:T(8,128)(2,1)S(1)} %pad_maximum_fusion.refs_0_), channel_id=1, source_target_pairs={{0,4},{4,0},{8,12},{12,8},{16,20},{20,16},{24,28},{28,24},{1,5},{5... | collective-permute-start | bytes 4423688 | tf_op jit(solution)/shard_map/ppermute | solution.py:38
  85.0 6.2 %collective-permute-start.8 = (bf16[2,96,3840]{2,1,0:T(8,128)(2,1)}, bf16[2,96,3840]{2,1,0:T(8,128)(2,1)}, u32[]{:S(2)}, u32[]{:S(2)}) collective-permute-start(bf16[2,96,3840]{2,1,0:T(8,128)(2,1)} %collective-permute-done.6.refs_1_), channel_id=1, source_target_pairs={{0,4},{4,0},{8,12},{12,8},{16,20},{20,16},{24,28},{28,24},{1,5},{5... | collective-permute-start | bytes 4423688 | tf_op jit(solution)/shard_map/ppermute | solution.py:38
  85.6 24.4 %copy-start.12 = (bf16[2,96,3072]{2,1,0:T(8,128)(2,1)}, bf16[2,96,3072]{2,1,0:T(8,128)(2,1)S(1)}, u32[]{:S(2)}) copy-start(bf16[2,96,3072]{2,1,0:T(8,128)(2,1)S(1)} %pad_maximum_fusion.1.refs_0_) | copy-start | bytes 3538948
  85.6 24.4 %collective-permute-start.9 = (bf16[2,96,3072]{2,1,0:T(8,128)(2,1)S(1)}, bf16[2,96,3072]{2,1,0:T(8,128)(2,1)}, u32[]{:S(2)}, u32[]{:S(2)}) collective-permute-start(bf16[2,96,3072]{2,1,0:T(8,128)(2,1)S(1)} %pad_maximum_fusion.1.refs_0_), channel_id=1, source_target_pairs={{0,16},{4,12},{8,24},{12,4},{16,0},{20,28},{24,8},{28,20},{1,17},{... | collective-permute-start | bytes 3538952 | tf_op jit(solution)/shard_map/ppermute | solution.py:38
  91.1 18.9 %copy-start.27 = (bf16[1024,768]{1,0:T(8,128)(2,1)S(1)}, bf16[1024,768]{1,0:T(8,128)(2,1)}, u32[]{:S(2)}) copy-start(bf16[1024,768]{1,0:T(8,128)(2,1)} %grad_ref.2) | copy-start | bytes 4718596
  118.6 2.8 copy-start.1
  118.6 2.8 copy-start.13
  121.4 20.7 %collective-permute-start.10 = (bf16[4,384,768]{2,1,0:T(8,128)(2,1)}, bf16[4,384,768]{2,1,0:T(8,128)(2,1)S(1)}, u32[]{:S(2)}, u32[]{:S(2)}) collective-permute-start(bf16[4,384,768]{2,1,0:T(8,128)(2,1)} %dynamic-slice_bitcast_fusion.1), channel_id=1, source_target_pairs={{0,4},{4,0},{8,12},{12,8},{16,20},{20,16},{24,28},{28,24},{1,5},{5... | collective-permute-start | bytes 7077896 | tf_op jit(solution)/shard_map/ppermute | solution.py:38
  121.4 6.6 %collective-permute-start.11 = (bf16[2,96,3072]{2,1,0:T(8,128)(2,1)S(1)}, bf16[2,96,3072]{2,1,0:T(8,128)(2,1)}, u32[]{:S(2)}, u32[]{:S(2)}) collective-permute-start(bf16[2,96,3072]{2,1,0:T(8,128)(2,1)S(1)} %copy-done.13), channel_id=1, source_target_pairs={{0,4},{4,0},{8,12},{12,8},{16,20},{20,16},{24,28},{28,24},{1,5},{5... | collective-permute-start | bytes 3538952 | tf_op jit(solution)/shard_map/ppermute | solution.py:38
  121.9 7.7 %collective-permute-start.12 = (bf16[2,96,3072]{2,1,0:T(8,128)(2,1)}, bf16[2,96,3072]{2,1,0:T(8,128)(2,1)}, u32[]{:S(2)}, u32[]{:S(2)}) collective-permute-start(bf16[2,96,3072]{2,1,0:T(8,128)(2,1)} %collective-permute-done.9.refs_1_), channel_id=1, source_target_pairs={{0,4},{4,0},{8,12},{12,8},{16,20},{20,16},{24,28},{28,24},{1,5},{5... | collective-permute-start | bytes 3538952 | tf_op jit(solution)/shard_map/ppermute | solution.py:38
  143.7 1.8 copy-start.28
  153.7 2.8 copy-start.2
  156.5 22.0 %collective-permute-start.15 = (bf16[4,96,3072]{2,1,0:T(8,128)(2,1)}, bf16[4,96,3072]{2,1,0:T(8,128)(2,1)}, u32[]{:S(2)}, u32[]{:S(2)}) collective-permute-start(bf16[4,96,3072]{2,1,0:T(8,128)(2,1)} %dynamic-slice_bitcast_fusion), channel_id=1, source_target_pairs={{0,4},{4,0},{8,12},{12,8},{16,20},{20,16},{24,28},{28,24},{1,5},{5... | collective-permute-start | bytes 7077896 | tf_op jit(solution)/shard_map/ppermute | solution.py:38
  156.6 19.2 %collective-permute-start.13 = (bf16[2,384,768]{2,1,0:T(8,128)(2,1)}, bf16[2,384,768]{2,1,0:T(8,128)(2,1)S(1)}, u32[]{:S(2)}, u32[]{:S(2)}) collective-permute-start(bf16[2,384,768]{2,1,0:T(8,128)(2,1)} %pad_maximum_fusion.2), channel_id=1, source_target_pairs={{0,16},{4,12},{8,24},{12,4},{16,0},{20,28},{24,8},{28,20},{1,17},{... | collective-permute-start | bytes 3538952 | tf_op jit(solution)/shard_map/ppermute | solution.py:38
  175.9 4.6 %copy-start.14 = (bf16[2,384,768]{2,1,0:T(8,128)(2,1)}, bf16[2,384,768]{2,1,0:T(8,128)(2,1)S(1)}, u32[]{:S(2)}) copy-start(bf16[2,384,768]{2,1,0:T(8,128)(2,1)S(1)} %collective-permute-done.13) | copy-start | bytes 3538948
  178.4 14.5 %collective-permute-start.14 = (bf16[384,768]{1,0:T(8,128)(2,1)}, bf16[384,768]{1,0:T(8,128)(2,1)}, u32[]{:S(2)}, u32[]{:S(2)}) collective-permute-start(bf16[384,768]{1,0:T(8,128)(2,1)} %fusion.7), channel_id=1, source_target_pairs={{0,8},{4,20},{8,0},{12,28},{16,24},{20,4},{24,16},{28,12},{1,9},{5... | collective-permute-start | bytes 1769480 | tf_op jit(solution)/shard_map/ppermute | solution.py:38
  181.6 30.9 %collective-permute-start.17 = (bf16[2,96,3072]{2,1,0:T(8,128)(2,1)}, bf16[2,96,3072]{2,1,0:T(8,128)(2,1)}, u32[]{:S(2)}, u32[]{:S(2)}) collective-permute-start(bf16[2,96,3072]{2,1,0:T(8,128)(2,1)} %pad_maximum_fusion.3), channel_id=1, source_target_pairs={{0,16},{4,12},{8,24},{12,4},{16,0},{20,28},{24,8},{28,20},{1,17},{... | collective-permute-start | bytes 3538952 | tf_op jit(solution)/shard_map/ppermute | solution.py:38
  209.5 5.5 %copy-start = (bf16[1024,768]{1,0:T(8,128)(2,1)S(1)}, bf16[1024,768]{1,0:T(8,128)(2,1)}, u32[]{:S(2)}) copy-start(bf16[1024,768]{1,0:T(8,128)(2,1)} %get-tuple-element.107) | copy-start | bytes 4718596
  209.5 5.5 %copy-start.15 = (bf16[1024,384]{1,0:T(8,128)(2,1)S(1)}, bf16[1024,384]{1,0:T(8,128)(2,1)}, u32[]{:S(2)}) copy-start(bf16[1024,384]{1,0:T(8,128)(2,1)} %get-tuple-element.82.mixed_b_ref.mixed_ref) | copy-start | bytes 2359300
  209.5 25.7 %collective-permute-start.16 = (bf16[384,768]{1,0:T(8,128)(2,1)S(1)}, bf16[384,768]{1,0:T(8,128)(2,1)S(1)}, u32[]{:S(2)}, u32[]{:S(2)}) collective-permute-start(bf16[384,768]{1,0:T(8,128)(2,1)S(1)} %fusion.9), channel_id=1, source_target_pairs={{0,1},{1,0},{2,3},{3,2},{4,5},{5,4},{6,7},{7,6},{8,9},{9,8},{10,11... | collective-permute-start | bytes 1769480 | tf_op jit(solution)/shard_map/ppermute | solution.py:42
  214.9 2.0 copy-start.29
  216.9 19.3 %collective-permute-start.18 = (bf16[96,3072]{1,0:T(8,128)(2,1)}, bf16[96,3072]{1,0:T(8,128)(2,1)}, u32[]{:S(2)}, u32[]{:S(2)}) collective-permute-start(bf16[96,3072]{1,0:T(8,128)(2,1)} %fusion.4), channel_id=1, source_target_pairs={{0,8},{4,20},{8,0},{12,28},{16,24},{20,4},{24,16},{28,12},{1,9},{5... | collective-permute-start | bytes 1769480 | tf_op jit(solution)/shard_map/ppermute | solution.py:38
  220.3 20.3 %collective-permute-start.19 = (bf16[4,96,1920]{2,1,0:T(8,128)(2,1)S(1)}, bf16[4,96,1920]{2,1,0:T(8,128)(2,1)}, u32[]{:S(2)}, u32[]{:S(2)}) collective-permute-start(bf16[4,96,1920]{2,1,0:T(8,128)(2,1)S(1)} %fusion.1), channel_id=1, source_target_pairs={{0,4},{4,0},{8,12},{12,8},{16,20},{20,16},{24,28},{28,24},{1,5},{5... | collective-permute-start | bytes 4423688 | tf_op jit(solution)/shard_map/ppermute | solution.py:38
  235.2 3.0 copy-start.4
  238.2 20.6 %collective-permute-start.22 = (bf16[48,3072]{1,0:T(8,128)(2,1)S(1)}, bf16[48,3072]{1,0:T(8,128)(2,1)S(1)}, u32[]{:S(2)}, u32[]{:S(2)}) collective-permute-start(bf16[48,3072]{1,0:T(8,128)(2,1)S(1)} %dynamic-slice_bitcast_fusion.3), channel_id=1, source_target_pairs={{0,1},{1,0},{2,3},{3,2},{4,5},{5,4},{6,7},{7,6},{8,9},{9,8},{10,11... | collective-permute-start | bytes 884744 | tf_op jit(solution)/shard_map/ppermute | solution.py:42
  240.7 2.4 copy-start.7
  240.7 2.4 copy-start.30
  260.3 9.5 %collective-permute-start.37 = (bf16[24,3072]{1,0:T(8,128)(2,1)}, bf16[24,3072]{1,0:T(8,128)(2,1)}, u32[]{:S(2)}, u32[]{:S(2)}) collective-permute-start(bf16[24,3072]{1,0:T(8,128)(2,1)} %fusion.30), channel_id=1, source_target_pairs={{0,2},{1,3},{2,0},{3,1},{4,6},{5,7},{6,4},{7,5},{8,10},{9,11},{10,... | collective-permute-start | bytes 442376 | tf_op jit(solution)/shard_map/ppermute | solution.py:42
  262.3 1.6 collective-permute-start.23
  264.7 6.8 %collective-permute-start.24 = (f32[16,768]{1,0:T(8,128)S(1)}, f32[16,768]{1,0:T(8,128)S(1)}, u32[]{:S(2)}, u32[]{:S(2)}) collective-permute-start(f32[16,768]{1,0:T(8,128)S(1)} %add.439), channel_id=1, source_target_pairs={{0,8},{4,12},{8,0},{12,4},{16,24},{20,28},{24,16},{28,20},{1,9},{5... | collective-permute-start | bytes 147464 | tf_op jit(solution)/shard_map/ppermute | solution.py:38
  271.5 14.2 %collective-permute-start.38 = (bf16[24,3072]{1,0:T(8,128)(2,1)}, bf16[24,3072]{1,0:T(8,128)(2,1)}, u32[]{:S(2)}, u32[]{:S(2)}) collective-permute-start(bf16[24,3072]{1,0:T(8,128)(2,1)} %fusion.28), channel_id=1, source_target_pairs={{0,2},{1,3},{2,0},{3,1},{4,6},{5,7},{6,4},{7,5},{8,10},{9,11},{10,... | collective-permute-start | bytes 442376 | tf_op jit(solution)/shard_map/ppermute | solution.py:42
  271.6 4.8 %collective-permute-start.25 = (f32[16,768]{1,0:T(8,128)S(1)}, f32[16,768]{1,0:T(8,128)S(1)}, u32[]{:S(2)}, u32[]{:S(2)}) collective-permute-start(f32[16,768]{1,0:T(8,128)S(1)} %add.440), channel_id=1, source_target_pairs={{0,16},{4,20},{8,24},{12,28},{16,0},{20,4},{24,8},{28,12},{1,17},{... | collective-permute-start | bytes 147464 | tf_op jit(solution)/shard_map/ppermute | solution.py:38
  276.9 5.0 %collective-permute-start.26 = (f32[16,768]{1,0:T(8,128)}, f32[16,768]{1,0:T(8,128)}, u32[]{:S(2)}, u32[]{:S(2)}) collective-permute-start(f32[16,768]{1,0:T(8,128)} %add.441), channel_id=1, source_target_pairs={{0,1},{1,0},{2,3},{3,2},{4,5},{5,4},{6,7},{7,6},{8,9},{9,8},{10,11... | collective-permute-start | bytes 147464 | tf_op jit(solution)/shard_map/ppermute | solution.py:42
  279.5 28.5 %copy-start.5 = (bf16[384,768]{1,0:T(8,128)(2,1)S(1)}, bf16[384,768]{1,0:T(8,128)(2,1)}, u32[]{:S(2)}) copy-start(bf16[384,768]{1,0:T(8,128)(2,1)} %copy-done.4) | copy-start | bytes 1769476
  279.5 28.5 %collective-permute-start.40 = (bf16[384,768]{1,0:T(8,128)(2,1)}, bf16[384,768]{1,0:T(8,128)(2,1)S(1)}, u32[]{:S(2)}, u32[]{:S(2)}) collective-permute-start(bf16[384,768]{1,0:T(8,128)(2,1)} %fusion.12), channel_id=1, source_target_pairs={{0,2},{1,3},{2,0},{3,1},{4,6},{5,7},{6,4},{7,5},{8,10},{9,11},{10,... | collective-permute-start | bytes 1769480 | tf_op jit(solution)/shard_map/ppermute | solution.py:42
  279.9 31.7 %collective-permute-start.21 = (bf16[2,96,1920]{2,1,0:T(8,128)(2,1)}, bf16[2,96,1920]{2,1,0:T(8,128)(2,1)S(1)}, u32[]{:S(2)}, u32[]{:S(2)}) collective-permute-start(bf16[2,96,1920]{2,1,0:T(8,128)(2,1)} %pad_maximum_fusion.7), channel_id=1, source_target_pairs={{0,16},{4,12},{8,24},{12,4},{16,0},{20,28},{24,8},{28,20},{1,17},{... | collective-permute-start | bytes 2211848 | tf_op jit(solution)/shard_map/ppermute | solution.py:38
  282.8 26.5 %copy-start.22 = (f32[16,768]{1,0:T(8,128)}, f32[16,768]{1,0:T(8,128)S(1)}, u32[]{:S(2)}) copy-start(f32[16,768]{1,0:T(8,128)S(1)} %add.442.left_ref) | copy-start | bytes 147460
  282.8 26.5 %collective-permute-start.27 = (f32[16,768]{1,0:T(8,128)S(1)}, f32[16,768]{1,0:T(8,128)S(1)}, u32[]{:S(2)}, u32[]{:S(2)}) collective-permute-start(f32[16,768]{1,0:T(8,128)S(1)} %add.442.left_ref), channel_id=1, source_target_pairs={{0,2},{1,3},{2,0},{3,1},{4,6},{5,7},{6,4},{7,5},{8,10},{9,11},{10,... | collective-permute-start | bytes 147464 | tf_op jit(solution)/shard_map/ppermute | solution.py:42
  286.7 24.7 %collective-permute-start.39 = (bf16[48,3072]{1,0:T(8,128)(2,1)S(1)}, bf16[48,3072]{1,0:T(8,128)(2,1)S(1)}, u32[]{:S(2)}, u32[]{:S(2)}) collective-permute-start(bf16[48,3072]{1,0:T(8,128)(2,1)S(1)} %pad_maximum_fusion.10), channel_id=1, source_target_pairs={{0,1},{1,0},{2,3},{3,2},{4,5},{5,4},{6,7},{7,6},{8,9},{9,8},{10,11... | collective-permute-start | bytes 884744 | tf_op jit(solution)/shard_map/ppermute | solution.py:42
  309.3 6.6 %collective-permute-start.20 = (bf16[4,96,1152]{2,1,0:T(8,128)(2,1)}, bf16[4,96,1152]{2,1,0:T(8,128)(2,1)}, u32[]{:S(2)}, u32[]{:S(2)}) collective-permute-start(bf16[4,96,1152]{2,1,0:T(8,128)(2,1)} %dynamic-slice_bitcast_fusion.2), channel_id=1, source_target_pairs={{0,4},{4,0},{8,12},{12,8},{16,20},{20,16},{24,28},{28,24},{1,5},{5... | collective-permute-start | bytes 2654216 | tf_op jit(solution)/shard_map/ppermute | solution.py:38
  313.5 2.3 copy-start.10
  313.5 7.6 %collective-permute-start.28 = (bf16[96,1920]{1,0:T(8,128)(2,1)S(1)}, bf16[96,1920]{1,0:T(8,128)(2,1)S(1)}, u32[]{:S(2)}, u32[]{:S(2)}) collective-permute-start(bf16[96,1920]{1,0:T(8,128)(2,1)S(1)} %fusion.15), channel_id=1, source_target_pairs={{0,8},{4,20},{8,0},{12,28},{16,24},{20,4},{24,16},{28,12},{1,9},{5... | collective-permute-start | bytes 1105928 | tf_op jit(solution)/shard_map/ppermute | solution.py:38
  314.8 6.4 %copy-start.19 = (bf16[2,96,1920]{2,1,0:T(8,128)(2,1)S(1)}, bf16[2,96,1920]{2,1,0:T(8,128)(2,1)}, u32[]{:S(2)}) copy-start(bf16[2,96,1920]{2,1,0:T(8,128)(2,1)} %copy-done.18) | copy-start | bytes 2211844
  322.3 6.3 %collective-permute-start.29 = (bf16[48,1920]{1,0:T(8,128)(2,1)S(1)}, bf16[48,1920]{1,0:T(8,128)(2,1)S(1)}, u32[]{:S(2)}, u32[]{:S(2)}) collective-permute-start(bf16[48,1920]{1,0:T(8,128)(2,1)S(1)} %dynamic-slice_bitcast_fusion.4), channel_id=1, source_target_pairs={{0,1},{1,0},{2,3},{3,2},{4,5},{5,4},{6,7},{7,6},{8,9},{9,8},{10,11... | collective-permute-start | bytes 552968 | tf_op jit(solution)/shard_map/ppermute | solution.py:42
  322.5 20.8 %collective-permute-start.33 = (bf16[2,96,1152]{2,1,0:T(8,128)(2,1)S(1)}, bf16[2,96,1152]{2,1,0:T(8,128)(2,1)S(1)}, u32[]{:S(2)}, u32[]{:S(2)}) collective-permute-start(bf16[2,96,1152]{2,1,0:T(8,128)(2,1)S(1)} %pad_maximum_fusion.9), channel_id=1, source_target_pairs={{0,16},{4,12},{8,24},{12,4},{16,0},{20,28},{24,8},{28,20},{1,17},{... | collective-permute-start | bytes 1327112 | tf_op jit(solution)/shard_map/ppermute | solution.py:38
  328.7 12.4 %collective-permute-start.30 = (bf16[24,1920]{1,0:T(8,128)(2,1)S(1)}, bf16[24,1920]{1,0:T(8,128)(2,1)S(1)}, u32[]{:S(2)}, u32[]{:S(2)}) collective-permute-start(bf16[24,1920]{1,0:T(8,128)(2,1)S(1)} %fusion.32), channel_id=1, source_target_pairs={{0,2},{1,3},{2,0},{3,1},{4,6},{5,7},{6,4},{7,5},{8,10},{9,11},{10,... | collective-permute-start | bytes 276488 | tf_op jit(solution)/shard_map/ppermute | solution.py:42
  341.1 5.5 %collective-permute-start.31 = (bf16[24,1920]{1,0:T(8,128)(2,1)S(1)}, bf16[24,1920]{1,0:T(8,128)(2,1)S(1)}, u32[]{:S(2)}, u32[]{:S(2)}) collective-permute-start(bf16[24,1920]{1,0:T(8,128)(2,1)S(1)} %fusion.29), channel_id=1, source_target_pairs={{0,2},{1,3},{2,0},{3,1},{4,6},{5,7},{6,4},{7,5},{8,10},{9,11},{10,... | collective-permute-start | bytes 276488 | tf_op jit(solution)/shard_map/ppermute | solution.py:42
  344.3 6.0 %collective-permute-start.34 = (bf16[96,1152]{1,0:T(8,128)(2,1)S(1)}, bf16[96,1152]{1,0:T(8,128)(2,1)S(1)}, u32[]{:S(2)}, u32[]{:S(2)}) collective-permute-start(bf16[96,1152]{1,0:T(8,128)(2,1)S(1)} %fusion.18), channel_id=1, source_target_pairs={{0,8},{4,20},{8,0},{12,28},{16,24},{20,4},{24,16},{28,12},{1,9},{5... | collective-permute-start | bytes 663560 | tf_op jit(solution)/shard_map/ppermute | solution.py:38
  346.6 6.8 %collective-permute-start.32 = (bf16[48,1920]{1,0:T(8,128)(2,1)S(1)}, bf16[48,1920]{1,0:T(8,128)(2,1)S(1)}, u32[]{:S(2)}, u32[]{:S(2)}) collective-permute-start(bf16[48,1920]{1,0:T(8,128)(2,1)S(1)} %pad_maximum_fusion.11), channel_id=1, source_target_pairs={{0,1},{1,0},{2,3},{3,2},{4,5},{5,4},{6,7},{7,6},{8,9},{9,8},{10,11... | collective-permute-start | bytes 552968 | tf_op jit(solution)/shard_map/ppermute | solution.py:42
  351.4 6.0 %collective-permute-start.35 = (bf16[96,1152]{1,0:T(8,128)(2,1)S(1)}, bf16[96,1152]{1,0:T(8,128)(2,1)S(1)}, u32[]{:S(2)}, u32[]{:S(2)}) collective-permute-start(bf16[96,1152]{1,0:T(8,128)(2,1)S(1)} %fusion.20), channel_id=1, source_target_pairs={{0,1},{1,0},{2,3},{3,2},{4,5},{5,4},{6,7},{7,6},{8,9},{9,8},{10,11... | collective-permute-start | bytes 663560 | tf_op jit(solution)/shard_map/ppermute | solution.py:42
  357.5 10.4 %collective-permute-start.36 = (bf16[96,1152]{1,0:T(8,128)(2,1)S(1)}, bf16[96,1152]{1,0:T(8,128)(2,1)S(1)}, u32[]{:S(2)}, u32[]{:S(2)}) collective-permute-start(bf16[96,1152]{1,0:T(8,128)(2,1)S(1)} %fusion.23), channel_id=1, source_target_pairs={{0,2},{1,3},{2,0},{3,1},{4,6},{5,7},{6,4},{7,5},{8,10},{9,11},{10,... | collective-permute-start | bytes 663560 | tf_op jit(solution)/shard_map/ppermute | solution.py:42
  (8 other events, 8.3 us)

commit v3 on v2

--- a/solution.py
+++ b/solution.py
@@ -141,10 +141,12 @@
 
 
 class Grad:
-    def __init__(self, slabs, fsdp, dp, short=False):
+    def __init__(self, slabs, fsdp, dp, short=False, scattered=False):
         self.dp, self.short = dp, short
-        self.sum = self.scatter = None
-        if fsdp == 8:
+        self.sum = self.scatter = self.more = None
+        if scattered:
+            self.enter(slabs)
+        elif fsdp == 8:
             self.scatter = Scatter(slabs)
         else:
             self.enter(lax.psum_scatter(slabs, "fsdp", scatter_dimension=0, tiled=True)[0])
@@ -171,8 +173,17 @@
         stage.take(send(given, stage.pairs()))
         if len(stage.got) == 3:
             self.scatter = None
-            self.enter(stage.result())
+            value = stage.result()
+            self.enter(value if self.more is None else jnp.concatenate([value, self.more], axis=1))
         return given
+
+    def hold(self, *behind):
+        stage = self.scatter if self.scatter is not None else self.sum
+        if stage.got:
+            stage.got[-1] = after(stage.got[-1], *behind)
+        else:
+            stage.value = after(stage.value, *behind)
+            stage.split()
 
     def result(self):
         while self.step() is not None:
@@ -186,6 +197,7 @@
         self.shard = shard
 
     def whole(self):
+        self.fsdp = 1
         self.arrays = [lax.all_gather(self.shard, "fsdp", axis=0, tiled=True)]
         return self
 
@@ -219,8 +231,8 @@
         self.gathered, self.first, self.columns, self.deep = gathered, first, columns, deep
         self.arrays = gathered.arrays
         self.rows = gathered.shard.shape[0] - spare
-        self.shape = (self.rows * deep * gathered.fsdp, columns)
-        self.count = deep * gathered.fsdp if gathered.fsdp == 8 else 1
+        self.shape = (self.rows * deep * 8 if gathered.fsdp == 8 else self.arrays[0].shape[0], columns)
+        self.count = deep * 8 if gathered.fsdp == 8 else 1
 
     def copies(self, me, refs, scratch, sems):
         if self.gathered.fsdp != 8:
@@ -838,8 +850,6 @@
         vectors = jnp.concatenate([jnp.stack(pack[:8]), pack[8].reshape(-1, width)], axis=0).astype(F32)
         vectors = jnp.pad(vectors, ((0, 16 - vectors.shape[0]), (0, 0)))
     outer = jnp.concatenate([output_weight, up_weight], axis=1)
-    deep = own_up // own if eight else 1
-    lower = jnp.concatenate([down_weight[at * own : (at + 1) * own] for at in range(deep)], axis=1) if eight else down_weight
 
     starts = jnp.sum((crop_ids[None, :] < crop_ids[:, None]).astype(jnp.int32), axis=1)
     crops = jnp.broadcast_to(crop_ids.astype(F32)[:, None], (rows, 128))
@@ -852,67 +862,49 @@
         group.first()
         group.second()
         group.third()
-        outer_group = Gather(after(outer, group.more), fsdp)
-        outer_group.first()
-        source = after(source, outer_group.shard, starts, crops)
+        source = after(source, starts, crops)
     else:
         group.whole()
-        outer_group = Gather(outer, fsdp).whole()
-        lower_group = Gather(lower, fsdp).whole()
+    outer_group = Gather(outer, fsdp).whole()
+    lower_group = Gather(after(down_weight, outer), fsdp).whole()
     joint_full = Weight(group, 0, joint_width, spare=8 if eight else 0)
     joint, hidden_first, vectors = joint_forward(me, source, vectors, joint_full)
-    read = joint
-    if eight:
-        outer_group.two = after(outer_group.two, joint)
-        outer_group.second()
-        read = after(joint, outer_group.two)
-    mixed_a, logs_a = attend(starts, crops, read, 0, near)
-    if eight:
-        lower_group = Gather(after(lower, mixed_a), fsdp)
-        lower_group.first()
-        read = after(joint, lower_group.shard)
-    mixed_b, logs_b = attend(starts, crops, read, near, pairs - near)
-    source = tokens
-    if eight:
-        outer_group.more = after(outer_group.more, mixed_b)
-        outer_group.third()
-        lower_group.two = after(lower_group.two, mixed_b)
-        lower_group.second()
-        source = after(source, lower_group.two)
+    mixed_a, logs_a = attend(starts, crops, joint, 0, near)
+    mixed_b, logs_b = attend(starts, crops, joint, near, pairs - near)
     out_full = Weight(outer_group, 0, width)
     up_full = Weight(outer_group, width, inner)
-    middle, hidden_second, active, slope = up_forward(me, source, mixed_a, mixed_b, vectors, out_full, up_full)
+    middle, hidden_second, active, slope = up_forward(me, tokens, mixed_a, mixed_b, vectors, out_full, up_full)
     grad = cotangent
+    down_full = Weight(lower_group, 0, width)
+
+    start = lambda slabs, short=False, scattered=False: Grad(slabs, fsdp, dp, short, scattered)
+    behind = lambda value, *grads: after(value, *[g for g in grads if g is not None])
+
+    scattered = lambda value: lax.psum_scatter(value, "fsdp", scatter_dimension=0, tiled=True)
+    down_grad = weight_grad(active, grad)
+    grad_up, cotangent_sums, up_sums = slope_back(me, behind(cotangent, down_grad), slope, down_full)
+    down_grad = scattered(down_grad)
+    up_grad = weight_grad(hidden_second, grad_up)
+    grad_middle, grad_low, grad_mixed, sums = middle_back(
+        me, middle, cotangent, behind(grad_up, up_grad), vectors, out_full, up_full
+    )
+    up_grad = scattered(up_grad)
+    down_grad = start(down_grad, scattered=True)
+    grad_a = attend_back(starts, crops, joint, mixed_a, grad_mixed, logs_a, 0, near)
+    low = behind(grad_low, grad_a)
+    out_slabs = jnp.concatenate([weight_grad(mixed_a, low), weight_grad(mixed_b, low)], axis=0).reshape(fsdp, own, width)
+    slabs_a = weight_grad(hidden_first, grad_a).reshape(fsdp, own, -1)
+    mixed_grad = start(jnp.concatenate([out_slabs, slabs_a], axis=2))
     if eight:
-        lower_group.more = after(lower_group.more, middle)
-        lower_group.third()
-        grad = after(grad, lower_group.more)
-    down_full = Weight(lower_group, 0, width, deep)
-
-    start = lambda slabs, short=False: Grad(slabs, fsdp, dp, short)
-    behind = lambda value, *grads: after(value, *[g for g in grads if g is not None])
-
-    down_grad = start(weight_grad(active, grad).reshape(fsdp, own_up, width), True)
-    grad_up, cotangent_sums, up_sums = slope_back(me, behind(cotangent, down_grad.step()), slope, down_full)
-    sent = down_grad.step(grad_up)
-    up_grad = start(weight_grad(behind(hidden_second, sent), grad_up).reshape(fsdp, own, inner))
-    grad_middle, grad_low, grad_mixed, sums = middle_back(
-        me, middle, cotangent, behind(grad_up, up_grad.step()), vectors, out_full, up_full
-    )
-    sent = [down_grad.step(grad_low), up_grad.step(grad_low)]
-    grad_a = attend_back(starts, crops, joint, mixed_a, behind(grad_mixed, *sent), logs_a, 0, near)
-    sent = [down_grad.step(grad_a), up_grad.step(grad_a)]
-    low = behind(grad_low, *sent)
-    out_slabs = jnp.concatenate([weight_grad(mixed_a, low), weight_grad(mixed_b, low)], axis=0).reshape(fsdp, own, width)
-    slabs_a = weight_grad(behind(hidden_first, *sent), grad_a).reshape(fsdp, own, -1)
-    mixed_grad = start(jnp.concatenate([out_slabs, slabs_a], axis=2))
-    sent = mixed_grad.step()
-    grad_b = attend_back(starts, crops, joint, mixed_b, behind(grad_mixed, sent), logs_b, near, pairs - near)
-    sent = [down_grad.step(grad_b), up_grad.step(grad_b), mixed_grad.step(grad_b)]
-    last_grad = start(weight_grad(behind(hidden_first, *sent), grad_b).reshape(fsdp, own, -1), True)
+        mixed_grad.more = up_grad
+    sent = [mixed_grad.step(), down_grad.step(grad_a)]
+    grad_b = attend_back(starts, crops, joint, mixed_b, behind(grad_mixed, *sent), logs_b, near, pairs - near)
+    last_slabs = weight_grad(behind(hidden_first, mixed_grad.step(grad_b)), grad_b)
+    last_grad = start(last_slabs.reshape(fsdp, own, -1), True)
+    sent = [last_grad.step(), down_grad.step(last_slabs)]
     input_grad, total = first_back(
         me,
-        behind(tokens, last_grad.step()),
+        behind(tokens, *sent),
         grad_middle,
         grad_a,
         grad_b,
@@ -922,13 +914,20 @@
         up_sums,
         joint_full,
     )
-    sent = [last_grad.step(total), mixed_grad.step(total), up_grad.step(total)]
+    sent = [last_grad.step(total), mixed_grad.step(total), down_grad.step(total)]
     if eight and dp == 4:
-        other = send(total, CORE)
+        total = behind(total, *sent)
+        total = total + send(total, CORE)
+        sent = [down_grad.step(total), last_grad.step(total)]
+        total = behind(total, *sent)
+        total = total + send(total, FIRST)
+        sent = [mixed_grad.step(total)]
+        total = behind(total, *sent)
+        total = total + send(total, SECOND)
+        sent = [last_grad.step(total)]
         acts = down_forward(me, behind(middle, *sent), active, vectors, down_full)
-        total = total + other
-        for bit in (2, 4):
-            total = total + send(total, [(i, i ^ bit) for i in range(8)])
+        sent = [mixed_grad.step(acts)]
+        total = behind(total, *sent)
         total = total + send_dp(total, 1)
         vecs = own_rows(me, total, send_dp(total, 2))
     else:
@@ -939,6 +938,11 @@
         vecs = vecs[:2] + [jnp.stack(vecs[2:4])] + vecs[4:]
     last = last_grad.result()
     mixed_out = mixed_grad.result()
+    down_grad = down_grad.result()
+    if eight:
+        mixed_out, up_grad = mixed_out[:, : -up_grad.shape[1]], mixed_out[:, -up_grad.shape[1] :]
+    else:
+        up_grad = lax.psum(up_grad, "dp").astype(F32)
     wide_grads = [mixed_out[:, width:], last]
     grad_joint = jnp.concatenate(
         [
@@ -961,9 +965,9 @@
         out_b,
         gain_b,
         shift_b,
-        up_grad.result(),
+        up_grad,
         up_b,
-        down_grad.result(),
+        down_grad,
         down_b,
     )
 

time: 370 us -> 323 us (0.87)
  waiting for transfers between devices: 97.1 us -> 73 us
  other arithmetic: 37.3 us -> 19.4 us
  starting transfers between devices: 51.6 us -> 37.6 us
  between operations: 1.43 us -> 14.6 us
  local copies, waits for them, and re-layouts: 17.2 us -> 10.2 us
    ppermute x27 -> x13, starting transfers between devices: 31.1 us -> 14.3 us  [send(): return lax.ppermute(value, 'fsdp', pairs)]
    ppermute x27 -> x13, waiting for transfers between devices: 52.4 us -> 35.9 us  [send(): return lax.ppermute(value, 'fsdp', pairs)]
    ppermute x14 -> x12, waiting for transfers between devices: 44.7 us -> 36.4 us  [send_dp(): return lax.ppermute(value, 'dp', [(i, i ^ bit) for i in range(4)])]
    unnamed x70 -> x79, local copies, waits for them, and re-layouts: 9.72 us -> 6.9 us
    ppermute x14 -> x12, starting transfers between devices: 20.4 us -> 23 us  [send_dp(): return lax.ppermute(value, 'dp', [(i, i ^ bit) for i in range(4)])]
  transfers between devices with their start and end apart: 41 -> 29, of which waited for: 18 -> 15; matrix products, arithmetic and copies ran while one was open for 11% -> 14% of each run, Pallas kernels for 36% -> 44%
where the time goes in v3:
time: 323 us
  Pallas kernels  141 us (44%)
  waiting for transfers between devices  73 us (23%)
  starting transfers between devices  37.6 us (12%)
  matrix products  26.2 us (8%)
  other arithmetic  19.4 us (6%)
  between operations  14.6 us (5%)
  local copies, waits for them, and re-layouts  10.2 us (3%)
    ppermute x12, waiting for transfers between devices, send_dp(): return lax.ppermute(value, 'dp', [(i, i ^ bit) for i in range(4)])  36.4 us
    ppermute x13, waiting for transfers between devices, send(): return lax.ppermute(value, 'fsdp', pairs)  35.9 us
    pallas_call x2, Pallas kernels, attend(): pl.pallas_call(functools.partial(attend_kernel, rows), grid_spec=pltpu.Pr...  30.7 us
    pallas_call x2, Pallas kernels, attend_back(): pl.pallas_call(functools.partial(attend_back_kernel, rows), grid_spec=plt...  29.9 us
    dot_general x6, matrix products, weight_grad(): lax.dot_general(left, right, (((0,), (0,)), ((), ())), preferred_element_...  26.2 us
    ppermute x12, starting transfers between devices, send_dp(): return lax.ppermute(value, 'dp', [(i, i ^ bit) for i in range(4)])  23 us
    pallas_call x1, Pallas kernels, up_forward(): pl.pallas_call(functools.partial(up_kernel, out_weight, up_weight), grid_...  18.8 us
    pallas_call x1, Pallas kernels, middle_back(): pl.pallas_call(functools.partial(middle_kernel, out_weight, up_weight), g...  16 us
  transfers between devices with their start and end apart: 29, of which 15 were waited for; matrix products, arithmetic and copies ran while one was open for 14% of the time, Pallas kernels for 44%

profile of v3, /device:TPU:0, one launch (start us, length us, event | category | flops | bytes accessed | tf_op | source)
XLA Modules:
  0.0 322.5 jit_solution(14580786294226769460)
XLA Ops:
  7.3 1.0 constant_dynamic-update-slice_fusion.1
  8.4 1.1 constant_dynamic-update-slice_fusion
  9.5 0.9 copy-done.8
  11.3 3.0 collective-permute-start
  14.4 6.6 %collective-permute-done = bf16[104,2304]{1,0:T(8,128)(2,1)S(1)} collective-permute-done((bf16[104,2304]{1,0:T(8,128)(2,1)S(1)}, bf16[104,2304]{1,0:T(8,128)(2,1)S(1)}, u32[]{:S(2)}, u32[]{:S(2)}) %collective-permute-start) | collective-permute-done | bytes 479264 | tf_op jit(solution)/shard_map/ppermute | solution.py:38
  21.2 2.1 collective-permute-start.1
  23.3 18.8 %collective-permute-done.1.refs_1_ = bf16[2,104,2304]{2,1,0:T(8,128)(2,1)S(1)} collective-permute-done((bf16[2,104,2304]{2,1,0:T(8,128)(2,1)S(1)}, bf16[2,104,2304]{2,1,0:T(8,128)(2,1)S(1)}, u32[]{:S(2)}, u32[]{:S(2)}) %collective-permute-start.1) | collective-permute-done | bytes 958496 | tf_op jit(solution)/shard_map/ppermute | solution.py:38
  42.1 1.2 convert_reduce_fusion.starts_ref
  43.4 1.0 broadcast_in_dim.29.crops_ref
  45.4 9.5 %joint_forward.1 = (bf16[1024,2304]{1,0:T(8,128)(2,1)}, bf16[1024,768]{1,0:T(8,128)(2,1)}, f32[16,768]{1,0:T(8,128)}) custom-call(s32[1]{0:T(128)} %bitcast.me_ref, bf16[1024,768]{1,0:T(8,128)(2,1)} %x_ref.3, bf16[2,104,2304]{2,1,0:T(8,128)(2,1)} %copy-done.1, bf16[2,104,2304]{2,1,0:T(8,128)(2,1)} %copy-done.9, bf16[2,104,2304]{2,1,0:T(8,128)(2,1)} %copy-done.10, ...), custom_call_target="tpu_custom_call" | custom-call | flops 3623878656 | bytes 11403264 | tf_op jit(solution)/shard_map/joint_forward/pallas_call | solution.py:356
  54.9 15.4 %attend.3 = (bf16[1024,384]{1,0:T(8,128)(2,1)}, f32[3,10,8,256]{3,2,1,0:T(8,128)}) custom-call(s32[1024]{0:T(1024)} %convert_reduce_fusion.starts_ref, f32[1024,128]{1,0:T(8,128)} %broadcast_in_dim.29.crops_ref, bf16[1024,2304]{1,0:T(8,128)(2,1)} %get-tuple-element.67.query_ref.key_ref.value_ref, ...), custom_call_target="tpu_custom_call" | custom-call | flops 2415919104 | bytes 3145728 | tf_op jit(solution)/shard_map/attend/pallas_call | solution.py:439
  70.3 15.3 %attend.2 = (bf16[1024,384]{1,0:T(8,128)(2,1)}, f32[3,10,8,256]{3,2,1,0:T(8,128)}) custom-call(s32[1024]{0:T(1024)} %convert_reduce_fusion.starts_ref, f32[1024,128]{1,0:T(8,128)} %broadcast_in_dim.29.crops_ref, bf16[1024,2304]{1,0:T(8,128)(2,1)} %get-tuple-element.67.query_ref.key_ref.value_ref, ...), custom_call_target="tpu_custom_call" | custom-call | flops 2415919104 | bytes 3145728 | tf_op jit(solution)/shard_map/attend/pallas_call | solution.py:439
  85.6 18.8 %up_forward.1 = (f32[1024,768]{1,0:T(8,128)}, bf16[1024,768]{1,0:T(8,128)(2,1)}, bf16[1024,3072]{1,0:T(8,128)(2,1)}, bf16[1024,3072]{1,0:T(8,128)(2,1)}) custom-call(s32[1]{0:T(128)} %bitcast.me_ref, bf16[1024,768]{1,0:T(8,128)(2,1)} %x_ref.3, bf16[1024,384]{1,0:T(8,128)(2,1)} %get-tuple-element.68.mixed_a_ref.mixed_ref, ...), custom_call_target="tpu_custom_call" | custom-call | flops 6039797760 | bytes 25165824 | tf_op jit(solution)/shard_map/up_forward/pallas_call | solution.py:566
  104.4 9.8 %convolution_convert_fusion.1 = bf16[3072,768]{1,0:T(8,128)(2,1)} fusion(bf16[1024,3072]{1,0:T(8,128)(2,1)} %get-tuple-element.73.active_ref, bf16[1024,768]{1,0:T(8,128)(2,1)S(1)} %copy-done.31), kind=kOutput, calls=%fused_computation.6 | convolution fusion | flops 4834197504 | bytes 12582912 | tf_op jit(solution)/shard_map/dot_general | solution.py:808
  114.5 12.3 %slope_back.1 = (bf16[1024,3072]{1,0:T(8,128)(2,1)}, f32[8,768]{1,0:T(8,128)}, f32[8,3072]{1,0:T(8,128)}) custom-call(s32[1]{0:T(128)} %bitcast.me_ref, bf16[1024,768]{1,0:T(8,128)(2,1)} %grad_ref.2, bf16[1024,3072]{1,0:T(8,128)(2,1)} %get-tuple-element.75.slope_ref, bf16[3072,768]{1,0:T(8,128)(2,1)} %all-gather.5.cloned.1.call-done.refs_0_), custom_call_target="tpu_custom_call" | custom-call | flops 4831838208 | bytes 18874368 | tf_op jit(solution)/shard_map/slope_back/pallas_call | solution.py:610
  126.9 10.3 %convolution_convert_fusion = bf16[768,3072]{1,0:T(8,128)(2,1)} fusion(bf16[1024,768]{1,0:T(8,128)(2,1)S(1)} %copy-done.32, bf16[1024,3072]{1,0:T(8,128)(2,1)} %get-tuple-element.79.ga_ref), kind=kOutput, calls=%fused_computation.5 | convolution fusion | flops 4834197504 | bytes 12582912 | tf_op jit(solution)/shard_map/dot_general | solution.py:808
  137.2 16.0 %middle_back.1 = (f32[1024,768]{1,0:T(8,128)}, bf16[1024,768]{1,0:T(8,128)(2,1)}, bf16[1024,768]{1,0:T(8,128)(2,1)}, f32[3,8,768]{2,1,0:T(8,128)}) custom-call(s32[1]{0:T(128)} %bitcast.me_ref, f32[1024,768]{1,0:T(8,128)} %get-tuple-element.106.middle_ref, bf16[1024,768]{1,0:T(8,128)(2,1)} %grad_ref.2, bf16[1024,3072]{1,0:T(8,128)(2,1)} %get-tuple-element.79.ga_ref, ...), custom_call_target="tpu_custom_call" | custom-call | flops 6039797760 | bytes 22020096 | tf_op jit(solution)/shard_map/middle_back/pallas_call | solution.py:654
  153.2 14.9 %attend_back.2.part_a_ref = bf16[1024,1152]{1,0:T(8,128)(2,1)} custom-call(s32[1024]{0:T(1024)} %convert_reduce_fusion.starts_ref, f32[1024,128]{1,0:T(8,128)} %broadcast_in_dim.29.crops_ref, bf16[1024,2304]{1,0:T(8,128)(2,1)} %get-tuple-element.67.query_ref.key_ref.value_ref, bf16[1024,2304]{1,0:T(8,128)(2,1)} %get-tuple-element.67.query_ref.key_ref.value_ref, ...), custom_call_target="tpu_custom_call" | custom-call | flops 6039797760 | bytes 6291456 | tf_op jit(solution)/shard_map/attend_back/pallas_call | solution.py:518
  168.1 0.8 convolution_convert_fusion.5
  169.3 0.8 convolution_convert_fusion.4
  170.7 1.2 copy-done.2
  171.9 2.3 convolution_convert_fusion.3
  174.2 1.2 fusion.1
  176.0 1.0 dynamic-slice_bitcast_fusion.2
  177.0 9.0 %collective-permute-start.6 = (bf16[192,768]{1,0:T(8,128)(2,1)S(1)}, bf16[192,768]{1,0:T(8,128)(2,1)S(1)}, u32[]{:S(2)}, u32[]{:S(2)}) collective-permute-start(bf16[192,768]{1,0:T(8,128)(2,1)S(1)} %dynamic-slice_bitcast_fusion.2), channel_id=1, source_target_pairs={{0,1},{1,0},{2,3},{3,2},{4,5},{5,4},{6,7},{7,6},{8,9},{9,8},{10,11... | collective-permute-start | bytes 884744 | tf_op jit(solution)/shard_map/ppermute | solution.py:42
  186.0 15.0 %attend_back.3.part_b_ref = bf16[1024,1152]{1,0:T(8,128)(2,1)} custom-call(s32[1024]{0:T(1024)} %convert_reduce_fusion.starts_ref, f32[1024,128]{1,0:T(8,128)} %broadcast_in_dim.29.crops_ref, bf16[1024,2304]{1,0:T(8,128)(2,1)} %get-tuple-element.67.query_ref.key_ref.value_ref, bf16[1024,2304]{1,0:T(8,128)(2,1)} %get-tuple-element.67.query_ref.key_ref.value_ref, ...), custom_call_target="tpu_custom_call" | custom-call | flops 6039797760 | bytes 6291456 | tf_op jit(solution)/shard_map/attend_back/pallas_call | solution.py:518
  201.1 1.4 fusion.6
  202.5 0.9 pad_maximum_fusion.3
  203.5 2.3 convolution_convert_fusion.2
  205.9 2.0 collective-permute-start.5
  208.0 4.1 %collective-permute-start.9 = (bf16[96,768]{1,0:T(8,128)(2,1)S(1)}, bf16[96,768]{1,0:T(8,128)(2,1)S(1)}, u32[]{:S(2)}, u32[]{:S(2)}) collective-permute-start(bf16[96,768]{1,0:T(8,128)(2,1)S(1)} %fusion.21), channel_id=1, source_target_pairs={{0,2},{1,3},{2,0},{3,1},{4,6},{5,7},{6,4},{7,5},{8,10},{9,11},{10,... | collective-permute-start | bytes 442376 | tf_op jit(solution)/shard_map/ppermute | solution.py:42
  212.1 11.3 %first_back.1 = (f32[1024,768]{1,0:T(8,128)}, f32[16,768]{1,0:T(8,128)}) custom-call(s32[1]{0:T(128)} %bitcast.me_ref, bf16[1024,768]{1,0:T(8,128)(2,1)} %x_ref.3, f32[1024,768]{1,0:T(8,128)} %get-tuple-element.91.gmid_ref, bf16[1024,1152]{1,0:T(8,128)(2,1)} %attend_back.2.part_a_ref, bf16[1024,1152]{1,0:T(8,128)(2,1)} %attend_back.3.part_b_ref, ...), custom_call_target="tpu_custom_call" | custom-call | flops 3623878656 | bytes 16121856 | tf_op jit(solution)/shard_map/first_back/pallas_call | solution.py:755
  223.5 2.0 fusion.4
  225.5 1.5 fusion.13
  227.0 0.8 pad_maximum_fusion.6
  227.8 2.9 collective-permute-start.14
  230.7 1.5 collective-permute-done.12
  232.3 0.8 pad_maximum_fusion.7
  233.0 8.3 %collective-permute-done.14 = bf16[96,1920]{1,0:T(8,128)(2,1)} collective-permute-done((bf16[96,1920]{1,0:T(8,128)(2,1)}, bf16[96,1920]{1,0:T(8,128)(2,1)}, u32[]{:S(2)}, u32[]{:S(2)}) %collective-permute-start.14) | collective-permute-done | bytes 368672 | tf_op jit(solution)/shard_map/ppermute | solution.py:38
  241.4 1.4 fusion.3
  242.8 0.8 copy-done.15
  243.6 1.8 fusion.9
  245.4 1.1 collective-permute-start.13
  246.5 1.1 pad_maximum_fusion.2
  247.6 1.0 collective-permute-start.11
  248.6 0.9 collective-permute-done.13
  249.5 1.6 collective-permute-start.15
  251.1 1.5 collective-permute-start.24
  253.8 1.2 fusion.11
  255.0 11.4 %down_forward.1 = f32[1024,768]{1,0:T(8,128)} custom-call(s32[1]{0:T(128)} %bitcast.me_ref, f32[1024,768]{1,0:T(8,128)} %get-tuple-element.106.middle_ref, bf16[1024,3072]{1,0:T(8,128)(2,1)} %get-tuple-element.73.active_ref, f32[16,768]{1,0:T(8,128)} %get-tuple-element.70.vec_ref, bf16[3072,768]{1,0:T(8,128)(2,1)} %all-gather.5.cloned.1.call-done.refs_0_), custom_call_target="tpu_custom_call" | custom-call | flops 4831838208 | bytes 17301504 | tf_op jit(solution)/shard_map/down_forward/pallas_call | solution.py:686
  266.4 2.4 collective-permute-done.16
  268.9 2.5 collective-permute-start.19
  271.6 1.8 collective-permute-start.17
  273.3 1.1 maximum_convert_fusion
  274.7 3.6 %collective-permute-done.17 = f32[16,768]{1,0:T(8,128)S(1)} collective-permute-done((f32[16,768]{1,0:T(8,128)S(1)}, f32[16,768]{1,0:T(8,128)S(1)}, u32[]{:S(2)}, u32[]{:S(2)}) %collective-permute-start.17) | collective-permute-done | bytes 49184 | tf_op jit(solution)/shard_map/ppermute | solution.py:42
  278.3 3.0 collective-permute-start.18
  281.7 5.1 %collective-permute-done.22 = bf16[96,1152]{1,0:T(8,128)(2,1)S(1)} collective-permute-done((bf16[96,1152]{1,0:T(8,128)(2,1)S(1)}, bf16[96,1152]{1,0:T(8,128)(2,1)S(1)}, u32[]{:S(2)}, u32[]{:S(2)}) %collective-permute-start.22) | collective-permute-done | bytes 221216 | tf_op jit(solution)/shard_map/ppermute | solution.py:42
  287.5 1.5 own_rows.1
  289.0 11.2 %collective-permute-done.20 = bf16[24,4992]{1,0:T(8,128)(2,1)S(1)} collective-permute-done((bf16[24,4992]{1,0:T(8,128)(2,1)S(1)}, bf16[24,4992]{1,0:T(8,128)(2,1)S(1)}, u32[]{:S(2)}, u32[]{:S(2)}) %collective-permute-start.20) | collective-permute-done | bytes 239648 | tf_op jit(solution)/shard_map/ppermute | solution.py:42
  300.4 2.2 collective-permute-done.23
  302.7 10.1 %collective-permute-done.21 = bf16[48,4992]{1,0:T(8,128)(2,1)S(1)} collective-permute-done((bf16[48,4992]{1,0:T(8,128)(2,1)S(1)}, bf16[48,4992]{1,0:T(8,128)(2,1)S(1)}, u32[]{:S(2)}, u32[]{:S(2)}) %collective-permute-start.21) | collective-permute-done | bytes 479264 | tf_op jit(solution)/shard_map/ppermute | solution.py:42
  313.0 0.7 maximum_convert_fusion.1
  313.7 1.1 fusion.7
  315.1 0.9 copy-done.22
  (148 shorter events, 7.6 us)
Async XLA Ops:
  7.2 4.0 %copy-start.30 = (bf16[384]{0:T(512)(128)(2,1)S(1)}, bf16[384]{0:T(512)(128)(2,1)}, u32[]{:S(2)}) copy-start(bf16[384]{0:T(512)(128)(2,1)} %param.26) | copy-start | bytes 2308
  7.2 4.0 %copy-start.29 = (bf16[2,96]{1,0:T(2,128)(2,1)S(1)}, bf16[2,96]{1,0:T(2,128)(2,1)}, u32[]{:S(2)}) copy-start(bf16[2,96]{1,0:T(2,128)(2,1)} %param.20) | copy-start | bytes 1156
  7.2 4.0 %copy-start.5 = (bf16[96,2304]{1,0:T(8,128)(2,1)S(1)}, bf16[96,2304]{1,0:T(8,128)(2,1)}, u32[]{:S(2)}) copy-start(bf16[96,2304]{1,0:T(8,128)(2,1)} %param.19) | copy-start | bytes 1327108
  7.2 4.0 %copy-start.23 = (bf16[96]{0:T(256)(128)(2,1)S(1)}, bf16[96]{0:T(256)(128)(2,1)}, u32[]{:S(2)}) copy-start(bf16[96]{0:T(256)(128)(2,1)} %param.28) | copy-start | bytes 580
  7.2 4.0 %copy-start.24 = (bf16[96]{0:T(256)(128)(2,1)S(1)}, bf16[96]{0:T(256)(128)(2,1)}, u32[]{:S(2)}) copy-start(bf16[96]{0:T(256)(128)(2,1)} %param.24) | copy-start | bytes 580
  7.2 4.0 %copy-start.25 = (bf16[96]{0:T(256)(128)(2,1)S(1)}, bf16[96]{0:T(256)(128)(2,1)}, u32[]{:S(2)}) copy-start(bf16[96]{0:T(256)(128)(2,1)} %param.23) | copy-start | bytes 580
  7.2 4.0 %copy-start.26 = (bf16[96]{0:T(256)(128)(2,1)S(1)}, bf16[96]{0:T(256)(128)(2,1)}, u32[]{:S(2)}) copy-start(bf16[96]{0:T(256)(128)(2,1)} %param.22) | copy-start | bytes 580
  7.3 4.0 %copy-start.27 = (bf16[96]{0:T(256)(128)(2,1)S(1)}, bf16[96]{0:T(256)(128)(2,1)}, u32[]{:S(2)}) copy-start(bf16[96]{0:T(256)(128)(2,1)} %param.18) | copy-start | bytes 580
  7.3 4.0 %copy-start.28 = (bf16[96]{0:T(256)(128)(2,1)S(1)}, bf16[96]{0:T(256)(128)(2,1)}, u32[]{:S(2)}) copy-start(bf16[96]{0:T(256)(128)(2,1)} %param.17) | copy-start | bytes 580
  7.3 78.3 %all-gather.3.cloned.1.call-start = ((), (), s32[]{:S(2)}) async-start(), calls=%async_computation.2 | async-start | bytes 6635520 | tf_op jit(solution)/shard_map/all_gather | solution.py:201
  9.5 0.9 copy-start.8
  10.4 104.1 %all-gather.5.cloned.1.call-start = ((), (), s32[]{:S(2)}) async-start(), calls=%async_computation.3 | async-start | bytes 5308416 | tf_op jit(solution)/shard_map/all_gather | solution.py:201
  11.1 164.9 %reduce-scatter.3.cloned.1.call-start = ((), (), s32[]{:S(2)}) async-start(), calls=%async_computation.4 | async-start | bytes 5308416 | tf_op jit(solution)/shard_map/reduce_scatter | solution.py:883
  11.3 30.8 %copy-start.21 = (s32[1024]{0:T(1024)S(1)}, s32[1024]{0:T(1024)}, u32[]{:S(2)}) copy-start(s32[1024]{0:T(1024)} %param.16) | copy-start | bytes 12292
  11.3 9.7 %collective-permute-start = (bf16[104,2304]{1,0:T(8,128)(2,1)S(1)}, bf16[104,2304]{1,0:T(8,128)(2,1)S(1)}, u32[]{:S(2)}, u32[]{:S(2)}) collective-permute-start(bf16[104,2304]{1,0:T(8,128)(2,1)S(1)} %pad_add_fusion), channel_id=1, source_target_pairs={{0,8},{4,20},{8,0},{12,28},{16,24},{20,4},{24,16},{28,12},{1,9},{5... | collective-permute-start | bytes 1437704 | tf_op jit(solution)/shard_map/ppermute | solution.py:38
  21.1 23.7 %copy-start.1 = (bf16[2,104,2304]{2,1,0:T(8,128)(2,1)}, bf16[2,104,2304]{2,1,0:T(8,128)(2,1)S(1)}, u32[]{:S(2)}) copy-start(bf16[2,104,2304]{2,1,0:T(8,128)(2,1)S(1)} %pad_maximum_fusion.1.refs_0_) | copy-start | bytes 2875396
  21.2 21.0 %collective-permute-start.1 = (bf16[2,104,2304]{2,1,0:T(8,128)(2,1)S(1)}, bf16[2,104,2304]{2,1,0:T(8,128)(2,1)S(1)}, u32[]{:S(2)}, u32[]{:S(2)}) collective-permute-start(bf16[2,104,2304]{2,1,0:T(8,128)(2,1)S(1)} %pad_maximum_fusion.1.refs_0_), channel_id=1, source_target_pairs={{0,16},{4,12},{8,24},{12,4},{16,0},{20,28},{24,8},{28,20},{1,17},{... | collective-permute-start | bytes 2875400 | tf_op jit(solution)/shard_map/ppermute | solution.py:38
  23.3 21.1 %collective-permute-start.2 = (bf16[2,104,2304]{2,1,0:T(8,128)(2,1)S(1)}, bf16[2,104,2304]{2,1,0:T(8,128)(2,1)S(1)}, u32[]{:S(2)}, u32[]{:S(2)}) collective-permute-start(bf16[2,104,2304]{2,1,0:T(8,128)(2,1)S(1)} %pad_maximum_fusion.1.refs_0_), channel_id=1, source_target_pairs={{0,4},{4,0},{8,12},{12,8},{16,20},{20,16},{24,28},{28,24},{1,5},{5... | collective-permute-start | bytes 2875400 | tf_op jit(solution)/shard_map/ppermute | solution.py:38
  42.1 2.8 copy-start.9
  42.1 2.8 collective-permute-start.3
  44.4 1.0 copy-start.10
  85.6 18.8 %copy-start.31 = (bf16[1024,768]{1,0:T(8,128)(2,1)S(1)}, bf16[1024,768]{1,0:T(8,128)(2,1)}, u32[]{:S(2)}) copy-start(bf16[1024,768]{1,0:T(8,128)(2,1)} %grad_ref.2) | copy-start | bytes 4718596
  114.2 132.2 %reduce-scatter.5.cloned.1.call-start = ((), (), s32[]{:S(2)}) async-start(), calls=%async_computation.5 | async-start | bytes 5308416 | tf_op jit(solution)/shard_map/reduce_scatter | solution.py:883
  114.5 12.4 %copy-start.32 = (bf16[1024,768]{1,0:T(8,128)(2,1)S(1)}, bf16[1024,768]{1,0:T(8,128)(2,1)}, u32[]{:S(2)}) copy-start(bf16[1024,768]{1,0:T(8,128)(2,1)} %get-tuple-element.78) | copy-start | bytes 4718596
  153.2 15.0 %copy-start = (bf16[1024,768]{1,0:T(8,128)(2,1)S(1)}, bf16[1024,768]{1,0:T(8,128)(2,1)}, u32[]{:S(2)}) copy-start(bf16[1024,768]{1,0:T(8,128)(2,1)} %get-tuple-element.83) | copy-start | bytes 4718596
  153.2 15.0 %copy-start.13 = (bf16[1024,384]{1,0:T(8,128)(2,1)S(1)}, bf16[1024,384]{1,0:T(8,128)(2,1)}, u32[]{:S(2)}) copy-start(bf16[1024,384]{1,0:T(8,128)(2,1)} %get-tuple-element.68.mixed_a_ref.mixed_ref) | copy-start | bytes 2359300
  168.1 1.1 copy-start.12
  169.3 1.4 copy-start.33
  170.1 1.8 copy-start.2
  175.4 25.6 %collective-permute-start.4 = (bf16[4,96,1920]{2,1,0:T(8,128)(2,1)}, bf16[4,96,1920]{2,1,0:T(8,128)(2,1)}, u32[]{:S(2)}, u32[]{:S(2)}) collective-permute-start(bf16[4,96,1920]{2,1,0:T(8,128)(2,1)} %fusion.1), channel_id=1, source_target_pairs={{0,4},{4,0},{8,12},{12,8},{16,20},{20,16},{24,28},{28,24},{1,5},{5... | collective-permute-start | bytes 4423688 | tf_op jit(solution)/shard_map/ppermute | solution.py:38
  177.0 30.9 %collective-permute-start.6 = (bf16[192,768]{1,0:T(8,128)(2,1)S(1)}, bf16[192,768]{1,0:T(8,128)(2,1)S(1)}, u32[]{:S(2)}, u32[]{:S(2)}) collective-permute-start(bf16[192,768]{1,0:T(8,128)(2,1)S(1)} %dynamic-slice_bitcast_fusion.2), channel_id=1, source_target_pairs={{0,1},{1,0},{2,3},{3,2},{4,5},{5,4},{6,7},{7,6},{8,9},{9,8},{10,11... | collective-permute-start | bytes 884744 | tf_op jit(solution)/shard_map/ppermute | solution.py:42
  201.1 2.4 copy-start.3
  201.1 2.4 copy-start.34
  203.5 20.0 %collective-permute-start.8 = (bf16[2,96,1920]{2,1,0:T(8,128)(2,1)}, bf16[2,96,1920]{2,1,0:T(8,128)(2,1)}, u32[]{:S(2)}, u32[]{:S(2)}) collective-permute-start(bf16[2,96,1920]{2,1,0:T(8,128)(2,1)} %pad_maximum_fusion.3), channel_id=1, source_target_pairs={{0,16},{4,12},{8,24},{12,4},{16,0},{20,28},{24,8},{28,20},{1,17},{... | collective-permute-start | bytes 2211848 | tf_op jit(solution)/shard_map/ppermute | solution.py:38
  205.8 2.1 copy-start.4
  205.8 2.1 copy-start.14
  205.9 19.6 %collective-permute-start.5 = (bf16[4,96,1152]{2,1,0:T(8,128)(2,1)S(1)}, bf16[4,96,1152]{2,1,0:T(8,128)(2,1)S(1)}, u32[]{:S(2)}, u32[]{:S(2)}) collective-permute-start(bf16[4,96,1152]{2,1,0:T(8,128)(2,1)S(1)} %dynamic-slice_bitcast_fusion), channel_id=1, source_target_pairs={{0,4},{4,0},{8,12},{12,8},{16,20},{20,16},{24,28},{28,24},{1,5},{5... | collective-permute-start | bytes 2654216 | tf_op jit(solution)/shard_map/ppermute | solution.py:38
  208.0 15.4 %collective-permute-start.9 = (bf16[96,768]{1,0:T(8,128)(2,1)S(1)}, bf16[96,768]{1,0:T(8,128)(2,1)S(1)}, u32[]{:S(2)}, u32[]{:S(2)}) collective-permute-start(bf16[96,768]{1,0:T(8,128)(2,1)S(1)} %fusion.21), channel_id=1, source_target_pairs={{0,2},{1,3},{2,0},{3,1},{4,6},{5,7},{6,4},{7,5},{8,10},{9,11},{10,... | collective-permute-start | bytes 442376 | tf_op jit(solution)/shard_map/ppermute | solution.py:42
  223.4 8.8 %collective-permute-start.12 = (bf16[96,768]{1,0:T(8,128)(2,1)S(1)}, bf16[96,768]{1,0:T(8,128)(2,1)S(1)}, u32[]{:S(2)}, u32[]{:S(2)}) collective-permute-start(bf16[96,768]{1,0:T(8,128)(2,1)S(1)} %fusion.19), channel_id=1, source_target_pairs={{0,2},{1,3},{2,0},{3,1},{4,6},{5,7},{6,4},{7,5},{8,10},{9,11},{10,... | collective-permute-start | bytes 442376 | tf_op jit(solution)/shard_map/ppermute | solution.py:42
  225.5 2.3 copy-start.20
  225.5 2.3 copy-start.11
  227.8 2.9 collective-permute-start.10
  227.8 13.6 %collective-permute-start.14 = (bf16[96,1920]{1,0:T(8,128)(2,1)}, bf16[96,1920]{1,0:T(8,128)(2,1)}, u32[]{:S(2)}, u32[]{:S(2)}) collective-permute-start(bf16[96,1920]{1,0:T(8,128)(2,1)} %fusion.4), channel_id=1, source_target_pairs={{0,8},{4,20},{8,0},{12,28},{16,24},{20,4},{24,16},{28,12},{1,9},{5... | collective-permute-start | bytes 1105928 | tf_op jit(solution)/shard_map/ppermute | solution.py:38
  230.7 12.1 %collective-permute-start.7 = (bf16[2,96,1152]{2,1,0:T(8,128)(2,1)}, bf16[2,96,1152]{2,1,0:T(8,128)(2,1)S(1)}, u32[]{:S(2)}, u32[]{:S(2)}) collective-permute-start(bf16[2,96,1152]{2,1,0:T(8,128)(2,1)} %pad_maximum_fusion.6), channel_id=1, source_target_pairs={{0,16},{4,12},{8,24},{12,4},{16,0},{20,28},{24,8},{28,20},{1,17},{... | collective-permute-start | bytes 1327112 | tf_op jit(solution)/shard_map/ppermute | solution.py:38
  232.3 0.8 copy-start.6
  242.8 8.3 %copy-start.17 = (bf16[192,768]{1,0:T(8,128)(2,1)S(1)}, bf16[192,768]{1,0:T(8,128)(2,1)}, u32[]{:S(2)}) copy-start(bf16[192,768]{1,0:T(8,128)(2,1)} %pad_maximum_fusion.7) | copy-start | bytes 884740
  242.8 0.8 copy-start.15
  245.4 8.5 %copy-start.16 = (bf16[2,96,1152]{2,1,0:T(8,128)(2,1)S(1)}, bf16[2,96,1152]{2,1,0:T(8,128)(2,1)}, u32[]{:S(2)}) copy-start(bf16[2,96,1152]{2,1,0:T(8,128)(2,1)} %copy-done.15) | copy-start | bytes 1327108
  245.4 4.1 %collective-permute-start.13 = (f32[16,768]{1,0:T(8,128)S(1)}, f32[16,768]{1,0:T(8,128)S(1)}, u32[]{:S(2)}, u32[]{:S(2)}) collective-permute-start(f32[16,768]{1,0:T(8,128)S(1)} %add.305), channel_id=1, source_target_pairs={{0,8},{4,20},{8,0},{12,28},{16,24},{20,4},{24,16},{28,12},{1,9},{5... | collective-permute-start | bytes 147464 | tf_op jit(solution)/shard_map/ppermute | solution.py:38
  247.6 6.2 %collective-permute-start.11 = (bf16[96,1152]{1,0:T(8,128)(2,1)}, bf16[96,1152]{1,0:T(8,128)(2,1)S(1)}, u32[]{:S(2)}, u32[]{:S(2)}) collective-permute-start(bf16[96,1152]{1,0:T(8,128)(2,1)} %fusion.9), channel_id=1, source_target_pairs={{0,8},{4,20},{8,0},{12,28},{16,24},{20,4},{24,16},{28,12},{1,9},{5... | collective-permute-start | bytes 663560 | tf_op jit(solution)/shard_map/ppermute | solution.py:38
  249.5 4.2 %collective-permute-start.15 = (f32[16,768]{1,0:T(8,128)S(1)}, f32[16,768]{1,0:T(8,128)S(1)}, u32[]{:S(2)}, u32[]{:S(2)}) collective-permute-start(f32[16,768]{1,0:T(8,128)S(1)} %add.311), channel_id=1, source_target_pairs={{0,16},{4,12},{8,24},{12,4},{16,0},{20,28},{24,8},{28,20},{1,17},{... | collective-permute-start | bytes 147464 | tf_op jit(solution)/shard_map/ppermute | solution.py:38
  251.1 20.4 %collective-permute-start.24 = (bf16[192,768]{1,0:T(8,128)(2,1)S(1)}, bf16[192,768]{1,0:T(8,128)(2,1)S(1)}, u32[]{:S(2)}, u32[]{:S(2)}) collective-permute-start(bf16[192,768]{1,0:T(8,128)(2,1)S(1)} %copy-done.17), channel_id=1, source_target_pairs={{0,1},{1,0},{2,3},{3,2},{4,5},{5,4},{6,7},{7,6},{8,9},{9,8},{10,11... | collective-permute-start | bytes 884744 | tf_op jit(solution)/shard_map/ppermute | solution.py:42
  252.6 16.1 %collective-permute-start.16 = (bf16[48,4992]{1,0:T(8,128)(2,1)S(1)}, bf16[48,4992]{1,0:T(8,128)(2,1)S(1)}, u32[]{:S(2)}, u32[]{:S(2)}) collective-permute-start(bf16[48,4992]{1,0:T(8,128)(2,1)S(1)} %dynamic-slice_bitcast_fusion.1), channel_id=1, source_target_pairs={{0,1},{1,0},{2,3},{3,2},{4,5},{5,4},{6,7},{7,6},{8,9},{9,8},{10,11... | collective-permute-start | bytes 1437704 | tf_op jit(solution)/shard_map/ppermute | solution.py:42
  266.4 5.0 %copy-start.7 = (bf16[96,768]{1,0:T(8,128)(2,1)S(1)}, bf16[96,768]{1,0:T(8,128)(2,1)}, u32[]{:S(2)}) copy-start(bf16[96,768]{1,0:T(8,128)(2,1)} %copy-done.6) | copy-start | bytes 442372
  268.9 12.6 %collective-permute-start.19 = (bf16[24,4992]{1,0:T(8,128)(2,1)S(1)}, bf16[24,4992]{1,0:T(8,128)(2,1)S(1)}, u32[]{:S(2)}, u32[]{:S(2)}) collective-permute-start(bf16[24,4992]{1,0:T(8,128)(2,1)S(1)} %fusion.20), channel_id=1, source_target_pairs={{0,2},{1,3},{2,0},{3,1},{4,6},{5,7},{6,4},{7,5},{8,10},{9,11},{10,... | collective-permute-start | bytes 718856 | tf_op jit(solution)/shard_map/ppermute | solution.py:42
  271.6 6.8 %collective-permute-start.17 = (f32[16,768]{1,0:T(8,128)S(1)}, f32[16,768]{1,0:T(8,128)S(1)}, u32[]{:S(2)}, u32[]{:S(2)}) collective-permute-start(f32[16,768]{1,0:T(8,128)S(1)} %add.315), channel_id=1, source_target_pairs={{0,1},{1,0},{2,3},{3,2},{4,5},{5,4},{6,7},{7,6},{8,9},{9,8},{10,11... | collective-permute-start | bytes 147464 | tf_op jit(solution)/shard_map/ppermute | solution.py:42
  274.4 12.3 %collective-permute-start.22 = (bf16[96,1152]{1,0:T(8,128)(2,1)S(1)}, bf16[96,1152]{1,0:T(8,128)(2,1)S(1)}, u32[]{:S(2)}, u32[]{:S(2)}) collective-permute-start(bf16[96,1152]{1,0:T(8,128)(2,1)S(1)} %fusion.11), channel_id=1, source_target_pairs={{0,1},{1,0},{2,3},{3,2},{4,5},{5,4},{6,7},{7,6},{8,9},{9,8},{10,11... | collective-permute-start | bytes 663560 | tf_op jit(solution)/shard_map/ppermute | solution.py:42
  278.3 8.6 %copy-start.18 = (f32[16,768]{1,0:T(8,128)}, f32[16,768]{1,0:T(8,128)S(1)}, u32[]{:S(2)}) copy-start(f32[16,768]{1,0:T(8,128)S(1)} %add.317.left_ref) | copy-start | bytes 147460
  278.3 8.6 %collective-permute-start.18 = (f32[16,768]{1,0:T(8,128)S(1)}, f32[16,768]{1,0:T(8,128)S(1)}, u32[]{:S(2)}, u32[]{:S(2)}) collective-permute-start(f32[16,768]{1,0:T(8,128)S(1)} %add.317.left_ref), channel_id=1, source_target_pairs={{0,2},{1,3},{2,0},{3,1},{4,6},{5,7},{6,4},{7,5},{8,10},{9,11},{10,... | collective-permute-start | bytes 147464 | tf_op jit(solution)/shard_map/ppermute | solution.py:42
  281.6 18.7 %collective-permute-start.20 = (bf16[24,4992]{1,0:T(8,128)(2,1)S(1)}, bf16[24,4992]{1,0:T(8,128)(2,1)S(1)}, u32[]{:S(2)}, u32[]{:S(2)}) collective-permute-start(bf16[24,4992]{1,0:T(8,128)(2,1)S(1)} %fusion.8), channel_id=1, source_target_pairs={{0,2},{1,3},{2,0},{3,1},{4,6},{5,7},{6,4},{7,5},{8,10},{9,11},{10,... | collective-permute-start | bytes 718856 | tf_op jit(solution)/shard_map/ppermute | solution.py:42
  286.8 15.8 %collective-permute-start.23 = (bf16[96,1152]{1,0:T(8,128)(2,1)S(1)}, bf16[96,1152]{1,0:T(8,128)(2,1)S(1)}, u32[]{:S(2)}, u32[]{:S(2)}) collective-permute-start(bf16[96,1152]{1,0:T(8,128)(2,1)S(1)} %fusion.14), channel_id=1, source_target_pairs={{0,2},{1,3},{2,0},{3,1},{4,6},{5,7},{6,4},{7,5},{8,10},{9,11},{10,... | collective-permute-start | bytes 663560 | tf_op jit(solution)/shard_map/ppermute | solution.py:42
  286.9 0.6 copy-start.19
  300.3 12.5 %collective-permute-start.21 = (bf16[48,4992]{1,0:T(8,128)(2,1)S(1)}, bf16[48,4992]{1,0:T(8,128)(2,1)S(1)}, u32[]{:S(2)}, u32[]{:S(2)}) collective-permute-start(bf16[48,4992]{1,0:T(8,128)(2,1)S(1)} %pad_maximum_fusion.5), channel_id=1, source_target_pairs={{0,1},{1,0},{2,3},{3,2},{4,5},{5,4},{6,7},{7,6},{8,9},{9,8},{10,11... | collective-permute-start | bytes 1437704 | tf_op jit(solution)/shard_map/ppermute | solution.py:42
  315.1 0.9 copy-start.22
Sparse Core Ops, SparseCore 0:
  10.5 50.2 all-gather.2
  62.7 38.9 all-gather.4
  114.4 59.3 reduce-scatter.2
  177.1 58.7 reduce-scatter.4

commit v4 on v3

--- a/solution.py
+++ b/solution.py
@@ -92,7 +92,7 @@
 class Sum:
     def __init__(self, value, short=False):
         me = lax.axis_index("dp")
-        self.low, self.high = me & 1, me >> 1
+        self.low, self.high = (me ^ (me >> 1)) & 1, me >> 1
         self.value = value
         self.short = short
         self.got = []
@@ -128,7 +128,7 @@
         return self.join(self.own(), self.got[2], self.high)
 
     def bit(self):
-        return ((1, 2) if self.short else (1, 2, 2, 1))[len(self.got)]
+        return ((1, 3) if self.short else (1, 3, 3, 1))[len(self.got)]
 
     def take(self, value):
         self.got.append(value)
@@ -410,50 +410,51 @@
     def one(at, carry):
         base = pl.multiple_of(table_ref[0, at], SNAP)
         start = table_ref[1, at]
-        window = pl.ds(base, WIN)
-        query = query_ref[window, :] * jnp.asarray(HD**-0.5, BF16)
-        key = key_ref[window, :]
-        value_t = value_ref[window, :].T
-        outs = []
-        for head in range(2):
-            mine = (lane >= HD) if head else (lane < HD)
-            scores = mm(jnp.where(mine, key, jnp.zeros_like(key)), query, NT) + bias_ref[at]
-            top = jnp.max(scores, axis=0, keepdims=True)
-            expo = jnp.exp(scores - top)
-            total = jnp.sum(expo, axis=0, keepdims=True)
-            mixed = mm(value_t[head * HD : (head + 1) * HD, :], expo.astype(BF16))
-            outs.append(mixed * (1.0 / total))
-            log_ref[0, at, pl.ds(head, 1), :] = top + jnp.log(total)
-        keep_from(mixed_ref, base, start, 0, jnp.concatenate(outs, axis=0).T)
+        for pair in range(query_ref.shape[1] // PAIR):
+            window = (pl.ds(base, WIN), pl.ds(pair * PAIR, PAIR))
+            query = query_ref[window] * jnp.asarray(HD**-0.5, BF16)
+            key = key_ref[window]
+            value_t = value_ref[window].T
+            outs = []
+            for head in range(2):
+                mine = (lane >= HD) if head else (lane < HD)
+                scores = mm(jnp.where(mine, key, jnp.zeros_like(key)), query, NT) + bias_ref[at]
+                top = jnp.max(scores, axis=0, keepdims=True)
+                expo = jnp.exp(scores - top)
+                total = jnp.sum(expo, axis=0, keepdims=True)
+                mixed = mm(value_t[head * HD : (head + 1) * HD, :], expo.astype(BF16))
+                outs.append(mixed * (1.0 / total))
+                log_ref[pair, at, pl.ds(head, 1), :] = top + jnp.log(total)
+            keep_from(mixed_ref, base, start, pair * PAIR, jnp.concatenate(outs, axis=0).T)
         return carry
 
     lax.fori_loop(0, table_ref[2, 0], one, 0)
 
 
-def attend(starts, crops, joint, first, pairs):
+def attend_scratch(rows):
+    return [pltpu.SMEM((3, 16), jnp.int32), pltpu.VMEM((group_bound(rows), WIN, WIN), F32)]
+
+
+def attend(starts, crops, joint, count):
     rows = joint.shape[0]
-    columns = pairs * 3 * PAIR
-    all_pairs = joint.shape[1] // (3 * PAIR)
-    part = lambda at: pl.BlockSpec((rows, PAIR), lambda i, *_: (0, at * all_pairs + first + i))
+    pairs = joint.shape[1] // (3 * PAIR)
     groups = group_bound(rows)
+    part = lambda at: pl.BlockSpec((rows, count * PAIR), lambda i, *_: (0, at * (pairs // count) + i))
     return pl.pallas_call(
         functools.partial(attend_kernel, rows),
         grid_spec=pltpu.PrefetchScalarGridSpec(
             num_scalar_prefetch=1,
-            grid=(pairs,),
+            grid=(pairs // count,),
             in_specs=[whole_spec((rows, 128)), part(0), part(1), part(2)],
-            out_specs=[
-                pl.BlockSpec((rows, PAIR), lambda i, *_: (0, i)),
-                pl.BlockSpec((1, groups, 8, WIN), lambda i, *_: (i, 0, 0, 0)),
-            ],
-            scratch_shapes=[pltpu.SMEM((3, 16), jnp.int32), pltpu.VMEM((groups, WIN, WIN), F32)],
+            out_specs=[part(0), pl.BlockSpec((count, groups, 8, WIN), lambda i, *_: (i, 0, 0, 0))],
+            scratch_shapes=attend_scratch(rows),
         ),
         out_shape=[
             jax.ShapeDtypeStruct((rows, pairs * PAIR), BF16),
             jax.ShapeDtypeStruct((pairs, groups, 8, WIN), F32),
         ],
         compiler_params=params(),
-        cost_estimate=cost(pairs * 6 * 8 * WIN**3, 2 * rows * columns * 4 // 3, pairs * 12 * WIN * WIN),
+        cost_estimate=cost(pairs * 6 * 8 * WIN**3, 2 * rows * pairs * 4 * PAIR, pairs * 12 * WIN * WIN),
         name="attend",
     )(starts, crops, joint, joint, joint)
 
@@ -472,38 +473,37 @@
     table_ref,
     bias_ref,
 ):
-    @pl.when(pl.program_id(0) == 0)
-    def _():
-        plan_groups(starts_ref, crops_ref, table_ref, bias_ref, rows)
-
+    plan_groups(starts_ref, crops_ref, table_ref, bias_ref, rows)
     lane = lax.broadcasted_iota(jnp.int32, (WIN, PAIR), 1)
+    low = lane < HD
 
     def one(at, carry):
         base = pl.multiple_of(table_ref[0, at], SNAP)
         start = table_ref[1, at]
-        window = pl.ds(base, WIN)
-        query = query_ref[window, :] * jnp.asarray(HD**-0.5, BF16)
-        key = key_ref[window, :]
-        value = value_ref[window, :]
-        key_t = key.T
-        grad = grad_ref[window, :]
-        inner_t = (grad.astype(F32) * mixed_ref[window, :].astype(F32)).T
-        d_query, d_key, d_value = [], [], []
-        for head in range(2):
-            mine = (lane >= HD) if head else (lane < HD)
-            zero = jnp.zeros_like(key)
-            scores = mm(jnp.where(mine, key, zero), query, NT) + bias_ref[at]
-            weights = jnp.exp(scores - log_ref[0, at, pl.ds(head, 1), :])
-            inner = jnp.sum(inner_t[head * HD : (head + 1) * HD, :], axis=0, keepdims=True)
-            d_weights = mm(jnp.where(mine, value, zero), grad, NT)
-            d_scores = (weights * (d_weights - inner)).astype(BF16)
-            d_value.append(mm(weights.astype(BF16), grad))
-            d_key.append(mm(d_scores, query))
-            d_query.append(mm(key_t[head * HD : (head + 1) * HD, :], d_scores) * HD**-0.5)
-        low = lane < HD
-        keep_from(out_ref, base, start, 0, jnp.concatenate(d_query, axis=0).T)
-        keep_from(out_ref, base, start, PAIR, jnp.where(low, d_key[0], d_key[1]))
-        keep_from(out_ref, base, start, 2 * PAIR, jnp.where(low, d_value[0], d_value[1]))
+        for pair in range(query_ref.shape[1] // PAIR):
+            window = (pl.ds(base, WIN), pl.ds(pair * PAIR, PAIR))
+            query = query_ref[window] * jnp.asarray(HD**-0.5, BF16)
+            key = key_ref[window]
+            value = value_ref[window]
+            key_t = key.T
+            grad = grad_ref[window]
+            inner_t = (grad.astype(F32) * mixed_ref[window].astype(F32)).T
+            d_query, d_key, d_value = [], [], []
+            for head in range(2):
+                mine = (lane >= HD) if head else low
+                zero = jnp.zeros_like(key)
+                scores = mm(jnp.where(mine, key, zero), query, NT) + bias_ref[at]
+                weights = jnp.exp(scores - log_ref[pair, at, pl.ds(head, 1), :])
+                inner = jnp.sum(inner_t[head * HD : (head + 1) * HD, :], axis=0, keepdims=True)
+                d_weights = mm(jnp.where(mine, value, zero), grad, NT)
+                d_scores = (weights * (d_weights - inner)).astype(BF16)
+                d_value.append(mm(weights.astype(BF16), grad))
+                d_key.append(mm(d_scores, query))
+                d_query.append(mm(key_t[head * HD : (head + 1) * HD, :], d_scores) * HD**-0.5)
+            column = 3 * PAIR * pair
+            keep_from(out_ref, base, start, column, jnp.concatenate(d_query, axis=0).T)
+            keep_from(out_ref, base, start, column + PAIR, jnp.where(low, d_key[0], d_key[1]))
+            keep_from(out_ref, base, start, column + 2 * PAIR, jnp.where(low, d_value[0], d_value[1]))
         return carry
 
     lax.fori_loop(0, table_ref[2, 0], one, 0)
@@ -512,25 +512,17 @@
 def attend_back(starts, crops, joint, mixed, grad, logs, first, count):
     rows = joint.shape[0]
     groups = group_bound(rows)
-    far = lambda columns: pl.BlockSpec((rows, columns), lambda i, *_: (0, first + i))
-    all_pairs = joint.shape[1] // (3 * PAIR)
-    part = lambda at: pl.BlockSpec((rows, PAIR), lambda i, *_: (0, at * all_pairs + first + i))
+    at, halves = first // count, joint.shape[1] // (3 * PAIR * count)
+    part = lambda at: pl.BlockSpec((rows, count * PAIR), lambda i, *_: (0, at))
     return pl.pallas_call(
         functools.partial(attend_back_kernel, rows),
         grid_spec=pltpu.PrefetchScalarGridSpec(
             num_scalar_prefetch=1,
-            grid=(count,),
-            in_specs=[
-                whole_spec((rows, 128)),
-                part(0),
-                part(1),
-                part(2),
-                pl.BlockSpec((rows, PAIR), lambda i, *_: (0, i)),
-                far(PAIR),
-                pl.BlockSpec((1, groups, 8, WIN), lambda i, *_: (i, 0, 0, 0)),
-            ],
-            out_specs=pl.BlockSpec((rows, 3 * PAIR), lambda i, *_: (0, i)),
-            scratch_shapes=[pltpu.SMEM((3, 16), jnp.int32), pltpu.VMEM((groups, WIN, WIN), F32)],
+            grid=(1,),
+            in_specs=[whole_spec((rows, 128)), part(at), part(halves + at), part(2 * halves + at), part(at), part(at)]
+            + [pl.BlockSpec((count, groups, 8, WIN), lambda i, *_: (at, 0, 0, 0))],
+            out_specs=whole_spec((rows, count * 3 * PAIR)),
+            scratch_shapes=attend_scratch(rows),
         ),
         out_shape=jax.ShapeDtypeStruct((rows, count * 3 * PAIR), BF16),
         compiler_params=params(),
@@ -539,12 +531,11 @@
     )(starts, crops, joint, joint, joint, mixed, grad, logs)
 
 
-def up_kernel(out_weight, up_weight, me_ref, x_ref, mixed_a_ref, mixed_b_ref, vec_ref, *refs):
+def up_kernel(out_weight, up_weight, me_ref, x_ref, mixed_ref, vec_ref, *refs):
     count = len(out_weight.arrays)
     middle_ref, hidden_ref, active_ref, slope_ref, out_s, out_sem, up_s, up_sem = refs[count:]
     load_first([out_weight, up_weight], me_ref[0], refs[:count], [(out_s, out_sem), (up_s, up_sem)])
-    mixed = jnp.concatenate([mixed_a_ref[...], mixed_b_ref[...]], axis=1)
-    middle = x_ref[...].astype(F32) + mm(mixed, out_s[...]) + vec_ref[4:5, :]
+    middle = x_ref[...].astype(F32) + mm(mixed_ref[...], out_s[...]) + vec_ref[4:5, :]
     middle_ref[...] = middle
     unit, _ = normed(middle)
     hidden = (unit * vec_ref[5:6, :] + vec_ref[6:7, :]).astype(BF16)
@@ -559,7 +550,7 @@
         slope_ref[:, part] = (below + value * bell).astype(BF16)
 
 
-def up_forward(me, tokens, mixed_a, mixed_b, vectors, out_weight, up_weight):
+def up_forward(me, tokens, mixed, vectors, out_weight, up_weight):
     rows, width = tokens.shape
     inner = up_weight.shape[1]
     arrays = out_weight.arrays
@@ -568,7 +559,7 @@
         grid_spec=pltpu.PrefetchScalarGridSpec(
             num_scalar_prefetch=1,
             grid=(rows // TILE,),
-            in_specs=[row_spec(width), row_spec(width // 2), row_spec(width // 2), whole_spec(vectors.shape)]
+            in_specs=[row_spec(width), row_spec(width), whole_spec(vectors.shape)]
             + any_specs(len(arrays)),
             out_specs=[row_spec(width), row_spec(width), row_spec(inner), row_spec(inner)],
             scratch_shapes=out_weight.scratch() + up_weight.scratch(),
@@ -582,7 +573,7 @@
         compiler_params=params(),
         cost_estimate=cost(2 * rows * width * (width + inner), rows * (10 * width + 4 * inner) + 2 * width * inner, rows * inner * 2),
         name="up_forward",
-    )(me, tokens, mixed_a, mixed_b, vectors, *arrays)
+    )(me, tokens, mixed, vectors, *arrays)
 
 
 def slope_kernel(down_weight, me_ref, grad_ref, slope_ref, *refs):
@@ -869,11 +860,10 @@
     lower_group = Gather(after(down_weight, outer), fsdp).whole()
     joint_full = Weight(group, 0, joint_width, spare=8 if eight else 0)
     joint, hidden_first, vectors = joint_forward(me, source, vectors, joint_full)
-    mixed_a, logs_a = attend(starts, crops, joint, 0, near)
-    mixed_b, logs_b = attend(starts, crops, joint, near, pairs - near)
+    mixed, logs = attend(starts, crops, joint, near)
     out_full = Weight(outer_group, 0, width)
     up_full = Weight(outer_group, width, inner)
-    middle, hidden_second, active, slope = up_forward(me, tokens, mixed_a, mixed_b, vectors, out_full, up_full)
+    middle, hidden_second, active, slope = up_forward(me, tokens, mixed, vectors, out_full, up_full)
     grad = cotangent
     down_full = Weight(lower_group, 0, width)
 
@@ -890,15 +880,15 @@
     )
     up_grad = scattered(up_grad)
     down_grad = start(down_grad, scattered=True)
-    grad_a = attend_back(starts, crops, joint, mixed_a, grad_mixed, logs_a, 0, near)
+    grad_a = attend_back(starts, crops, joint, mixed, grad_mixed, logs, 0, near)
     low = behind(grad_low, grad_a)
-    out_slabs = jnp.concatenate([weight_grad(mixed_a, low), weight_grad(mixed_b, low)], axis=0).reshape(fsdp, own, width)
+    out_slabs = weight_grad(mixed, low).reshape(fsdp, own, width)
     slabs_a = weight_grad(hidden_first, grad_a).reshape(fsdp, own, -1)
     mixed_grad = start(jnp.concatenate([out_slabs, slabs_a], axis=2))
     if eight:
         mixed_grad.more = up_grad
     sent = [mixed_grad.step(), down_grad.step(grad_a)]
-    grad_b = attend_back(starts, crops, joint, mixed_b, behind(grad_mixed, *sent), logs_b, near, pairs - near)
+    grad_b = attend_back(starts, crops, joint, mixed, behind(grad_mixed, *sent), logs, near, pairs - near)
     last_slabs = weight_grad(behind(hidden_first, mixed_grad.step(grad_b)), grad_b)
     last_grad = start(last_slabs.reshape(fsdp, own, -1), True)
     sent = [last_grad.step(), down_grad.step(last_slabs)]
@@ -914,22 +904,25 @@
         up_sums,
         joint_full,
     )
-    sent = [last_grad.step(total), mixed_grad.step(total), down_grad.step(total)]
+    sent = [mixed_grad.step(total), last_grad.step(total), down_grad.step(total)]
     if eight and dp == 4:
         total = behind(total, *sent)
-        total = total + send(total, CORE)
-        sent = [down_grad.step(total), last_grad.step(total)]
+        other = send(total, CORE)
+        acts = down_forward(me, behind(middle, *sent), active, vectors, down_full)
+        sent = [mixed_grad.step(acts)]
+        total = behind(total + other, *sent)
+        sent = [last_grad.step(total), down_grad.step(total)]
         total = behind(total, *sent)
         total = total + send(total, FIRST)
+        total = total + send(total, SECOND)
         sent = [mixed_grad.step(total)]
         total = behind(total, *sent)
-        total = total + send(total, SECOND)
         sent = [last_grad.step(total)]
-        acts = down_forward(me, behind(middle, *sent), active, vectors, down_full)
-        sent = [mixed_grad.step(acts)]
         total = behind(total, *sent)
         total = total + send_dp(total, 1)
-        vecs = own_rows(me, total, send_dp(total, 2))
+        sent = [mixed_grad.step(total)]
+        total = behind(total, *sent)
+        vecs = own_rows(me, total, send_dp(total, 3))
     else:
         acts = down_forward(me, behind(middle, *sent), active, vectors, down_full)
         total = lax.psum(total, ("fsdp", "dp"))

time: 323 us -> 311 us (0.963)
  waiting for transfers between devices: 73 us -> 57.5 us
  starting transfers between devices: 37.6 us -> 48.6 us
  Pallas kernels: 141 us -> 133 us
    ppermute x12, starting transfers between devices: 23 us -> 36.5 us  [send_dp(): return lax.ppermute(value, 'dp', [(i, i ^ bit) for i in range(4)])]
    ppermute x12, waiting for transfers between devices: 36.4 us -> 22.9 us  [send_dp(): return lax.ppermute(value, 'dp', [(i, i ^ bit) for i in range(4)])]
    pallas_call x2 -> x1, Pallas kernels: 30.7 us -> 24 us  [attend(): pl.pallas_call(functools.partial(attend_kernel, rows), grid_spec=pltpu.Pr...]
    ppermute x13, waiting for transfers between devices: 35.9 us -> 32.6 us  [send(): return lax.ppermute(value, 'fsdp', pairs)]
    unnamed x79 -> x69, local copies, waits for them, and re-layouts: 6.9 us -> 6.13 us
    dot_general x6 -> x5, matrix products: 26.2 us -> 26 us  [weight_grad(): lax.dot_general(left, right, (((0,), (0,)), ((), ())), preferred_element_...]
  transfers between devices with their start and end apart: 29 -> 29, of which waited for: 15 -> 13; matrix products, arithmetic and copies ran while one was open for 14% -> 15% of each run, Pallas kernels for 44% -> 43%
where the time goes in v4:
time: 311 us; the launch traced here: 309 us
  Pallas kernels  133 us (43%)
  waiting for transfers between devices  57.5 us (18%)
  starting transfers between devices  48.6 us (16%)
  matrix products  26 us (8%)
  other arithmetic  20.5 us (7%)
  between operations  14.5 us (5%)
  local copies, waits for them, and re-layouts  9.47 us (3%)
    ppermute x12, starting transfers between devices, send_dp(): return lax.ppermute(value, 'dp', [(i, i ^ bit) for i in range(4)])  36.5 us
    ppermute x13, waiting for transfers between devices, send(): return lax.ppermute(value, 'fsdp', pairs)  32.6 us
    pallas_call x2, Pallas kernels, attend_back(): pl.pallas_call(functools.partial(attend_back_kernel, rows), grid_spec=plt...  28.1 us
    dot_general x5, matrix products, weight_grad(): lax.dot_general(left, right, (((0,), (0,)), ((), ())), preferred_element_...  26 us
    pallas_call x1, Pallas kernels, attend(): pl.pallas_call(functools.partial(attend_kernel, rows), grid_spec=pltpu.Pr...  24 us
    ppermute x12, waiting for transfers between devices, send_dp(): return lax.ppermute(value, 'dp', [(i, i ^ bit) for i in range(4)])  22.9 us
    pallas_call x1, Pallas kernels, up_forward(): pl.pallas_call(functools.partial(up_kernel, out_weight, up_weight), grid_...  18.8 us
    pallas_call x1, Pallas kernels, middle_back(): pl.pallas_call(functools.partial(middle_kernel, out_weight, up_weight), g...  16 us
  transfers between devices with their start and end apart: 29, of which 13 were waited for; matrix products, arithmetic and copies ran while one was open for 15% of the time, Pallas kernels for 43%

profile of v4, /device:TPU:0, one launch (start us, length us, event | category | flops | bytes accessed | tf_op | source)
XLA Modules:
  0.0 309.2 jit_solution(12846021827266876180)
XLA Ops:
  7.3 1.0 constant_dynamic-update-slice_fusion.1
  8.4 1.1 constant_dynamic-update-slice_fusion
  9.5 0.9 copy-done.5
  11.3 3.0 collective-permute-start
  14.4 6.6 %collective-permute-done = bf16[104,2304]{1,0:T(8,128)(2,1)S(1)} collective-permute-done((bf16[104,2304]{1,0:T(8,128)(2,1)S(1)}, bf16[104,2304]{1,0:T(8,128)(2,1)S(1)}, u32[]{:S(2)}, u32[]{:S(2)}) %collective-permute-start) | collective-permute-done | bytes 479264 | tf_op jit(solution)/shard_map/ppermute | solution.py:38
  21.2 2.1 collective-permute-start.1
  23.3 18.8 %collective-permute-done.1.refs_1_ = bf16[2,104,2304]{2,1,0:T(8,128)(2,1)S(1)} collective-permute-done((bf16[2,104,2304]{2,1,0:T(8,128)(2,1)S(1)}, bf16[2,104,2304]{2,1,0:T(8,128)(2,1)S(1)}, u32[]{:S(2)}, u32[]{:S(2)}) %collective-permute-start.1) | collective-permute-done | bytes 958496 | tf_op jit(solution)/shard_map/ppermute | solution.py:38
  42.1 1.2 convert_reduce_fusion.starts_ref
  43.4 1.1 broadcast_in_dim.29.crops_ref
  45.4 9.5 %joint_forward.1 = (bf16[1024,2304]{1,0:T(8,128)(2,1)}, bf16[1024,768]{1,0:T(8,128)(2,1)}, f32[16,768]{1,0:T(8,128)}) custom-call(s32[1]{0:T(128)} %bitcast.me_ref, bf16[1024,768]{1,0:T(8,128)(2,1)} %x_ref.3, bf16[2,104,2304]{2,1,0:T(8,128)(2,1)} %copy-done, bf16[2,104,2304]{2,1,0:T(8,128)(2,1)} %copy-done.6, bf16[2,104,2304]{2,1,0:T(8,128)(2,1)} %copy-done.7, ...), custom_call_target="tpu_custom_call" | custom-call | flops 3623878656 | bytes 11403264 | tf_op jit(solution)/shard_map/joint_forward/pallas_call | solution.py:356
  54.9 24.0 %attend.1 = (bf16[1024,768]{1,0:T(8,128)(2,1)}, f32[6,10,8,256]{3,2,1,0:T(8,128)}) custom-call(s32[1024]{0:T(1024)} %convert_reduce_fusion.starts_ref, f32[1024,128]{1,0:T(8,128)} %broadcast_in_dim.29.crops_ref, bf16[1024,2304]{1,0:T(8,128)(2,1)} %get-tuple-element.68.query_ref.key_ref.value_ref, ...), custom_call_target="tpu_custom_call" | custom-call | flops 4831838208 | bytes 6291456 | tf_op jit(solution)/shard_map/attend/pallas_call | solution.py:443
  78.9 18.8 %up_forward.1 = (f32[1024,768]{1,0:T(8,128)}, bf16[1024,768]{1,0:T(8,128)(2,1)}, bf16[1024,3072]{1,0:T(8,128)(2,1)}, bf16[1024,3072]{1,0:T(8,128)(2,1)}) custom-call(s32[1]{0:T(128)} %bitcast.me_ref, bf16[1024,768]{1,0:T(8,128)(2,1)} %x_ref.3, bf16[1024,768]{1,0:T(8,128)(2,1)} %get-tuple-element.69.mixed_ref, f32[16,768]{1,0:T(8,128)} %get-tuple-element.70.vec_ref, ...), custom_call_target="tpu_custom_call" | custom-call | flops 6039797760 | bytes 25165824 | tf_op jit(solution)/shard_map/up_forward/pallas_call | solution.py:557
  97.7 9.8 %convolution_convert_fusion.1 = bf16[3072,768]{1,0:T(8,128)(2,1)} fusion(bf16[1024,3072]{1,0:T(8,128)(2,1)} %get-tuple-element.72.active_ref, bf16[1024,768]{1,0:T(8,128)(2,1)S(1)} %copy-done.24), kind=kOutput, calls=%fused_computation.6 | convolution fusion | flops 4834197504 | bytes 12582912 | tf_op jit(solution)/shard_map/dot_general | solution.py:799
  107.8 12.3 %slope_back.1 = (bf16[1024,3072]{1,0:T(8,128)(2,1)}, f32[8,768]{1,0:T(8,128)}, f32[8,3072]{1,0:T(8,128)}) custom-call(s32[1]{0:T(128)} %bitcast.me_ref, bf16[1024,768]{1,0:T(8,128)(2,1)} %grad_ref.2, bf16[1024,3072]{1,0:T(8,128)(2,1)} %get-tuple-element.74.slope_ref, bf16[3072,768]{1,0:T(8,128)(2,1)} %all-gather.5.cloned.1.call-done.refs_0_), custom_call_target="tpu_custom_call" | custom-call | flops 4831838208 | bytes 18874368 | tf_op jit(solution)/shard_map/slope_back/pallas_call | solution.py:601
  120.1 10.2 %convolution_convert_fusion = bf16[768,3072]{1,0:T(8,128)(2,1)} fusion(bf16[1024,768]{1,0:T(8,128)(2,1)S(1)} %copy-done.27, bf16[1024,3072]{1,0:T(8,128)(2,1)} %get-tuple-element.78.ga_ref), kind=kOutput, calls=%fused_computation.5 | convolution fusion | flops 4834197504 | bytes 12582912 | tf_op jit(solution)/shard_map/dot_general | solution.py:799
  130.3 16.0 %middle_back.1 = (f32[1024,768]{1,0:T(8,128)}, bf16[1024,768]{1,0:T(8,128)(2,1)}, bf16[1024,768]{1,0:T(8,128)(2,1)}, f32[3,8,768]{2,1,0:T(8,128)}) custom-call(s32[1]{0:T(128)} %bitcast.me_ref, f32[1024,768]{1,0:T(8,128)} %get-tuple-element.98.middle_ref, bf16[1024,768]{1,0:T(8,128)(2,1)} %grad_ref.2, bf16[1024,3072]{1,0:T(8,128)(2,1)} %get-tuple-element.78.ga_ref, ...), custom_call_target="tpu_custom_call" | custom-call | flops 6039797760 | bytes 22020096 | tf_op jit(solution)/shard_map/middle_back/pallas_call | solution.py:645
  146.3 13.8 %attend_back.2.part_a_ref = bf16[1024,1152]{1,0:T(8,128)(2,1)} custom-call(s32[1024]{0:T(1024)} %convert_reduce_fusion.starts_ref, f32[1024,128]{1,0:T(8,128)} %broadcast_in_dim.29.crops_ref, bf16[1024,2304]{1,0:T(8,128)(2,1)} %get-tuple-element.68.query_ref.key_ref.value_ref, bf16[1024,2304]{1,0:T(8,128)(2,1)} %get-tuple-element.68.query_ref.key_ref.value_ref, ...), custom_call_target="tpu_custom_call" | custom-call | flops 6039797760 | bytes 6291456 | tf_op jit(solution)/shard_map/attend_back/pallas_call | solution.py:517
  160.1 1.4 convolution_convert_fusion.4
  162.3 2.3 convolution_convert_fusion.3
  164.6 1.2 fusion.1
  165.8 0.9 collective-permute-start.4
  166.7 1.0 dynamic-slice_bitcast_fusion.2
  167.7 7.5 %collective-permute-start.6 = (bf16[192,768]{1,0:T(8,128)(2,1)S(1)}, bf16[192,768]{1,0:T(8,128)(2,1)S(1)}, u32[]{:S(2)}, u32[]{:S(2)}) collective-permute-start(bf16[192,768]{1,0:T(8,128)(2,1)S(1)} %dynamic-slice_bitcast_fusion.2), channel_id=1, source_target_pairs={{0,1},{1,0},{2,3},{3,2},{4,5},{5,4},{6,7},{7,6},{8,9},{9,8},{10,11... | collective-permute-start | bytes 884744 | tf_op jit(solution)/shard_map/ppermute | solution.py:42
  175.2 14.3 %attend_back.3.part_b_ref = bf16[1024,1152]{1,0:T(8,128)(2,1)} custom-call(s32[1024]{0:T(1024)} %convert_reduce_fusion.starts_ref, f32[1024,128]{1,0:T(8,128)} %broadcast_in_dim.29.crops_ref, bf16[1024,2304]{1,0:T(8,128)(2,1)} %get-tuple-element.68.query_ref.key_ref.value_ref, bf16[1024,2304]{1,0:T(8,128)(2,1)} %get-tuple-element.68.query_ref.key_ref.value_ref, ...), custom_call_target="tpu_custom_call" | custom-call | flops 6039797760 | bytes 6291456 | tf_op jit(solution)/shard_map/attend_back/pallas_call | solution.py:517
  189.4 1.4 fusion.6
  190.9 0.9 pad_maximum_fusion.2
  191.8 0.9 collective-permute-start.5
  192.8 2.3 convolution_convert_fusion.2
  195.2 1.0 copy-done.3
  196.7 3.7 %collective-permute-start.8 = (bf16[96,768]{1,0:T(8,128)(2,1)S(1)}, bf16[96,768]{1,0:T(8,128)(2,1)S(1)}, u32[]{:S(2)}, u32[]{:S(2)}) collective-permute-start(bf16[96,768]{1,0:T(8,128)(2,1)S(1)} %fusion.21), channel_id=1, source_target_pairs={{0,3},{1,2},{2,1},{3,0},{4,7},{5,6},{6,5},{7,4},{8,11},{9,10},{10,... | collective-permute-start | bytes 442376 | tf_op jit(solution)/shard_map/ppermute | solution.py:42
  200.4 11.2 %first_back.1 = (f32[1024,768]{1,0:T(8,128)}, f32[16,768]{1,0:T(8,128)}) custom-call(s32[1]{0:T(128)} %bitcast.me_ref, bf16[1024,768]{1,0:T(8,128)(2,1)} %x_ref.3, f32[1024,768]{1,0:T(8,128)} %get-tuple-element.90.gmid_ref, bf16[1024,1152]{1,0:T(8,128)(2,1)} %attend_back.2.part_a_ref, bf16[1024,1152]{1,0:T(8,128)(2,1)} %attend_back.3.part_b_ref, ...), custom_call_target="tpu_custom_call" | custom-call | flops 3623878656 | bytes 16121856 | tf_op jit(solution)/shard_map/first_back/pallas_call | solution.py:746
  212.0 2.6 collective-permute-done.5
  214.6 1.2 fusion.4
  215.9 1.5 collective-permute-start.10
  217.4 1.5 fusion.13
  218.9 0.8 pad_maximum_fusion.5
  220.2 11.4 %down_forward.1 = f32[1024,768]{1,0:T(8,128)} custom-call(s32[1]{0:T(128)} %bitcast.me_ref, f32[1024,768]{1,0:T(8,128)} %get-tuple-element.98.middle_ref, bf16[1024,3072]{1,0:T(8,128)(2,1)} %get-tuple-element.72.active_ref, f32[16,768]{1,0:T(8,128)} %get-tuple-element.70.vec_ref, bf16[3072,768]{1,0:T(8,128)(2,1)} %all-gather.5.cloned.1.call-done.refs_0_), custom_call_target="tpu_custom_call" | custom-call | flops 4831838208 | bytes 17301504 | tf_op jit(solution)/shard_map/down_forward/pallas_call | solution.py:677
  231.7 1.3 fusion.3
  233.0 1.3 reduce-scatter.5.cloned.1.call-done
  234.3 1.1 pad_maximum_fusion.1
  235.5 0.9 broadcast_select_fusion.7
  236.4 1.5 collective-permute-start.24
  238.5 1.8 fusion.11
  240.3 1.3 collective-permute-start.13
  242.4 2.2 collective-permute-done.13
  244.5 0.8 add.311
  246.5 1.1 broadcast_select_fusion.3
  247.5 1.9 collective-permute-done.14
  249.4 6.1 %collective-permute-done.15 = bf16[48,4992]{1,0:T(8,128)(2,1)S(1)} collective-permute-done((bf16[48,4992]{1,0:T(8,128)(2,1)S(1)}, bf16[48,4992]{1,0:T(8,128)(2,1)S(1)}, u32[]{:S(2)}, u32[]{:S(2)}) %collective-permute-start.15) | collective-permute-done | bytes 479264 | tf_op jit(solution)/shard_map/ppermute | solution.py:42
  255.7 3.7 %collective-permute-start.18 = (bf16[24,4992]{1,0:T(8,128)(2,1)S(1)}, bf16[24,4992]{1,0:T(8,128)(2,1)S(1)}, u32[]{:S(2)}, u32[]{:S(2)}) collective-permute-start(bf16[24,4992]{1,0:T(8,128)(2,1)S(1)} %fusion.20), channel_id=1, source_target_pairs={{0,3},{1,2},{2,1},{3,0},{4,7},{5,6},{6,5},{7,4},{8,11},{9,10},{10,... | collective-permute-start | bytes 718856 | tf_op jit(solution)/shard_map/ppermute | solution.py:42
  259.4 1.2 fusion.10
  260.7 1.1 maximum_convert_fusion
  261.8 2.0 collective-permute-start.22
  263.8 2.9 collective-permute-done.17
  266.8 3.3 %collective-permute-start.20 = (bf16[24,4992]{1,0:T(8,128)(2,1)S(1)}, bf16[24,4992]{1,0:T(8,128)(2,1)S(1)}, u32[]{:S(2)}, u32[]{:S(2)}) collective-permute-start(bf16[24,4992]{1,0:T(8,128)(2,1)S(1)} %fusion.8), channel_id=1, source_target_pairs={{0,3},{1,2},{2,1},{3,0},{4,7},{5,6},{6,5},{7,4},{8,11},{9,10},{10,... | collective-permute-start | bytes 718856 | tf_op jit(solution)/shard_map/ppermute | solution.py:42
  270.7 1.4 collective-permute-done.22
  272.2 2.7 collective-permute-start.23
  274.9 2.8 collective-permute-done.19.right_ref
  278.3 1.5 own_rows.1
  279.9 10.4 %collective-permute-start.21 = (bf16[48,4992]{1,0:T(8,128)(2,1)S(1)}, bf16[48,4992]{1,0:T(8,128)(2,1)S(1)}, u32[]{:S(2)}, u32[]{:S(2)}) collective-permute-start(bf16[48,4992]{1,0:T(8,128)(2,1)S(1)} %pad_maximum_fusion.4), channel_id=1, source_target_pairs={{0,1},{1,0},{2,3},{3,2},{4,5},{5,4},{6,7},{7,6},{8,9},{9,8},{10,11... | collective-permute-start | bytes 1437704 | tf_op jit(solution)/shard_map/ppermute | solution.py:42
  290.4 9.0 %collective-permute-done.21 = bf16[48,4992]{1,0:T(8,128)(2,1)S(1)} collective-permute-done((bf16[48,4992]{1,0:T(8,128)(2,1)S(1)}, bf16[48,4992]{1,0:T(8,128)(2,1)S(1)}, u32[]{:S(2)}, u32[]{:S(2)}) %collective-permute-start.21) | collective-permute-done | bytes 479264 | tf_op jit(solution)/shard_map/ppermute | solution.py:42
  299.7 0.7 maximum_convert_fusion.1
  300.4 1.1 fusion.7
  301.8 0.9 copy-done.15
  (135 shorter events, 9.2 us)
Async XLA Ops:
  7.2 4.0 %copy-start.23 = (bf16[384]{0:T(512)(128)(2,1)S(1)}, bf16[384]{0:T(512)(128)(2,1)}, u32[]{:S(2)}) copy-start(bf16[384]{0:T(512)(128)(2,1)} %param.26) | copy-start | bytes 2308
  7.2 4.0 %copy-start.22 = (bf16[2,96]{1,0:T(2,128)(2,1)S(1)}, bf16[2,96]{1,0:T(2,128)(2,1)}, u32[]{:S(2)}) copy-start(bf16[2,96]{1,0:T(2,128)(2,1)} %param.20) | copy-start | bytes 1156
  7.2 4.0 %copy-start.4 = (bf16[96,2304]{1,0:T(8,128)(2,1)S(1)}, bf16[96,2304]{1,0:T(8,128)(2,1)}, u32[]{:S(2)}) copy-start(bf16[96,2304]{1,0:T(8,128)(2,1)} %param.19) | copy-start | bytes 1327108
  7.2 4.0 %copy-start.16 = (bf16[96]{0:T(256)(128)(2,1)S(1)}, bf16[96]{0:T(256)(128)(2,1)}, u32[]{:S(2)}) copy-start(bf16[96]{0:T(256)(128)(2,1)} %param.28) | copy-start | bytes 580
  7.2 4.0 %copy-start.17 = (bf16[96]{0:T(256)(128)(2,1)S(1)}, bf16[96]{0:T(256)(128)(2,1)}, u32[]{:S(2)}) copy-start(bf16[96]{0:T(256)(128)(2,1)} %param.24) | copy-start | bytes 580
  7.2 4.0 %copy-start.18 = (bf16[96]{0:T(256)(128)(2,1)S(1)}, bf16[96]{0:T(256)(128)(2,1)}, u32[]{:S(2)}) copy-start(bf16[96]{0:T(256)(128)(2,1)} %param.23) | copy-start | bytes 580
  7.2 4.0 %copy-start.19 = (bf16[96]{0:T(256)(128)(2,1)S(1)}, bf16[96]{0:T(256)(128)(2,1)}, u32[]{:S(2)}) copy-start(bf16[96]{0:T(256)(128)(2,1)} %param.22) | copy-start | bytes 580
  7.3 4.0 %copy-start.20 = (bf16[96]{0:T(256)(128)(2,1)S(1)}, bf16[96]{0:T(256)(128)(2,1)}, u32[]{:S(2)}) copy-start(bf16[96]{0:T(256)(128)(2,1)} %param.18) | copy-start | bytes 580
  7.3 4.0 %copy-start.21 = (bf16[96]{0:T(256)(128)(2,1)S(1)}, bf16[96]{0:T(256)(128)(2,1)}, u32[]{:S(2)}) copy-start(bf16[96]{0:T(256)(128)(2,1)} %param.17) | copy-start | bytes 580
  7.3 71.6 %all-gather.3.cloned.1.call-start = ((), (), s32[]{:S(2)}) async-start(), calls=%async_computation.2 | async-start | bytes 6635520 | tf_op jit(solution)/shard_map/all_gather | solution.py:201
  9.5 0.9 copy-start.5
  10.4 97.4 %all-gather.5.cloned.1.call-start = ((), (), s32[]{:S(2)}) async-start(), calls=%async_computation.3 | async-start | bytes 5308416 | tf_op jit(solution)/shard_map/all_gather | solution.py:201
  11.1 155.6 %reduce-scatter.3.cloned.1.call-start = ((), (), s32[]{:S(2)}) async-start(), calls=%async_computation.4 | async-start | bytes 5308416 | tf_op jit(solution)/shard_map/reduce_scatter | solution.py:873
  11.3 30.8 %copy-start.14 = (s32[1024]{0:T(1024)S(1)}, s32[1024]{0:T(1024)}, u32[]{:S(2)}) copy-start(s32[1024]{0:T(1024)} %param.16) | copy-start | bytes 12292
  11.3 9.7 %collective-permute-start = (bf16[104,2304]{1,0:T(8,128)(2,1)S(1)}, bf16[104,2304]{1,0:T(8,128)(2,1)S(1)}, u32[]{:S(2)}, u32[]{:S(2)}) collective-permute-start(bf16[104,2304]{1,0:T(8,128)(2,1)S(1)} %pad_add_fusion), channel_id=1, source_target_pairs={{0,8},{4,20},{8,0},{12,28},{16,24},{20,4},{24,16},{28,12},{1,9},{5... | collective-permute-start | bytes 1437704 | tf_op jit(solution)/shard_map/ppermute | solution.py:38
  21.1 23.7 %copy-start = (bf16[2,104,2304]{2,1,0:T(8,128)(2,1)}, bf16[2,104,2304]{2,1,0:T(8,128)(2,1)S(1)}, u32[]{:S(2)}) copy-start(bf16[2,104,2304]{2,1,0:T(8,128)(2,1)S(1)} %pad_maximum_fusion.refs_0_) | copy-start | bytes 2875396
  21.2 21.0 %collective-permute-start.1 = (bf16[2,104,2304]{2,1,0:T(8,128)(2,1)S(1)}, bf16[2,104,2304]{2,1,0:T(8,128)(2,1)S(1)}, u32[]{:S(2)}, u32[]{:S(2)}) collective-permute-start(bf16[2,104,2304]{2,1,0:T(8,128)(2,1)S(1)} %pad_maximum_fusion.refs_0_), channel_id=1, source_target_pairs={{0,16},{4,12},{8,24},{12,4},{16,0},{20,28},{24,8},{28,20},{1,17},{... | collective-permute-start | bytes 2875400 | tf_op jit(solution)/shard_map/ppermute | solution.py:38
  23.3 21.2 %collective-permute-start.2 = (bf16[2,104,2304]{2,1,0:T(8,128)(2,1)S(1)}, bf16[2,104,2304]{2,1,0:T(8,128)(2,1)S(1)}, u32[]{:S(2)}, u32[]{:S(2)}) collective-permute-start(bf16[2,104,2304]{2,1,0:T(8,128)(2,1)S(1)} %pad_maximum_fusion.refs_0_), channel_id=1, source_target_pairs={{0,4},{4,0},{8,12},{12,8},{16,20},{20,16},{24,28},{28,24},{1,5},{5... | collective-permute-start | bytes 2875400 | tf_op jit(solution)/shard_map/ppermute | solution.py:38
  42.1 2.8 copy-start.6
  42.1 2.8 collective-permute-start.3
  44.4 1.0 copy-start.7
  78.9 18.8 %copy-start.24 = (bf16[1024,768]{1,0:T(8,128)(2,1)S(1)}, bf16[1024,768]{1,0:T(8,128)(2,1)}, u32[]{:S(2)}) copy-start(bf16[1024,768]{1,0:T(8,128)(2,1)} %grad_ref.2) | copy-start | bytes 4718596
  107.5 126.7 %reduce-scatter.5.cloned.1.call-start = ((), (), s32[]{:S(2)}) async-start(), calls=%async_computation.5 | async-start | bytes 5308416 | tf_op jit(solution)/shard_map/reduce_scatter | solution.py:873
  107.8 12.3 %copy-start.27 = (bf16[1024,768]{1,0:T(8,128)(2,1)S(1)}, bf16[1024,768]{1,0:T(8,128)(2,1)}, u32[]{:S(2)}) copy-start(bf16[1024,768]{1,0:T(8,128)(2,1)} %get-tuple-element.77) | copy-start | bytes 4718596
  146.3 13.8 %copy-start.25 = (bf16[1024,768]{1,0:T(8,128)(2,1)S(1)}, bf16[1024,768]{1,0:T(8,128)(2,1)}, u32[]{:S(2)}) copy-start(bf16[1024,768]{1,0:T(8,128)(2,1)} %get-tuple-element.69.mixed_ref) | copy-start | bytes 4718596
  146.3 13.8 %copy-start.26 = (bf16[1024,768]{1,0:T(8,128)(2,1)S(1)}, bf16[1024,768]{1,0:T(8,128)(2,1)}, u32[]{:S(2)}) copy-start(bf16[1024,768]{1,0:T(8,128)(2,1)} %get-tuple-element.82) | copy-start | bytes 4718596
  160.1 1.7 copy-start.1
  160.1 2.2 copy-start.28
  165.8 23.6 %collective-permute-start.4 = (bf16[4,96,1920]{2,1,0:T(8,128)(2,1)}, bf16[4,96,1920]{2,1,0:T(8,128)(2,1)}, u32[]{:S(2)}, u32[]{:S(2)}) collective-permute-start(bf16[4,96,1920]{2,1,0:T(8,128)(2,1)} %fusion.1), channel_id=1, source_target_pairs={{0,4},{4,0},{8,12},{12,8},{16,20},{20,16},{24,28},{28,24},{1,5},{5... | collective-permute-start | bytes 4423688 | tf_op jit(solution)/shard_map/ppermute | solution.py:38
  167.7 28.5 %collective-permute-start.6 = (bf16[192,768]{1,0:T(8,128)(2,1)S(1)}, bf16[192,768]{1,0:T(8,128)(2,1)S(1)}, u32[]{:S(2)}, u32[]{:S(2)}) collective-permute-start(bf16[192,768]{1,0:T(8,128)(2,1)S(1)} %dynamic-slice_bitcast_fusion.2), channel_id=1, source_target_pairs={{0,1},{1,0},{2,3},{3,2},{4,5},{5,4},{6,7},{7,6},{8,9},{9,8},{10,11... | collective-permute-start | bytes 884744 | tf_op jit(solution)/shard_map/ppermute | solution.py:42
  189.4 3.3 %copy-start.2 = (bf16[1024,1152]{1,0:T(8,128)(2,1)S(1)}, bf16[1024,1152]{1,0:T(8,128)(2,1)}, u32[]{:S(2)}) copy-start(bf16[1024,1152]{1,0:T(8,128)(2,1)} %attend_back.3.part_b_ref) | copy-start | bytes 7077892
  189.4 3.3 %copy-start.29 = (bf16[1024,768]{1,0:T(8,128)(2,1)S(1)}, bf16[1024,768]{1,0:T(8,128)(2,1)}, u32[]{:S(2)}) copy-start(bf16[1024,768]{1,0:T(8,128)(2,1)} %get-tuple-element.87) | copy-start | bytes 4718596
  191.8 22.8 %collective-permute-start.5 = (bf16[2,96,1920]{2,1,0:T(8,128)(2,1)}, bf16[2,96,1920]{2,1,0:T(8,128)(2,1)}, u32[]{:S(2)}, u32[]{:S(2)}) collective-permute-start(bf16[2,96,1920]{2,1,0:T(8,128)(2,1)} %pad_maximum_fusion.2), channel_id=1, source_target_pairs={{0,16},{4,12},{8,24},{12,4},{16,0},{20,28},{24,8},{28,20},{1,17},{... | collective-permute-start | bytes 2211848 | tf_op jit(solution)/shard_map/ppermute | solution.py:38
  195.1 1.2 copy-start.3
  195.1 1.5 copy-start.10
  195.2 22.2 %collective-permute-start.7 = (bf16[4,96,1152]{2,1,0:T(8,128)(2,1)S(1)}, bf16[4,96,1152]{2,1,0:T(8,128)(2,1)S(1)}, u32[]{:S(2)}, u32[]{:S(2)}) collective-permute-start(bf16[4,96,1152]{2,1,0:T(8,128)(2,1)S(1)} %dynamic-slice_bitcast_fusion), channel_id=1, source_target_pairs={{0,4},{4,0},{8,12},{12,8},{16,20},{20,16},{24,28},{28,24},{1,5},{5... | collective-permute-start | bytes 2654216 | tf_op jit(solution)/shard_map/ppermute | solution.py:38
  196.7 14.9 %collective-permute-start.8 = (bf16[96,768]{1,0:T(8,128)(2,1)S(1)}, bf16[96,768]{1,0:T(8,128)(2,1)S(1)}, u32[]{:S(2)}, u32[]{:S(2)}) collective-permute-start(bf16[96,768]{1,0:T(8,128)(2,1)S(1)} %fusion.21), channel_id=1, source_target_pairs={{0,3},{1,2},{2,1},{3,0},{4,7},{5,6},{6,5},{7,4},{8,11},{9,10},{10,... | collective-permute-start | bytes 442376 | tf_op jit(solution)/shard_map/ppermute | solution.py:42
  211.6 23.8 %collective-permute-start.12 = (bf16[96,768]{1,0:T(8,128)(2,1)S(1)}, bf16[96,768]{1,0:T(8,128)(2,1)}, u32[]{:S(2)}, u32[]{:S(2)}) collective-permute-start(bf16[96,768]{1,0:T(8,128)(2,1)S(1)} %fusion.19), channel_id=1, source_target_pairs={{0,3},{1,2},{2,1},{3,0},{4,7},{5,6},{6,5},{7,4},{8,11},{9,10},{10,... | collective-permute-start | bytes 442376 | tf_op jit(solution)/shard_map/ppermute | solution.py:42
  215.9 4.4 %copy-start.13 = (f32[16,768]{1,0:T(8,128)S(1)}, f32[16,768]{1,0:T(8,128)}, u32[]{:S(2)}) copy-start(f32[16,768]{1,0:T(8,128)} %get-tuple-element.100) | copy-start | bytes 147460
  215.9 15.8 %collective-permute-start.10 = (bf16[96,1920]{1,0:T(8,128)(2,1)S(1)}, bf16[96,1920]{1,0:T(8,128)(2,1)S(1)}, u32[]{:S(2)}, u32[]{:S(2)}) collective-permute-start(bf16[96,1920]{1,0:T(8,128)(2,1)S(1)} %fusion.4), channel_id=1, source_target_pairs={{0,8},{4,20},{8,0},{12,28},{16,24},{20,4},{24,16},{28,12},{1,9},{5... | collective-permute-start | bytes 1105928 | tf_op jit(solution)/shard_map/ppermute | solution.py:38
  217.4 14.2 %copy-start.8 = (bf16[4,96,1152]{2,1,0:T(8,128)(2,1)}, bf16[4,96,1152]{2,1,0:T(8,128)(2,1)S(1)}, u32[]{:S(2)}) copy-start(bf16[4,96,1152]{2,1,0:T(8,128)(2,1)S(1)} %collective-permute-done.7) | copy-start | bytes 2654212
  219.7 18.8 %collective-permute-start.11 = (bf16[2,96,1152]{2,1,0:T(8,128)(2,1)}, bf16[2,96,1152]{2,1,0:T(8,128)(2,1)}, u32[]{:S(2)}, u32[]{:S(2)}) collective-permute-start(bf16[2,96,1152]{2,1,0:T(8,128)(2,1)} %pad_maximum_fusion.5), channel_id=1, source_target_pairs={{0,16},{4,12},{8,24},{12,4},{16,0},{20,28},{24,8},{28,20},{1,17},{... | collective-permute-start | bytes 1327112 | tf_op jit(solution)/shard_map/ppermute | solution.py:38
  220.2 11.4 %collective-permute-start.9 = (f32[16,768]{1,0:T(8,128)S(1)}, f32[16,768]{1,0:T(8,128)S(1)}, u32[]{:S(2)}, u32[]{:S(2)}) collective-permute-start(f32[16,768]{1,0:T(8,128)S(1)} %copy-done.13), channel_id=1, source_target_pairs={{0,4},{4,0},{8,12},{12,8},{16,20},{20,16},{24,28},{28,24},{1,5},{5... | collective-permute-start | bytes 147464 | tf_op jit(solution)/shard_map/ppermute | solution.py:38
  233.0 5.5 %copy-start.9 = (bf16[4,96,1152]{2,1,0:T(8,128)(2,1)S(1)}, bf16[4,96,1152]{2,1,0:T(8,128)(2,1)}, u32[]{:S(2)}) copy-start(bf16[4,96,1152]{2,1,0:T(8,128)(2,1)} %copy-done.8) | copy-start | bytes 2654212
  236.4 10.1 %collective-permute-start.24 = (bf16[192,768]{1,0:T(8,128)(2,1)S(1)}, bf16[192,768]{1,0:T(8,128)(2,1)}, u32[]{:S(2)}, u32[]{:S(2)}) collective-permute-start(bf16[192,768]{1,0:T(8,128)(2,1)S(1)} %pad_maximum_fusion.6), channel_id=1, source_target_pairs={{0,1},{1,0},{2,3},{3,2},{4,5},{5,4},{6,7},{7,6},{8,9},{9,8},{10,11... | collective-permute-start | bytes 884744 | tf_op jit(solution)/shard_map/ppermute | solution.py:42
  237.9 17.7 %collective-permute-start.15 = (bf16[48,4992]{1,0:T(8,128)(2,1)S(1)}, bf16[48,4992]{1,0:T(8,128)(2,1)S(1)}, u32[]{:S(2)}, u32[]{:S(2)}) collective-permute-start(bf16[48,4992]{1,0:T(8,128)(2,1)S(1)} %dynamic-slice_bitcast_fusion.1), channel_id=1, source_target_pairs={{0,1},{1,0},{2,3},{3,2},{4,5},{5,4},{6,7},{7,6},{8,9},{9,8},{10,11... | collective-permute-start | bytes 1437704 | tf_op jit(solution)/shard_map/ppermute | solution.py:42
  240.3 4.2 %collective-permute-start.13 = (f32[16,768]{1,0:T(8,128)S(1)}, f32[16,768]{1,0:T(8,128)}, u32[]{:S(2)}, u32[]{:S(2)}) collective-permute-start(f32[16,768]{1,0:T(8,128)S(1)} %add.302), channel_id=1, source_target_pairs={{0,8},{4,20},{8,0},{12,28},{16,24},{20,4},{24,16},{28,12},{1,9},{5... | collective-permute-start | bytes 147464 | tf_op jit(solution)/shard_map/ppermute | solution.py:38
  241.7 17.7 %collective-permute-start.16 = (bf16[96,1152]{1,0:T(8,128)(2,1)}, bf16[96,1152]{1,0:T(8,128)(2,1)S(1)}, u32[]{:S(2)}, u32[]{:S(2)}) collective-permute-start(bf16[96,1152]{1,0:T(8,128)(2,1)} %fusion.11), channel_id=1, source_target_pairs={{0,8},{4,20},{8,0},{12,28},{16,24},{20,4},{24,16},{28,12},{1,9},{5... | collective-permute-start | bytes 663560 | tf_op jit(solution)/shard_map/ppermute | solution.py:38
  245.3 4.1 %collective-permute-start.14 = (f32[16,768]{1,0:T(8,128)S(1)}, f32[16,768]{1,0:T(8,128)S(1)}, u32[]{:S(2)}, u32[]{:S(2)}) collective-permute-start(f32[16,768]{1,0:T(8,128)S(1)} %add.311), channel_id=1, source_target_pairs={{0,16},{4,12},{8,24},{12,4},{16,0},{20,28},{24,8},{28,20},{1,17},{... | collective-permute-start | bytes 147464 | tf_op jit(solution)/shard_map/ppermute | solution.py:38
  255.7 11.0 %collective-permute-start.18 = (bf16[24,4992]{1,0:T(8,128)(2,1)S(1)}, bf16[24,4992]{1,0:T(8,128)(2,1)S(1)}, u32[]{:S(2)}, u32[]{:S(2)}) collective-permute-start(bf16[24,4992]{1,0:T(8,128)(2,1)S(1)} %fusion.20), channel_id=1, source_target_pairs={{0,3},{1,2},{2,1},{3,0},{4,7},{5,6},{6,5},{7,4},{8,11},{9,10},{10,... | collective-permute-start | bytes 718856 | tf_op jit(solution)/shard_map/ppermute | solution.py:42
  260.6 6.1 %collective-permute-start.17 = (f32[16,768]{1,0:T(8,128)S(1)}, f32[16,768]{1,0:T(8,128)S(1)}, u32[]{:S(2)}, u32[]{:S(2)}) collective-permute-start(f32[16,768]{1,0:T(8,128)S(1)} %add.312), channel_id=1, source_target_pairs={{0,1},{1,0},{2,3},{3,2},{4,5},{5,4},{6,7},{7,6},{8,9},{9,8},{10,11... | collective-permute-start | bytes 147464 | tf_op jit(solution)/shard_map/ppermute | solution.py:42
  261.8 10.4 %collective-permute-start.22 = (bf16[96,1152]{1,0:T(8,128)(2,1)S(1)}, bf16[96,1152]{1,0:T(8,128)(2,1)S(1)}, u32[]{:S(2)}, u32[]{:S(2)}) collective-permute-start(bf16[96,1152]{1,0:T(8,128)(2,1)S(1)} %fusion.10), channel_id=1, source_target_pairs={{0,1},{1,0},{2,3},{3,2},{4,5},{5,4},{6,7},{7,6},{8,9},{9,8},{10,11... | collective-permute-start | bytes 663560 | tf_op jit(solution)/shard_map/ppermute | solution.py:42
  266.7 11.0 %copy-start.11 = (f32[16,768]{1,0:T(8,128)}, f32[16,768]{1,0:T(8,128)S(1)}, u32[]{:S(2)}) copy-start(f32[16,768]{1,0:T(8,128)S(1)} %add.317.left_ref) | copy-start | bytes 147460
  266.8 13.0 %collective-permute-start.20 = (bf16[24,4992]{1,0:T(8,128)(2,1)S(1)}, bf16[24,4992]{1,0:T(8,128)(2,1)S(1)}, u32[]{:S(2)}, u32[]{:S(2)}) collective-permute-start(bf16[24,4992]{1,0:T(8,128)(2,1)S(1)} %fusion.8), channel_id=1, source_target_pairs={{0,3},{1,2},{2,1},{3,0},{4,7},{5,6},{6,5},{7,4},{8,11},{9,10},{10,... | collective-permute-start | bytes 718856 | tf_op jit(solution)/shard_map/ppermute | solution.py:42
  270.1 7.6 %collective-permute-start.19 = (f32[16,768]{1,0:T(8,128)S(1)}, f32[16,768]{1,0:T(8,128)S(1)}, u32[]{:S(2)}, u32[]{:S(2)}) collective-permute-start(f32[16,768]{1,0:T(8,128)S(1)} %add.317.left_ref), channel_id=1, source_target_pairs={{0,3},{1,2},{2,1},{3,0},{4,7},{5,6},{6,5},{7,4},{8,11},{9,10},{10,... | collective-permute-start | bytes 147464 | tf_op jit(solution)/shard_map/ppermute | solution.py:42
  272.2 18.2 %collective-permute-start.23 = (bf16[96,1152]{1,0:T(8,128)(2,1)S(1)}, bf16[96,1152]{1,0:T(8,128)(2,1)S(1)}, u32[]{:S(2)}, u32[]{:S(2)}) collective-permute-start(bf16[96,1152]{1,0:T(8,128)(2,1)S(1)} %fusion.14), channel_id=1, source_target_pairs={{0,3},{1,2},{2,1},{3,0},{4,7},{5,6},{6,5},{7,4},{8,11},{9,10},{10,... | collective-permute-start | bytes 663560 | tf_op jit(solution)/shard_map/ppermute | solution.py:42
  277.7 0.6 copy-start.12
  279.9 19.6 %collective-permute-start.21 = (bf16[48,4992]{1,0:T(8,128)(2,1)S(1)}, bf16[48,4992]{1,0:T(8,128)(2,1)S(1)}, u32[]{:S(2)}, u32[]{:S(2)}) collective-permute-start(bf16[48,4992]{1,0:T(8,128)(2,1)S(1)} %pad_maximum_fusion.4), channel_id=1, source_target_pairs={{0,1},{1,0},{2,3},{3,2},{4,5},{5,4},{6,7},{7,6},{8,9},{9,8},{10,11... | collective-permute-start | bytes 1437704 | tf_op jit(solution)/shard_map/ppermute | solution.py:42
  301.7 0.9 copy-start.15
Sparse Core Ops, SparseCore 0:
  10.5 50.1 all-gather.2
  62.7 38.7 all-gather.4
  107.7 58.2 reduce-scatter.2
  169.3 64.9 reduce-scatter.4

commit v5 on v4

--- a/solution.py
+++ b/solution.py
@@ -920,7 +920,10 @@
         sent = [last_grad.step(total)]
         total = behind(total, *sent)
         total = total + send_dp(total, 1)
-        sent = [mixed_grad.step(total)]
+        sent = [mixed_grad.step(total, last_grad.sum.got[-1], down_grad.sum.got[-1])]
+        sent = [mixed_grad.step(*sent)]
+        last_grad.hold(*sent)
+        last_grad.step()
         total = behind(total, *sent)
         vecs = own_rows(me, total, send_dp(total, 3))
     else:

time: 311 us -> 309 us (level)
  Pallas kernels: 133 us -> 141 us
  starting transfers between devices: 48.6 us -> 41.5 us
    ppermute x12, starting transfers between devices: 36.5 us -> 29.7 us  [send_dp(): return lax.ppermute(value, 'dp', [(i, i ^ bit) for i in range(4)])]
    pallas_call x1, Pallas kernels: 24 us -> 28 us  [attend(): pl.pallas_call(functools.partial(attend_kernel, rows), grid_spec=pltpu.Pr...]
    pallas_call x2, Pallas kernels: 28.1 us -> 31.6 us  [attend_back(): pl.pallas_call(functools.partial(attend_back_kernel, rows), grid_spec=plt...]
  transfers between devices with their start and end apart: 29 -> 29, of which waited for: 13 -> 11; matrix products, arithmetic and copies ran while one was open for 15% -> 14% of each run, Pallas kernels for 43% -> 46%
where the time goes in v5:
time: 309 us; the launch traced here: 307 us
  Pallas kernels  141 us (46%)
  waiting for transfers between devices  56.6 us (18%)
  starting transfers between devices  41.5 us (13%)
  matrix products  25.5 us (8%)
  other arithmetic  18.2 us (6%)
  between operations  14.5 us (5%)
  local copies, waits for them, and re-layouts  9.67 us (3%)
    ppermute x13, waiting for transfers between devices, send(): return lax.ppermute(value, 'fsdp', pairs)  31.8 us
    pallas_call x2, Pallas kernels, attend_back(): pl.pallas_call(functools.partial(attend_back_kernel, rows), grid_spec=plt...  31.6 us
    ppermute x12, starting transfers between devices, send_dp(): return lax.ppermute(value, 'dp', [(i, i ^ bit) for i in range(4)])  29.7 us
    pallas_call x1, Pallas kernels, attend(): pl.pallas_call(functools.partial(attend_kernel, rows), grid_spec=pltpu.Pr...  28 us
    dot_general x5, matrix products, weight_grad(): lax.dot_general(left, right, (((0,), (0,)), ((), ())), preferred_element_...  25.5 us
    ppermute x12, waiting for transfers between devices, send_dp(): return lax.ppermute(value, 'dp', [(i, i ^ bit) for i in range(4)])  22.7 us
    pallas_call x1, Pallas kernels, up_forward(): pl.pallas_call(functools.partial(up_kernel, out_weight, up_weight), grid_...  19.5 us
    pallas_call x1, Pallas kernels, middle_back(): pl.pallas_call(functools.partial(middle_kernel, out_weight, up_weight), g...  15.9 us
  transfers between devices with their start and end apart: 29, of which 11 were waited for; matrix products, arithmetic and copies ran while one was open for 14% of the time, Pallas kernels for 46%

profile of v5, /device:TPU:0, one launch (start us, length us, event | category | flops | bytes accessed | tf_op | source)
XLA Modules:
  0.0 307.1 jit_solution(16516011086272684109)
XLA Ops:
  7.3 1.0 constant_dynamic-update-slice_fusion.1
  8.4 1.1 constant_dynamic-update-slice_fusion
  9.5 0.9 copy-done.5
  10.4 0.7 all-gather.5.cloned.1.call-update
  11.3 3.0 collective-permute-start
  14.4 6.6 %collective-permute-done = bf16[104,2304]{1,0:T(8,128)(2,1)S(1)} collective-permute-done((bf16[104,2304]{1,0:T(8,128)(2,1)S(1)}, bf16[104,2304]{1,0:T(8,128)(2,1)S(1)}, u32[]{:S(2)}, u32[]{:S(2)}) %collective-permute-start) | collective-permute-done | bytes 479264 | tf_op jit(solution)/shard_map/ppermute | solution.py:38
  21.2 2.1 collective-permute-start.1
  23.3 18.8 %collective-permute-done.1.refs_1_ = bf16[2,104,2304]{2,1,0:T(8,128)(2,1)S(1)} collective-permute-done((bf16[2,104,2304]{2,1,0:T(8,128)(2,1)S(1)}, bf16[2,104,2304]{2,1,0:T(8,128)(2,1)S(1)}, u32[]{:S(2)}, u32[]{:S(2)}) %collective-permute-start.1) | collective-permute-done | bytes 958496 | tf_op jit(solution)/shard_map/ppermute | solution.py:38
  42.1 1.2 convert_reduce_fusion.starts_ref
  43.4 1.1 broadcast_in_dim.29.crops_ref
  45.4 9.5 %joint_forward.1 = (bf16[1024,2304]{1,0:T(8,128)(2,1)}, bf16[1024,768]{1,0:T(8,128)(2,1)}, f32[16,768]{1,0:T(8,128)}) custom-call(s32[1]{0:T(128)} %bitcast.me_ref, bf16[1024,768]{1,0:T(8,128)(2,1)} %x_ref.3, bf16[2,104,2304]{2,1,0:T(8,128)(2,1)} %copy-done, bf16[2,104,2304]{2,1,0:T(8,128)(2,1)} %copy-done.6, bf16[2,104,2304]{2,1,0:T(8,128)(2,1)} %copy-done.7, ...), custom_call_target="tpu_custom_call" | custom-call | flops 3623878656 | bytes 11403264 | tf_op jit(solution)/shard_map/joint_forward/pallas_call | solution.py:356
  54.9 28.0 %attend.1 = (bf16[1024,768]{1,0:T(8,128)(2,1)}, f32[6,10,8,256]{3,2,1,0:T(8,128)}) custom-call(s32[1024]{0:T(1024)} %convert_reduce_fusion.starts_ref, f32[1024,128]{1,0:T(8,128)} %broadcast_in_dim.29.crops_ref, bf16[1024,2304]{1,0:T(8,128)(2,1)} %get-tuple-element.70.query_ref.key_ref.value_ref, ...), custom_call_target="tpu_custom_call" | custom-call | flops 4831838208 | bytes 6291456 | tf_op jit(solution)/shard_map/attend/pallas_call | solution.py:443
  82.9 19.5 %up_forward.1 = (f32[1024,768]{1,0:T(8,128)}, bf16[1024,768]{1,0:T(8,128)(2,1)}, bf16[1024,3072]{1,0:T(8,128)(2,1)}, bf16[1024,3072]{1,0:T(8,128)(2,1)}) custom-call(s32[1]{0:T(128)} %bitcast.me_ref, bf16[1024,768]{1,0:T(8,128)(2,1)} %x_ref.3, bf16[1024,768]{1,0:T(8,128)(2,1)} %get-tuple-element.71.mixed_ref, f32[16,768]{1,0:T(8,128)} %get-tuple-element.72.vec_ref, ...), custom_call_target="tpu_custom_call" | custom-call | flops 6039797760 | bytes 25165824 | tf_op jit(solution)/shard_map/up_forward/pallas_call | solution.py:557
  102.5 9.8 %convolution_convert_fusion.1 = bf16[3072,768]{1,0:T(8,128)(2,1)} fusion(bf16[1024,3072]{1,0:T(8,128)(2,1)} %get-tuple-element.74.active_ref, bf16[1024,768]{1,0:T(8,128)(2,1)S(1)} %copy-done.24), kind=kOutput, calls=%fused_computation.6 | convolution fusion | flops 4834197504 | bytes 12582912 | tf_op jit(solution)/shard_map/dot_general | solution.py:799
  112.6 12.5 %slope_back.1 = (bf16[1024,3072]{1,0:T(8,128)(2,1)}, f32[8,768]{1,0:T(8,128)}, f32[8,3072]{1,0:T(8,128)}) custom-call(s32[1]{0:T(128)} %bitcast.me_ref, bf16[1024,768]{1,0:T(8,128)(2,1)} %grad_ref.2, bf16[1024,3072]{1,0:T(8,128)(2,1)} %get-tuple-element.76.slope_ref, bf16[3072,768]{1,0:T(8,128)(2,1)} %all-gather.5.cloned.1.call-done.refs_0_), custom_call_target="tpu_custom_call" | custom-call | flops 4831838208 | bytes 18874368 | tf_op jit(solution)/shard_map/slope_back/pallas_call | solution.py:601
  125.1 9.7 %convolution_convert_fusion = bf16[768,3072]{1,0:T(8,128)(2,1)} fusion(bf16[1024,768]{1,0:T(8,128)(2,1)S(1)} %copy-done.27, bf16[1024,3072]{1,0:T(8,128)(2,1)} %get-tuple-element.80.ga_ref), kind=kOutput, calls=%fused_computation.5 | convolution fusion | flops 4834197504 | bytes 12582912 | tf_op jit(solution)/shard_map/dot_general | solution.py:799
  134.8 15.9 %middle_back.1 = (f32[1024,768]{1,0:T(8,128)}, bf16[1024,768]{1,0:T(8,128)(2,1)}, bf16[1024,768]{1,0:T(8,128)(2,1)}, f32[3,8,768]{2,1,0:T(8,128)}) custom-call(s32[1]{0:T(128)} %bitcast.me_ref, f32[1024,768]{1,0:T(8,128)} %get-tuple-element.100.middle_ref, bf16[1024,768]{1,0:T(8,128)(2,1)} %grad_ref.2, bf16[1024,3072]{1,0:T(8,128)(2,1)} %get-tuple-element.80.ga_ref, ...), custom_call_target="tpu_custom_call" | custom-call | flops 6039797760 | bytes 22020096 | tf_op jit(solution)/shard_map/middle_back/pallas_call | solution.py:645
  150.8 15.5 %attend_back.2.part_a_ref = bf16[1024,1152]{1,0:T(8,128)(2,1)} custom-call(s32[1024]{0:T(1024)} %convert_reduce_fusion.starts_ref, f32[1024,128]{1,0:T(8,128)} %broadcast_in_dim.29.crops_ref, bf16[1024,2304]{1,0:T(8,128)(2,1)} %get-tuple-element.70.query_ref.key_ref.value_ref, bf16[1024,2304]{1,0:T(8,128)(2,1)} %get-tuple-element.70.query_ref.key_ref.value_ref, ...), custom_call_target="tpu_custom_call" | custom-call | flops 6039797760 | bytes 6291456 | tf_op jit(solution)/shard_map/attend_back/pallas_call | solution.py:517
  166.4 1.4 convolution_convert_fusion.4
  168.5 2.3 convolution_convert_fusion.3
  170.7 1.2 fusion.1
  172.3 1.0 dynamic-slice_bitcast_fusion.2
  173.3 1.2 collective-permute-start.6
  174.6 16.1 %attend_back.3.part_b_ref = bf16[1024,1152]{1,0:T(8,128)(2,1)} custom-call(s32[1024]{0:T(1024)} %convert_reduce_fusion.starts_ref, f32[1024,128]{1,0:T(8,128)} %broadcast_in_dim.29.crops_ref, bf16[1024,2304]{1,0:T(8,128)(2,1)} %get-tuple-element.70.query_ref.key_ref.value_ref, bf16[1024,2304]{1,0:T(8,128)(2,1)} %get-tuple-element.70.query_ref.key_ref.value_ref, ...), custom_call_target="tpu_custom_call" | custom-call | flops 6039797760 | bytes 6291456 | tf_op jit(solution)/shard_map/attend_back/pallas_call | solution.py:517
  190.7 1.7 fusion.6
  192.3 0.9 pad_maximum_fusion.2
  193.8 2.3 convolution_convert_fusion.2
  196.6 0.7 copy-done.3
  197.7 1.1 collective-permute-start.8
  198.8 11.2 %first_back.1 = (f32[1024,768]{1,0:T(8,128)}, f32[16,768]{1,0:T(8,128)}) custom-call(s32[1]{0:T(128)} %bitcast.me_ref, bf16[1024,768]{1,0:T(8,128)(2,1)} %x_ref.3, f32[1024,768]{1,0:T(8,128)} %get-tuple-element.92.gmid_ref, bf16[1024,1152]{1,0:T(8,128)(2,1)} %attend_back.2.part_a_ref, bf16[1024,1152]{1,0:T(8,128)(2,1)} %attend_back.3.part_b_ref, ...), custom_call_target="tpu_custom_call" | custom-call | flops 3623878656 | bytes 16121856 | tf_op jit(solution)/shard_map/first_back/pallas_call | solution.py:746
  210.0 2.9 collective-permute-start.12
  212.9 1.0 collective-permute-done.5
  213.9 1.2 fusion.4
  215.1 1.5 collective-permute-start.10
  216.7 1.5 fusion.13
  218.2 0.8 pad_maximum_fusion.5
  219.5 11.4 %down_forward.1 = f32[1024,768]{1,0:T(8,128)} custom-call(s32[1]{0:T(128)} %bitcast.me_ref, f32[1024,768]{1,0:T(8,128)} %get-tuple-element.100.middle_ref, bf16[1024,3072]{1,0:T(8,128)(2,1)} %get-tuple-element.74.active_ref, f32[16,768]{1,0:T(8,128)} %get-tuple-element.72.vec_ref, bf16[3072,768]{1,0:T(8,128)(2,1)} %all-gather.5.cloned.1.call-done.refs_0_), custom_call_target="tpu_custom_call" | custom-call | flops 4831838208 | bytes 17301504 | tf_op jit(solution)/shard_map/down_forward/pallas_call | solution.py:677
  231.0 1.3 fusion.3
  232.3 1.2 reduce-scatter.5.cloned.1.call-done
  233.5 1.1 pad_maximum_fusion.1
  234.7 1.8 collective-permute-start.15
  236.5 0.9 broadcast_select_fusion.7
  237.5 1.1 fusion.11
  238.6 1.1 collective-permute-start.13
  239.7 3.0 collective-permute-done.13
  242.8 0.9 collective-permute-start.14
  244.0 1.5 collective-permute-start.16
  245.6 1.9 collective-permute-done.14
  247.5 1.1 collective-permute-done.15
  248.8 3.6 %collective-permute-start.18 = (bf16[24,4992]{1,0:T(8,128)(2,1)S(1)}, bf16[24,4992]{1,0:T(8,128)(2,1)S(1)}, u32[]{:S(2)}, u32[]{:S(2)}) collective-permute-start(bf16[24,4992]{1,0:T(8,128)(2,1)S(1)} %fusion.20), channel_id=1, source_target_pairs={{0,3},{1,2},{2,1},{3,0},{4,7},{5,6},{6,5},{7,4},{8,11},{9,10},{10,... | collective-permute-start | bytes 718856 | tf_op jit(solution)/shard_map/ppermute | solution.py:42
  252.4 1.2 fusion.10
  253.7 2.0 collective-permute-start.17
  255.7 9.2 %collective-permute-done.17 = f32[16,768]{1,0:T(8,128)S(1)} collective-permute-done((f32[16,768]{1,0:T(8,128)S(1)}, f32[16,768]{1,0:T(8,128)S(1)}, u32[]{:S(2)}, u32[]{:S(2)}) %collective-permute-start.17) | collective-permute-done | bytes 49184 | tf_op jit(solution)/shard_map/ppermute | solution.py:42
  265.0 3.6 %collective-permute-start.21 = (bf16[24,4992]{1,0:T(8,128)(2,1)S(1)}, bf16[24,4992]{1,0:T(8,128)(2,1)S(1)}, u32[]{:S(2)}, u32[]{:S(2)}) collective-permute-start(bf16[24,4992]{1,0:T(8,128)(2,1)S(1)} %fusion.8), channel_id=1, source_target_pairs={{0,3},{1,2},{2,1},{3,0},{4,7},{5,6},{6,5},{7,4},{8,11},{9,10},{10,... | collective-permute-start | bytes 718856 | tf_op jit(solution)/shard_map/ppermute | solution.py:42
  268.5 5.1 %collective-permute-done.21 = bf16[24,4992]{1,0:T(8,128)(2,1)S(1)} collective-permute-done((bf16[24,4992]{1,0:T(8,128)(2,1)S(1)}, bf16[24,4992]{1,0:T(8,128)(2,1)S(1)}, u32[]{:S(2)}, u32[]{:S(2)}) %collective-permute-start.21) | collective-permute-done | bytes 239648 | tf_op jit(solution)/shard_map/ppermute | solution.py:42
  273.8 3.6 %collective-permute-start.24 = (bf16[96,1152]{1,0:T(8,128)(2,1)S(1)}, bf16[96,1152]{1,0:T(8,128)(2,1)S(1)}, u32[]{:S(2)}, u32[]{:S(2)}) collective-permute-start(bf16[96,1152]{1,0:T(8,128)(2,1)S(1)} %fusion.14), channel_id=1, source_target_pairs={{0,3},{1,2},{2,1},{3,0},{4,7},{5,6},{6,5},{7,4},{8,11},{9,10},{10,... | collective-permute-start | bytes 663560 | tf_op jit(solution)/shard_map/ppermute | solution.py:42
  277.9 1.1 maximum_convert_fusion
  279.0 9.0 %collective-permute-start.23 = (bf16[48,4992]{1,0:T(8,128)(2,1)S(1)}, bf16[48,4992]{1,0:T(8,128)(2,1)S(1)}, u32[]{:S(2)}, u32[]{:S(2)}) collective-permute-start(bf16[48,4992]{1,0:T(8,128)(2,1)S(1)} %pad_maximum_fusion.4), channel_id=1, source_target_pairs={{0,1},{1,0},{2,3},{3,2},{4,5},{5,4},{6,7},{7,6},{8,9},{9,8},{10,11... | collective-permute-start | bytes 1437704 | tf_op jit(solution)/shard_map/ppermute | solution.py:42
  288.0 0.6 copy-done.12
  288.6 1.5 own_rows.1
  290.2 7.2 %collective-permute-done.23 = bf16[48,4992]{1,0:T(8,128)(2,1)S(1)} collective-permute-done((bf16[48,4992]{1,0:T(8,128)(2,1)S(1)}, bf16[48,4992]{1,0:T(8,128)(2,1)S(1)}, u32[]{:S(2)}, u32[]{:S(2)}) %collective-permute-start.23) | collective-permute-done | bytes 479264 | tf_op jit(solution)/shard_map/ppermute | solution.py:42
  297.6 0.7 maximum_convert_fusion.1
  298.3 1.1 fusion.7
  299.7 0.9 copy-done.15
  (135 shorter events, 6.4 us)
Async XLA Ops:
  7.2 4.0 %copy-start.23 = (bf16[384]{0:T(512)(128)(2,1)S(1)}, bf16[384]{0:T(512)(128)(2,1)}, u32[]{:S(2)}) copy-start(bf16[384]{0:T(512)(128)(2,1)} %param.26) | copy-start | bytes 2308
  7.2 4.0 %copy-start.22 = (bf16[2,96]{1,0:T(2,128)(2,1)S(1)}, bf16[2,96]{1,0:T(2,128)(2,1)}, u32[]{:S(2)}) copy-start(bf16[2,96]{1,0:T(2,128)(2,1)} %param.20) | copy-start | bytes 1156
  7.2 4.0 %copy-start.4 = (bf16[96,2304]{1,0:T(8,128)(2,1)S(1)}, bf16[96,2304]{1,0:T(8,128)(2,1)}, u32[]{:S(2)}) copy-start(bf16[96,2304]{1,0:T(8,128)(2,1)} %param.19) | copy-start | bytes 1327108
  7.2 4.0 %copy-start.16 = (bf16[96]{0:T(256)(128)(2,1)S(1)}, bf16[96]{0:T(256)(128)(2,1)}, u32[]{:S(2)}) copy-start(bf16[96]{0:T(256)(128)(2,1)} %param.28) | copy-start | bytes 580
  7.2 4.0 %copy-start.17 = (bf16[96]{0:T(256)(128)(2,1)S(1)}, bf16[96]{0:T(256)(128)(2,1)}, u32[]{:S(2)}) copy-start(bf16[96]{0:T(256)(128)(2,1)} %param.24) | copy-start | bytes 580
  7.2 4.0 %copy-start.18 = (bf16[96]{0:T(256)(128)(2,1)S(1)}, bf16[96]{0:T(256)(128)(2,1)}, u32[]{:S(2)}) copy-start(bf16[96]{0:T(256)(128)(2,1)} %param.23) | copy-start | bytes 580
  7.2 4.0 %copy-start.19 = (bf16[96]{0:T(256)(128)(2,1)S(1)}, bf16[96]{0:T(256)(128)(2,1)}, u32[]{:S(2)}) copy-start(bf16[96]{0:T(256)(128)(2,1)} %param.22) | copy-start | bytes 580
  7.3 4.0 %copy-start.20 = (bf16[96]{0:T(256)(128)(2,1)S(1)}, bf16[96]{0:T(256)(128)(2,1)}, u32[]{:S(2)}) copy-start(bf16[96]{0:T(256)(128)(2,1)} %param.18) | copy-start | bytes 580
  7.3 4.0 %copy-start.21 = (bf16[96]{0:T(256)(128)(2,1)S(1)}, bf16[96]{0:T(256)(128)(2,1)}, u32[]{:S(2)}) copy-start(bf16[96]{0:T(256)(128)(2,1)} %param.17) | copy-start | bytes 580
  7.3 75.6 %all-gather.3.cloned.1.call-start = ((), (), s32[]{:S(2)}) async-start(), calls=%async_computation.2 | async-start | bytes 6635520 | tf_op jit(solution)/shard_map/all_gather | solution.py:201
  9.5 0.9 copy-start.5
  10.4 102.2 %all-gather.5.cloned.1.call-start = ((), (), s32[]{:S(2)}) async-start(), calls=%async_computation.3 | async-start | bytes 5308416 | tf_op jit(solution)/shard_map/all_gather | solution.py:201
  11.1 161.2 %reduce-scatter.3.cloned.1.call-start = ((), (), s32[]{:S(2)}) async-start(), calls=%async_computation.4 | async-start | bytes 5308416 | tf_op jit(solution)/shard_map/reduce_scatter | solution.py:873
  11.3 30.8 %copy-start.14 = (s32[1024]{0:T(1024)S(1)}, s32[1024]{0:T(1024)}, u32[]{:S(2)}) copy-start(s32[1024]{0:T(1024)} %param.16) | copy-start | bytes 12292
  11.3 9.7 %collective-permute-start = (bf16[104,2304]{1,0:T(8,128)(2,1)S(1)}, bf16[104,2304]{1,0:T(8,128)(2,1)S(1)}, u32[]{:S(2)}, u32[]{:S(2)}) collective-permute-start(bf16[104,2304]{1,0:T(8,128)(2,1)S(1)} %pad_add_fusion), channel_id=1, source_target_pairs={{0,8},{4,20},{8,0},{12,28},{16,24},{20,4},{24,16},{28,12},{1,9},{5... | collective-permute-start | bytes 1437704 | tf_op jit(solution)/shard_map/ppermute | solution.py:38
  21.1 23.7 %copy-start = (bf16[2,104,2304]{2,1,0:T(8,128)(2,1)}, bf16[2,104,2304]{2,1,0:T(8,128)(2,1)S(1)}, u32[]{:S(2)}) copy-start(bf16[2,104,2304]{2,1,0:T(8,128)(2,1)S(1)} %pad_maximum_fusion.refs_0_) | copy-start | bytes 2875396
  21.2 21.0 %collective-permute-start.1 = (bf16[2,104,2304]{2,1,0:T(8,128)(2,1)S(1)}, bf16[2,104,2304]{2,1,0:T(8,128)(2,1)S(1)}, u32[]{:S(2)}, u32[]{:S(2)}) collective-permute-start(bf16[2,104,2304]{2,1,0:T(8,128)(2,1)S(1)} %pad_maximum_fusion.refs_0_), channel_id=1, source_target_pairs={{0,16},{4,12},{8,24},{12,4},{16,0},{20,28},{24,8},{28,20},{1,17},{... | collective-permute-start | bytes 2875400 | tf_op jit(solution)/shard_map/ppermute | solution.py:38
  23.3 21.2 %collective-permute-start.2 = (bf16[2,104,2304]{2,1,0:T(8,128)(2,1)S(1)}, bf16[2,104,2304]{2,1,0:T(8,128)(2,1)S(1)}, u32[]{:S(2)}, u32[]{:S(2)}) collective-permute-start(bf16[2,104,2304]{2,1,0:T(8,128)(2,1)S(1)} %pad_maximum_fusion.refs_0_), channel_id=1, source_target_pairs={{0,4},{4,0},{8,12},{12,8},{16,20},{20,16},{24,28},{28,24},{1,5},{5... | collective-permute-start | bytes 2875400 | tf_op jit(solution)/shard_map/ppermute | solution.py:38
  42.1 2.8 copy-start.6
  42.1 2.8 collective-permute-start.3
  44.4 1.0 copy-start.7
  82.9 19.6 %copy-start.24 = (bf16[1024,768]{1,0:T(8,128)(2,1)S(1)}, bf16[1024,768]{1,0:T(8,128)(2,1)}, u32[]{:S(2)}) copy-start(bf16[1024,768]{1,0:T(8,128)(2,1)} %grad_ref.2) | copy-start | bytes 4718596
  112.3 121.2 %reduce-scatter.5.cloned.1.call-start = ((), (), s32[]{:S(2)}) async-start(), calls=%async_computation.5 | async-start | bytes 5308416 | tf_op jit(solution)/shard_map/reduce_scatter | solution.py:873
  112.5 12.5 %copy-start.27 = (bf16[1024,768]{1,0:T(8,128)(2,1)S(1)}, bf16[1024,768]{1,0:T(8,128)(2,1)}, u32[]{:S(2)}) copy-start(bf16[1024,768]{1,0:T(8,128)(2,1)} %get-tuple-element.79) | copy-start | bytes 4718596
  150.8 15.5 %copy-start.25 = (bf16[1024,768]{1,0:T(8,128)(2,1)S(1)}, bf16[1024,768]{1,0:T(8,128)(2,1)}, u32[]{:S(2)}) copy-start(bf16[1024,768]{1,0:T(8,128)(2,1)} %get-tuple-element.71.mixed_ref) | copy-start | bytes 4718596
  150.8 15.5 %copy-start.26 = (bf16[1024,768]{1,0:T(8,128)(2,1)S(1)}, bf16[1024,768]{1,0:T(8,128)(2,1)}, u32[]{:S(2)}) copy-start(bf16[1024,768]{1,0:T(8,128)(2,1)} %get-tuple-element.84) | copy-start | bytes 4718596
  166.3 1.7 copy-start.1
  166.3 2.1 copy-start.28
  172.0 18.7 %collective-permute-start.4 = (bf16[4,96,1920]{2,1,0:T(8,128)(2,1)}, bf16[4,96,1920]{2,1,0:T(8,128)(2,1)}, u32[]{:S(2)}, u32[]{:S(2)}) collective-permute-start(bf16[4,96,1920]{2,1,0:T(8,128)(2,1)} %fusion.1), channel_id=1, source_target_pairs={{0,4},{4,0},{8,12},{12,8},{16,20},{20,16},{24,28},{28,24},{1,5},{5... | collective-permute-start | bytes 4423688 | tf_op jit(solution)/shard_map/ppermute | solution.py:38
  173.3 24.0 %collective-permute-start.6 = (bf16[192,768]{1,0:T(8,128)(2,1)S(1)}, bf16[192,768]{1,0:T(8,128)(2,1)S(1)}, u32[]{:S(2)}, u32[]{:S(2)}) collective-permute-start(bf16[192,768]{1,0:T(8,128)(2,1)S(1)} %dynamic-slice_bitcast_fusion.2), channel_id=1, source_target_pairs={{0,1},{1,0},{2,3},{3,2},{4,5},{5,4},{6,7},{7,6},{8,9},{9,8},{10,11... | collective-permute-start | bytes 884744 | tf_op jit(solution)/shard_map/ppermute | solution.py:42
  190.7 2.6 copy-start.2
  190.7 3.2 %copy-start.29 = (bf16[1024,768]{1,0:T(8,128)(2,1)S(1)}, bf16[1024,768]{1,0:T(8,128)(2,1)}, u32[]{:S(2)}) copy-start(bf16[1024,768]{1,0:T(8,128)(2,1)} %get-tuple-element.89) | copy-start | bytes 4718596
  193.3 20.6 %collective-permute-start.5 = (bf16[2,96,1920]{2,1,0:T(8,128)(2,1)}, bf16[2,96,1920]{2,1,0:T(8,128)(2,1)}, u32[]{:S(2)}, u32[]{:S(2)}) collective-permute-start(bf16[2,96,1920]{2,1,0:T(8,128)(2,1)} %pad_maximum_fusion.2), channel_id=1, source_target_pairs={{0,16},{4,12},{8,24},{12,4},{16,0},{20,28},{24,8},{28,20},{1,17},{... | collective-permute-start | bytes 2211848 | tf_op jit(solution)/shard_map/ppermute | solution.py:38
  196.1 1.2 copy-start.3
  196.1 1.5 copy-start.10
  196.2 20.5 %collective-permute-start.7 = (bf16[4,96,1152]{2,1,0:T(8,128)(2,1)S(1)}, bf16[4,96,1152]{2,1,0:T(8,128)(2,1)S(1)}, u32[]{:S(2)}, u32[]{:S(2)}) collective-permute-start(bf16[4,96,1152]{2,1,0:T(8,128)(2,1)S(1)} %dynamic-slice_bitcast_fusion), channel_id=1, source_target_pairs={{0,4},{4,0},{8,12},{12,8},{16,20},{20,16},{24,28},{28,24},{1,5},{5... | collective-permute-start | bytes 2654216 | tf_op jit(solution)/shard_map/ppermute | solution.py:38
  197.7 12.3 %collective-permute-start.8 = (bf16[96,768]{1,0:T(8,128)(2,1)S(1)}, bf16[96,768]{1,0:T(8,128)(2,1)S(1)}, u32[]{:S(2)}, u32[]{:S(2)}) collective-permute-start(bf16[96,768]{1,0:T(8,128)(2,1)S(1)} %fusion.21), channel_id=1, source_target_pairs={{0,3},{1,2},{2,1},{3,0},{4,7},{5,6},{6,5},{7,4},{8,11},{9,10},{10,... | collective-permute-start | bytes 442376 | tf_op jit(solution)/shard_map/ppermute | solution.py:42
  210.0 26.5 %collective-permute-start.12 = (bf16[96,768]{1,0:T(8,128)(2,1)S(1)}, bf16[96,768]{1,0:T(8,128)(2,1)}, u32[]{:S(2)}, u32[]{:S(2)}) collective-permute-start(bf16[96,768]{1,0:T(8,128)(2,1)S(1)} %fusion.19), channel_id=1, source_target_pairs={{0,3},{1,2},{2,1},{3,0},{4,7},{5,6},{6,5},{7,4},{8,11},{9,10},{10,... | collective-permute-start | bytes 442376 | tf_op jit(solution)/shard_map/ppermute | solution.py:42
  215.1 4.4 %copy-start.13 = (f32[16,768]{1,0:T(8,128)S(1)}, f32[16,768]{1,0:T(8,128)}, u32[]{:S(2)}) copy-start(f32[16,768]{1,0:T(8,128)} %get-tuple-element.102) | copy-start | bytes 147460
  215.1 15.8 %collective-permute-start.10 = (bf16[96,1920]{1,0:T(8,128)(2,1)S(1)}, bf16[96,1920]{1,0:T(8,128)(2,1)S(1)}, u32[]{:S(2)}, u32[]{:S(2)}) collective-permute-start(bf16[96,1920]{1,0:T(8,128)(2,1)S(1)} %fusion.4), channel_id=1, source_target_pairs={{0,8},{4,20},{8,0},{12,28},{16,24},{20,4},{24,16},{28,12},{1,9},{5... | collective-permute-start | bytes 1105928 | tf_op jit(solution)/shard_map/ppermute | solution.py:38
  216.7 14.2 %copy-start.8 = (bf16[4,96,1152]{2,1,0:T(8,128)(2,1)}, bf16[4,96,1152]{2,1,0:T(8,128)(2,1)S(1)}, u32[]{:S(2)}) copy-start(bf16[4,96,1152]{2,1,0:T(8,128)(2,1)S(1)} %collective-permute-done.7) | copy-start | bytes 2654212
  219.0 18.5 %collective-permute-start.11 = (bf16[2,96,1152]{2,1,0:T(8,128)(2,1)}, bf16[2,96,1152]{2,1,0:T(8,128)(2,1)}, u32[]{:S(2)}, u32[]{:S(2)}) collective-permute-start(bf16[2,96,1152]{2,1,0:T(8,128)(2,1)} %pad_maximum_fusion.5), channel_id=1, source_target_pairs={{0,16},{4,12},{8,24},{12,4},{16,0},{20,28},{24,8},{28,20},{1,17},{... | collective-permute-start | bytes 1327112 | tf_op jit(solution)/shard_map/ppermute | solution.py:38
  219.5 11.4 %collective-permute-start.9 = (f32[16,768]{1,0:T(8,128)S(1)}, f32[16,768]{1,0:T(8,128)S(1)}, u32[]{:S(2)}, u32[]{:S(2)}) collective-permute-start(f32[16,768]{1,0:T(8,128)S(1)} %copy-done.13), channel_id=1, source_target_pairs={{0,4},{4,0},{8,12},{12,8},{16,20},{20,16},{24,28},{28,24},{1,5},{5... | collective-permute-start | bytes 147464 | tf_op jit(solution)/shard_map/ppermute | solution.py:38
  232.3 5.2 %copy-start.9 = (bf16[4,96,1152]{2,1,0:T(8,128)(2,1)S(1)}, bf16[4,96,1152]{2,1,0:T(8,128)(2,1)}, u32[]{:S(2)}) copy-start(bf16[4,96,1152]{2,1,0:T(8,128)(2,1)} %copy-done.8) | copy-start | bytes 2654212
  234.7 13.9 %collective-permute-start.15 = (bf16[48,4992]{1,0:T(8,128)(2,1)S(1)}, bf16[48,4992]{1,0:T(8,128)(2,1)S(1)}, u32[]{:S(2)}, u32[]{:S(2)}) collective-permute-start(bf16[48,4992]{1,0:T(8,128)(2,1)S(1)} %dynamic-slice_bitcast_fusion.1), channel_id=1, source_target_pairs={{0,1},{1,0},{2,3},{3,2},{4,5},{5,4},{6,7},{7,6},{8,9},{9,8},{10,11... | collective-permute-start | bytes 1437704 | tf_op jit(solution)/shard_map/ppermute | solution.py:42
  238.6 4.2 %collective-permute-start.13 = (f32[16,768]{1,0:T(8,128)S(1)}, f32[16,768]{1,0:T(8,128)S(1)}, u32[]{:S(2)}, u32[]{:S(2)}) collective-permute-start(f32[16,768]{1,0:T(8,128)S(1)} %add.302), channel_id=1, source_target_pairs={{0,8},{4,20},{8,0},{12,28},{16,24},{20,4},{24,16},{28,12},{1,9},{5... | collective-permute-start | bytes 147464 | tf_op jit(solution)/shard_map/ppermute | solution.py:38
  242.8 4.7 %collective-permute-start.14 = (f32[16,768]{1,0:T(8,128)S(1)}, f32[16,768]{1,0:T(8,128)S(1)}, u32[]{:S(2)}, u32[]{:S(2)}) collective-permute-start(f32[16,768]{1,0:T(8,128)S(1)} %add.311), channel_id=1, source_target_pairs={{0,16},{4,12},{8,24},{12,4},{16,0},{20,28},{24,8},{28,20},{1,17},{... | collective-permute-start | bytes 147464 | tf_op jit(solution)/shard_map/ppermute | solution.py:38
  243.7 21.2 %collective-permute-start.20 = (bf16[192,768]{1,0:T(8,128)(2,1)S(1)}, bf16[192,768]{1,0:T(8,128)(2,1)S(1)}, u32[]{:S(2)}, u32[]{:S(2)}) collective-permute-start(bf16[192,768]{1,0:T(8,128)(2,1)S(1)} %pad_maximum_fusion.6), channel_id=1, source_target_pairs={{0,1},{1,0},{2,3},{3,2},{4,5},{5,4},{6,7},{7,6},{8,9},{9,8},{10,11... | collective-permute-start | bytes 884744 | tf_op jit(solution)/shard_map/ppermute | solution.py:42
  244.0 8.4 %collective-permute-start.16 = (bf16[96,1152]{1,0:T(8,128)(2,1)S(1)}, bf16[96,1152]{1,0:T(8,128)(2,1)S(1)}, u32[]{:S(2)}, u32[]{:S(2)}) collective-permute-start(bf16[96,1152]{1,0:T(8,128)(2,1)S(1)} %fusion.11), channel_id=1, source_target_pairs={{0,8},{4,20},{8,0},{12,28},{16,24},{20,4},{24,16},{28,12},{1,9},{5... | collective-permute-start | bytes 663560 | tf_op jit(solution)/shard_map/ppermute | solution.py:38
  248.8 16.2 %collective-permute-start.18 = (bf16[24,4992]{1,0:T(8,128)(2,1)S(1)}, bf16[24,4992]{1,0:T(8,128)(2,1)S(1)}, u32[]{:S(2)}, u32[]{:S(2)}) collective-permute-start(bf16[24,4992]{1,0:T(8,128)(2,1)S(1)} %fusion.20), channel_id=1, source_target_pairs={{0,3},{1,2},{2,1},{3,0},{4,7},{5,6},{6,5},{7,4},{8,11},{9,10},{10,... | collective-permute-start | bytes 718856 | tf_op jit(solution)/shard_map/ppermute | solution.py:42
  253.6 11.3 %collective-permute-start.19 = (bf16[96,1152]{1,0:T(8,128)(2,1)S(1)}, bf16[96,1152]{1,0:T(8,128)(2,1)S(1)}, u32[]{:S(2)}, u32[]{:S(2)}) collective-permute-start(bf16[96,1152]{1,0:T(8,128)(2,1)S(1)} %fusion.10), channel_id=1, source_target_pairs={{0,1},{1,0},{2,3},{3,2},{4,5},{5,4},{6,7},{7,6},{8,9},{9,8},{10,11... | collective-permute-start | bytes 663560 | tf_op jit(solution)/shard_map/ppermute | solution.py:42
  253.7 11.2 %collective-permute-start.17 = (f32[16,768]{1,0:T(8,128)S(1)}, f32[16,768]{1,0:T(8,128)S(1)}, u32[]{:S(2)}, u32[]{:S(2)}) collective-permute-start(f32[16,768]{1,0:T(8,128)S(1)} %add.312), channel_id=1, source_target_pairs={{0,1},{1,0},{2,3},{3,2},{4,5},{5,4},{6,7},{7,6},{8,9},{9,8},{10,11... | collective-permute-start | bytes 147464 | tf_op jit(solution)/shard_map/ppermute | solution.py:42
  264.9 12.6 %copy-start.11 = (f32[16,768]{1,0:T(8,128)}, f32[16,768]{1,0:T(8,128)S(1)}, u32[]{:S(2)}) copy-start(f32[16,768]{1,0:T(8,128)S(1)} %add.317.left_ref) | copy-start | bytes 147460
  265.0 8.7 %collective-permute-start.21 = (bf16[24,4992]{1,0:T(8,128)(2,1)S(1)}, bf16[24,4992]{1,0:T(8,128)(2,1)S(1)}, u32[]{:S(2)}, u32[]{:S(2)}) collective-permute-start(bf16[24,4992]{1,0:T(8,128)(2,1)S(1)} %fusion.8), channel_id=1, source_target_pairs={{0,3},{1,2},{2,1},{3,0},{4,7},{5,6},{6,5},{7,4},{8,11},{9,10},{10,... | collective-permute-start | bytes 718856 | tf_op jit(solution)/shard_map/ppermute | solution.py:42
  273.8 16.3 %collective-permute-start.24 = (bf16[96,1152]{1,0:T(8,128)(2,1)S(1)}, bf16[96,1152]{1,0:T(8,128)(2,1)S(1)}, u32[]{:S(2)}, u32[]{:S(2)}) collective-permute-start(bf16[96,1152]{1,0:T(8,128)(2,1)S(1)} %fusion.14), channel_id=1, source_target_pairs={{0,3},{1,2},{2,1},{3,0},{4,7},{5,6},{6,5},{7,4},{8,11},{9,10},{10,... | collective-permute-start | bytes 663560 | tf_op jit(solution)/shard_map/ppermute | solution.py:42
  277.5 10.4 %collective-permute-start.22 = (f32[16,768]{1,0:T(8,128)S(1)}, f32[16,768]{1,0:T(8,128)S(1)}, u32[]{:S(2)}, u32[]{:S(2)}) collective-permute-start(f32[16,768]{1,0:T(8,128)S(1)} %add.317.left_ref), channel_id=1, source_target_pairs={{0,3},{1,2},{2,1},{3,0},{4,7},{5,6},{6,5},{7,4},{8,11},{9,10},{10,... | collective-permute-start | bytes 147464 | tf_op jit(solution)/shard_map/ppermute | solution.py:42
  279.0 18.4 %collective-permute-start.23 = (bf16[48,4992]{1,0:T(8,128)(2,1)S(1)}, bf16[48,4992]{1,0:T(8,128)(2,1)S(1)}, u32[]{:S(2)}, u32[]{:S(2)}) collective-permute-start(bf16[48,4992]{1,0:T(8,128)(2,1)S(1)} %pad_maximum_fusion.4), channel_id=1, source_target_pairs={{0,1},{1,0},{2,3},{3,2},{4,5},{5,4},{6,7},{7,6},{8,9},{9,8},{10,11... | collective-permute-start | bytes 1437704 | tf_op jit(solution)/shard_map/ppermute | solution.py:42
  288.0 0.6 copy-start.12
  299.7 0.9 copy-start.15
Sparse Core Ops, SparseCore 0:
  10.5 50.1 all-gather.2
  62.6 38.7 all-gather.4
  112.4 52.8 reduce-scatter.2
  168.6 64.9 reduce-scatter.4
